TPU v7x, 256 devices: a whole 4x4x8 slice. The times are simulated.
256 devices in a mesh: gx: 4 (over x_hi, core), gy: 8 (over y, x_lo), ha: 8 (over z).
Axes of the slice: x: 4 (x_hi: 2, x_lo: 2; x = x_hi * 2 + x_lo), y: 4, z: 8, core: 2. Of those that a mesh axis runs over, the one named last changes fastest.
Arguments:
- initial_value: float32 [64, 128, 8192], P('gx', 'gy', 'ha'), may hold values from -6 to 6
- corner: int32 [256, 4, 256], P(('gx', 'gy', 'ha')), may hold values from -1 to 244670, as said below
- weights: float32 [256, 16, 4, 256], P(('gx', 'gy', 'ha')), may hold values from 0 to 0.125
Outputs:
- final_value: float32 [64, 128, 8192], P('gx', 'gy', 'ha')
- sample_values: float32 [256, 4, 256], P(('gx', 'gy', 'ha'))
Inputs may be any that keep to these rules, and one draw needn't show every extreme that they name: A live corner is ((a 16 + b) * 16 + k) * 64 + v with a <= 14, b <= 14, k <= 14, v <= 62; -1 marks an empty slot; in each bucket [s, :, o] the live slots come first; in every draw some owner's buckets are full from every source.
All inputs are finite; a program needn't handle non-finite values.
Results may differ from a plain program's by a relative error of at most 0.0003.
Values sent between devices are 32-bit elements; how exact they have to be, the bound alone decides.
No kernel may reach another device: no remote copies, remote signals or barrier semaphores. Data moves between devices by JAX's collectives and lax.ppermute only.
A program may use at most 64 MiB of HBM per device.

v0:
```python
import math

import jax
import jax.numpy as jnp
from jax import lax
from jax.sharding import PartitionSpec as P

NV = 64
STEPS = 4


epsilon = 1e-06
turn_rate = 1.0
time_step = 0.15
two_pi = 6.283185307179586


def extended(cells, sides, width, closed):
    for axis, dim in sides:
        count = lax.axis_size(axis)
        ends = count if closed else count - 1
        head = lax.slice_in_dim(cells, 0, width, axis=dim)
        tail = lax.slice_in_dim(cells, cells.shape[dim] - width, cells.shape[dim], axis=dim)
        cells = jnp.concatenate(
            [
                lax.ppermute(tail, axis, [(i, (i + 1) % count) for i in range(ends)]),
                cells,
                lax.ppermute(head, axis, [((i + 1) % count, i) for i in range(ends)]),
            ],
            axis=dim,
        )
    return cells


def window_of(array_in, begin_at, length_of, along, stride):
    return lax.slice_in_dim(
        array_in, begin_at * stride, (begin_at + length_of) * stride, axis=along
    )


def blend(outer_low, inner_low, center, inner_high, outer_high):
    guess_one = outer_low / 3.0 - 7.0 * inner_low / 6.0 + 11.0 * center / 6.0
    guess_two = -inner_low / 6.0 + 5.0 * center / 6.0 + inner_high / 3.0
    guess_three = center / 3.0 + 5.0 * inner_high / 6.0 - outer_high / 6.0
    rough_one = (
        13.0 / 12.0 * (outer_low - 2.0 * inner_low + center) ** 2
        + 0.25 * (outer_low - 4.0 * inner_low + 3.0 * center) ** 2
    )
    rough_two = (
        13.0 / 12.0 * (inner_low - 2.0 * center + inner_high) ** 2
        + 0.25 * (inner_low - inner_high) ** 2
    )
    rough_three = (
        13.0 / 12.0 * (center - 2.0 * inner_high + outer_high) ** 2
        + 0.25 * (3.0 * center - 4.0 * inner_high + outer_high) ** 2
    )
    weight_one = 0.1 / (rough_one + epsilon) ** 2
    weight_two = 0.6 / (rough_two + epsilon) ** 2
    weight_three = 0.3 / (rough_three + epsilon) ** 2
    return (weight_one * guess_one + weight_two * guess_two + weight_three * guess_three) / (
        weight_one + weight_two + weight_three
    )


def weno_pair(padded, along, stride, length_of):
    differences = window_of(padded, 1, length_of + 5, along, stride) - window_of(
        padded, 0, length_of + 5, along, stride
    )
    stencil = [window_of(differences, shift_at, length_of, along, stride) for shift_at in range(6)]
    slope_minus = blend(stencil[0], stencil[1], stencil[2], stencil[3], stencil[4])
    slope_plus = blend(stencil[5], stencil[4], stencil[3], stencil[2], stencil[1])
    return (slope_minus, slope_plus)


def drift_tables(first_heading, count_h, total_h):
    heading_index = first_heading + jnp.arange(count_h, dtype=jnp.int32)
    heading_angle = heading_index.astype(jnp.float32) * (two_pi / total_h)
    speeds = 0.5 + jnp.arange(NV, dtype=jnp.int32).astype(jnp.float32) / (NV - 1)
    drift_x = (jnp.cos(heading_angle)[:, None] * speeds[None, :]).reshape(-1)
    drift_y = (jnp.sin(heading_angle)[:, None] * speeds[None, :]).reshape(-1)
    return (drift_x, drift_y)


def advance(level_set, padded_x, padded_y, padded_h, drift_x, drift_y):
    count_x = level_set.shape[0]
    count_y = level_set.shape[1]
    count_h = level_set.shape[2] // NV
    xm_slope, xp_slope = weno_pair(padded_x, 0, 1, count_x)
    ym_slope, yp_slope = weno_pair(padded_y, 1, 1, count_y)
    hm_slope, hp_slope = weno_pair(padded_h, 2, NV, count_h)
    hamiltonian = drift_x * (0.5 * (xm_slope + xp_slope)) + drift_y * (0.5 * (ym_slope + yp_slope))
    hamiltonian = hamiltonian - turn_rate * jnp.abs(0.5 * (hm_slope + hp_slope))
    hamiltonian = hamiltonian - 0.5 * (
        jnp.abs(drift_x) * (xp_slope - xm_slope)
        + jnp.abs(drift_y) * (yp_slope - ym_slope)
        + turn_rate * (hp_slope - hm_slope)
    )
    return level_set - time_step * jnp.maximum(hamiltonian, 0.0)


def read_corners(code_table, level_set):
    count_y = level_set.shape[1]
    plane_rows = level_set.shape[0] * count_y
    plane_columns = level_set.shape[2]
    grid_plane = level_set.reshape(plane_rows, plane_columns)
    slot_total = code_table.size
    block_size = math.gcd(slot_total, 128)
    clamped = jnp.maximum(code_table.reshape(-1), 0)
    row_start = (clamped // plane_columns).reshape(slot_total // block_size, block_size)
    column_start = (clamped % plane_columns).reshape(slot_total // block_size, block_size)
    row_offsets = jnp.array([0, 1, count_y, count_y + 1], dtype=jnp.int32)
    column_offsets = jnp.array([0, 1, NV, NV + 1], dtype=jnp.int32)
    row_iota = jnp.arange(plane_rows, dtype=jnp.int32)
    column_iota = jnp.arange(plane_columns, dtype=jnp.int32)

    def one_block(starts):
        row_index = starts[0][:, None] + row_offsets[None, :]
        selector = (row_index[:, :, None] == row_iota[None, None, :]).astype(jnp.float32)
        selector = selector.reshape(block_size * 4, plane_rows)
        picked = jnp.dot(
            selector,
            grid_plane,
            precision=lax.Precision.HIGHEST,
            preferred_element_type=jnp.float32,
        )
        picked = picked.reshape(block_size, 4, plane_columns)
        column_index = starts[1][:, None] + column_offsets[None, :]
        column_match = column_index[:, :, None] == column_iota[None, None, :]
        corner_read = jnp.sum(
            jnp.where(column_match[:, None, :, :], picked[:, :, None, :], 0.0), axis=-1
        )
        return corner_read.reshape(block_size, 16)

    blocks_read = lax.map(one_block, (row_start, column_start))
    return blocks_read.reshape(slot_total, 16).T.reshape((16,) + code_table.shape[1:])


def local(initial_value, corner, weights):
    count_x = initial_value.shape[0]
    count_y = initial_value.shape[1]
    count_h = initial_value.shape[2] // NV
    total_h = count_h * lax.axis_size("ha")
    drift_x, drift_y = drift_tables(lax.axis_index("ha") * count_h, count_h, total_h)
    level_set = initial_value
    for step_index in range(STEPS):
        plane = extended(level_set, (("gx", 0), ("gy", 1)), 3, False)
        padded_x = plane[:, 3 : 3 + count_y, :]
        padded_y = plane[3 : 3 + count_x, :, :]
        padded_h = extended(level_set, (("ha", 2),), 3 * NV, True)
        level_set = advance(level_set, padded_x, padded_y, padded_h, drift_x, drift_y)
    size_x = lax.axis_size("gx")
    size_yh = lax.axis_size("gy") * lax.axis_size("ha")
    slot_count = corner.shape[1]
    request = corner.reshape(1, slot_count, size_x, size_yh)
    weight_table = weights.reshape(16, slot_count, size_x, size_yh)
    live_slot = request >= 0
    in_codes, in_weights = (
        lax.all_to_all(
            lax.all_to_all(
                request.astype(jnp.float32), "gx", split_axis=2, concat_axis=2, tiled=True
            ),
            ("gy", "ha"),
            split_axis=3,
            concat_axis=3,
            tiled=True,
        ),
        lax.all_to_all(
            lax.all_to_all(weight_table, "gx", split_axis=2, concat_axis=2, tiled=True),
            ("gy", "ha"),
            split_axis=3,
            concat_axis=3,
            tiled=True,
        ),
    )
    fetched = read_corners(in_codes.astype(jnp.int32), level_set)
    owner_sum = jnp.sum(in_weights * fetched, axis=0, keepdims=True)
    weighted = lax.all_to_all(
        lax.all_to_all(owner_sum, "gx", split_axis=2, concat_axis=2, tiled=True),
        ("gy", "ha"),
        split_axis=3,
        concat_axis=3,
        tiled=True,
    )
    sampled = jnp.where(live_slot, weighted, 0.0).reshape(1, slot_count, size_x * size_yh)
    return (level_set, sampled)


def solution(mesh):
    return jax.shard_map(
        local,
        mesh=mesh,
        in_specs=(
            P("gx", "gy", "ha"),
            P(("gx", "gy", "ha"), None, None),
            P(("gx", "gy", "ha"), None, None, None),
        ),
        out_specs=(P("gx", "gy", "ha"), P(("gx", "gy", "ha"), None, None)),
        check_vma=False,
    )
```

profile of v0, /device:TPU:1, one launch (start us, length us, event | category | flops | bytes accessed | tf_op | source)
XLA Modules:
  0.0 292.6 jit_solution(11870040047615237573)
XLA Ops:
  1.7 6.0 %collective-permute-start = (f32[3,16,1024]{2,1,0:T(8,128)S(1)}, f32[3,16,1024]{2,1,0:T(8,128)S(1)}, u32[]{:S(2)}, u32[]{:S(2)}) collective-permute-start(f32[3,16,1024]{2,1,0:T(8,128)S(1)} %get-tuple-element.124), channel_id=1, source_target_pairs={{0,64},{64,128},{128,192},{1,65},{65,129},{129,193},{2,66},{66,130... | collective-permute-start | bytes 589832 | tf_op jit(solution)/shard_map/ppermute | solution.py:26
  13.2 3.9 %collective-permute-start.5 = (f32[16,16,192]{2,1,0:T(8,128)}, f32[16,16,192]{2,1,0:T(8,128)}, u32[]{:S(2)}, u32[]{:S(2)}) collective-permute-start(f32[16,16,192]{2,1,0:T(8,128)} %get-tuple-element.125), channel_id=1, source_target_pairs={{1,0},{2,1},{3,2},{4,3},{5,4},{6,5},{7,6},{0,7},{9,8},{10,9},{11,1... | collective-permute-start | bytes 589832 | tf_op jit(solution)/shard_map/ppermute | solution.py:28
  18.0 5.2 %all-to-all-start.2 = ((f32[4,1,256]{2,1,0:T(1,128)}), f32[4,1,256]{2,1,0:T(1,128)S(1)}, u32[]{:S(2)}, u32[]{:S(2)}) async-start(f32[4,1,256]{2,1,0:T(1,128)} %reshape.231), calls=%async_computation.2 | async-start | bytes 8192 | tf_op jit(solution)/shard_map/all_to_all | solution.py:159
  23.2 4.5 %all-to-all-done.2 = f32[4,1,256]{2,1,0:T(1,128)S(1)} async-done(((f32[4,1,256]{2,1,0:T(1,128)}), f32[4,1,256]{2,1,0:T(1,128)S(1)}, u32[]{:S(2)}, u32[]{:S(2)}) %all-to-all-start.2) | async-done | bytes 4128 | tf_op jit(solution)/shard_map/all_to_all | solution.py:159
  29.7 9.2 %all-to-all-start.3 = ((f32[1,4,4,64]{2,1,0,3:T(4,128)}), f32[1,4,4,64]{2,1,0,3:T(4,128)S(1)}, u32[]{:S(2)}, u32[]{:S(2)}) async-start(f32[1,4,4,64]{2,1,0,3:T(4,128)} %copy.162), calls=%async_computation.3 | async-start | bytes 262144 | tf_op jit(solution)/shard_map/all_to_all | solution.py:158
  40.2 8.7 %all-to-all-done.3 = f32[1,4,4,64]{2,1,0,3:T(4,128)S(1)} async-done(((f32[1,4,4,64]{2,1,0,3:T(4,128)}), f32[1,4,4,64]{2,1,0,3:T(4,128)S(1)}, u32[]{:S(2)}, u32[]{:S(2)}) %all-to-all-start.3) | async-done | bytes 4128 | tf_op jit(solution)/shard_map/all_to_all | solution.py:158
  48.9 5.4 %all-to-all-start = ((f32[4,1,4096]{2,1,0:T(1,128)}), f32[4,1,4096]{2,1,0:T(1,128)S(1)}, u32[]{:S(2)}, u32[]{:S(2)}) async-start(f32[4,1,4096]{2,1,0:T(1,128)} %reshape.227), calls=%async_computation | async-start | bytes 131072 | tf_op jit(solution)/shard_map/all_to_all | solution.py:168
  54.8 4.4 %all-to-all-done = f32[4,1,4096]{2,1,0:T(1,128)S(1)} async-done(((f32[4,1,4096]{2,1,0:T(1,128)}), f32[4,1,4096]{2,1,0:T(1,128)S(1)}, u32[]{:S(2)}, u32[]{:S(2)}) %all-to-all-start) | async-done | bytes 65568 | tf_op jit(solution)/shard_map/all_to_all | solution.py:168
  61.4 4.5 %all-to-all-start.1 = ((f32[64,1,256]{2,1,0:T(1,128)}), f32[64,1,256]{2,1,0:T(1,128)S(1)}, u32[]{:S(2)}, u32[]{:S(2)}) async-start(f32[64,1,256]{2,1,0:T(1,128)} %reshape.229), calls=%async_computation.1 | async-start | bytes 131072 | tf_op jit(solution)/shard_map/all_to_all | solution.py:167
  66.6 8.9 %all-to-all-done.1 = f32[64,1,256]{2,1,0:T(1,128)S(1)} async-done(((f32[64,1,256]{2,1,0:T(1,128)}), f32[64,1,256]{2,1,0:T(1,128)S(1)}, u32[]{:S(2)}, u32[]{:S(2)}) %all-to-all-start.1) | async-done | bytes 65568 | tf_op jit(solution)/shard_map/all_to_all | solution.py:167
  86.8 5.6 %collective-permute-done.3 = f32[22,3,1024]{2,0,1:T(8,128)} collective-permute-done((f32[22,3,1024]{2,0,1:T(8,128)S(1)}, f32[22,3,1024]{2,0,1:T(8,128)}, u32[]{:S(2)}, u32[]{:S(2)}) %collective-permute-start.3) | collective-permute-done | bytes 270368 | tf_op jit(solution)/shard_map/ppermute | solution.py:28
  94.1 14.8 %multiply_subtract_fusion.3 = f32[16,16,1024]{2,1,0:T(8,128)S(1)} fusion(f32[16,16,1024]{2,1,0:T(8,128)S(1)} %copy-done.1, f32[16,16,1344]{2,1,0:T(8,128)S(1)} %slice_subtract_fusion.7, f32[16,21,1024]{2,1,0:T(8,128)S(1)} %slice_subtract_fusion.3, f32[21,16,1024]{2,1,0:T(8,128)S(1)} %slice_subtract_fusion.11, f32[1024]{0:T(1024)S(1)} %abs.42, ...), kind=kLoop, calls=%fused_computation.34 | loop fusion | flops 103022592 | bytes 20987904 | tf_op jit(solution)/shard_map/sub | solution.py:98
  109.0 4.8 %collective-permute-start.6 = (f32[3,16,1024]{2,1,0:T(8,128)S(1)}, f32[3,16,1024]{2,1,0:T(8,128)S(1)}, u32[]{:S(2)}, u32[]{:S(2)}) collective-permute-start(f32[3,16,1024]{2,1,0:T(8,128)S(1)} %get-tuple-element.119), channel_id=1, source_target_pairs={{0,64},{64,128},{128,192},{1,65},{65,129},{129,193},{2,66},{66,130... | collective-permute-start | bytes 589832 | tf_op jit(solution)/shard_map/ppermute | solution.py:26
  118.6 3.7 %collective-permute-done.7 = f32[3,16,1024]{2,1,0:T(8,128)S(1)} collective-permute-done((f32[3,16,1024]{2,1,0:T(8,128)S(1)}, f32[3,16,1024]{2,1,0:T(8,128)S(1)}, u32[]{:S(2)}, u32[]{:S(2)}) %collective-permute-start.7) | collective-permute-done | bytes 196640 | tf_op jit(solution)/shard_map/ppermute | solution.py:28
  132.4 4.7 %collective-permute-done.9 = f32[22,3,1024]{2,0,1:T(8,128)} collective-permute-done((f32[22,3,1024]{2,0,1:T(8,128)}, f32[22,3,1024]{2,0,1:T(8,128)}, u32[]{:S(2)}, u32[]{:S(2)}) %collective-permute-start.9) | collective-permute-done | bytes 270368 | tf_op jit(solution)/shard_map/ppermute | solution.py:28
  138.9 14.8 %multiply_subtract_fusion.2 = f32[16,16,1024]{2,1,0:T(8,128)S(1)} fusion(f32[16,16,1024]{2,1,0:T(8,128)S(1)} %multiply_subtract_fusion.3, f32[16,16,1344]{2,1,0:T(8,128)S(1)} %slice_subtract_fusion.6, f32[16,21,1024]{2,1,0:T(8,128)S(1)} %slice_subtract_fusion.2, f32[21,16,1024]{2,1,0:T(8,128)S(1)} %slice_subtract_fusion.10, f32[1024]{0:T(1024)S(1)} %abs.42, ...), kind=kLoop, calls=%fused_computation.33 | loop fusion | flops 103022592 | bytes 20987904 | tf_op jit(solution)/shard_map/sub | solution.py:98
  175.6 3.8 %collective-permute-done.15 = f32[22,3,1024]{2,0,1:T(8,128)} collective-permute-done((f32[22,3,1024]{2,0,1:T(8,128)}, f32[22,3,1024]{2,0,1:T(8,128)}, u32[]{:S(2)}, u32[]{:S(2)}) %collective-permute-start.15) | collective-permute-done | bytes 270368 | tf_op jit(solution)/shard_map/ppermute | solution.py:28
  181.1 14.8 %multiply_subtract_fusion.1 = f32[16,16,1024]{2,1,0:T(8,128)S(1)} fusion(f32[16,16,1024]{2,1,0:T(8,128)S(1)} %multiply_subtract_fusion.2, f32[16,16,1344]{2,1,0:T(8,128)S(1)} %slice_subtract_fusion.5, f32[16,21,1024]{2,1,0:T(8,128)S(1)} %slice_subtract_fusion.1, f32[21,16,1024]{2,1,0:T(8,128)S(1)} %slice_subtract_fusion.9, f32[1024]{0:T(1024)S(1)} %abs.42, ...), kind=kLoop, calls=%fused_computation.32 | loop fusion | flops 103022592 | bytes 20987904 | tf_op jit(solution)/shard_map/sub | solution.py:98
  218.1 3.7 %collective-permute-done.21 = f32[22,3,1024]{2,0,1:T(8,128)} collective-permute-done((f32[22,3,1024]{2,0,1:T(8,128)}, f32[22,3,1024]{2,0,1:T(8,128)}, u32[]{:S(2)}, u32[]{:S(2)}) %collective-permute-start.21) | collective-permute-done | bytes 270368 | tf_op jit(solution)/shard_map/ppermute | solution.py:28
  223.6 14.8 %multiply_subtract_fusion = f32[16,16,1024]{2,1,0:T(8,128)S(1)} fusion(f32[16,16,1024]{2,1,0:T(8,128)S(1)} %multiply_subtract_fusion.1, f32[16,16,1344]{2,1,0:T(8,128)S(1)} %slice_subtract_fusion.4, f32[16,21,1024]{2,1,0:T(8,128)S(1)} %slice_subtract_fusion, f32[21,16,1024]{2,1,0:T(8,128)S(1)} %slice_subtract_fusion.8, f32[1024]{0:T(1024)S(1)} %abs.42, ...), kind=kLoop, calls=%fused_computation.31 | loop fusion | flops 103022592 | bytes 20987904 | tf_op jit(solution)/shard_map/sub | solution.py:98
  238.5 29.1 %while.12 = (s32[]{:T(128)}, f32[8,128,16]{1,0,2:T(8,128)S(1)}, s32[8,128]{1,0:T(8,128)}, s32[8,128]{1,0:T(8,128)}, f32[256,1024]{1,0:T(8,128)S(1)}, /*index=5*/...) while((s32[]{:T(128)}, f32[8,128,16]{1,0,2:T(8,128)S(1)}, s32[8,128]{1,0:T(8,128)}, ...), condition=%wide.region_2.3_spmd.clone.clone, body=%wide.region_0.2_spmd.sunk.clone.clone.sunk | while | flops 1615461376 | bytes 6327429 | solution.py:134
  268.2 7.6 %all_to_all.30 = f32[4,1,256]{2,1,0:T(1,128)S(1)} all-to-all(f32[4,1,256]{2,1,0:T(1,128)S(1)} %reshape.233), channel_id=1, replica_groups=mesh['gx'=4,'gy'=8,'ha'=8] {'gx'}, dimensions={0} | all-to-all | bytes 8192 | tf_op jit(solution)/shard_map/all_to_all | solution.py:178
  277.2 4.6 %all-to-all-start.5 = ((f32[1,4,4,64]{2,1,0,3:T(4,128)}), f32[1,4,4,64]{2,1,0,3:T(4,128)S(1)}, u32[]{:S(2)}, u32[]{:S(2)}) async-start(f32[1,4,4,64]{2,1,0,3:T(4,128)} %copy.169), calls=%async_computation.5 | async-start | bytes 262144 | tf_op jit(solution)/shard_map/all_to_all | solution.py:177
  281.9 9.9 %all-to-all-done.5 = f32[1,4,4,64]{2,1,0,3:T(4,128)S(1)} async-done(((f32[1,4,4,64]{2,1,0,3:T(4,128)}), f32[1,4,4,64]{2,1,0,3:T(4,128)S(1)}, u32[]{:S(2)}, u32[]{:S(2)}) %all-to-all-start.5) | async-done | bytes 4128 | tf_op jit(solution)/shard_map/all_to_all | solution.py:177
  (215 shorter events, 122.4 us)
Async XLA Ops:
  1.7 75.8 %collective-permute-start = (f32[3,16,1024]{2,1,0:T(8,128)S(1)}, f32[3,16,1024]{2,1,0:T(8,128)S(1)}, u32[]{:S(2)}, u32[]{:S(2)}) collective-permute-start(f32[3,16,1024]{2,1,0:T(8,128)S(1)} %get-tuple-element.124), channel_id=1, source_target_pairs={{0,64},{64,128},{128,192},{1,65},{65,129},{129,193},{2,66},{66,130... | collective-permute-start | bytes 589832 | tf_op jit(solution)/shard_map/ppermute | solution.py:26
  7.8 69.9 %collective-permute-start.1 = (f32[3,16,1024]{2,1,0:T(8,128)S(1)}, f32[3,16,1024]{2,1,0:T(8,128)S(1)}, u32[]{:S(2)}, u32[]{:S(2)}) collective-permute-start(f32[3,16,1024]{2,1,0:T(8,128)S(1)} %get-tuple-element.123), channel_id=1, source_target_pairs={{64,0},{128,64},{192,128},{65,1},{129,65},{193,129},{66,2},{130,66... | collective-permute-start | bytes 589832 | tf_op jit(solution)/shard_map/ppermute | solution.py:28
  11.6 70.2 %collective-permute-start.4 = (f32[16,16,192]{2,1,0:T(8,128)}, f32[16,16,192]{2,1,0:T(8,128)}, u32[]{:S(2)}, u32[]{:S(2)}) collective-permute-start(f32[16,16,192]{2,1,0:T(8,128)} %get-tuple-element.126), channel_id=1, source_target_pairs={{0,1},{1,2},{2,3},{3,4},{4,5},{5,6},{6,7},{7,0},{8,9},{9,10},{10,1... | collective-permute-start | bytes 589832 | tf_op jit(solution)/shard_map/ppermute | solution.py:26
  13.2 68.6 %collective-permute-start.5 = (f32[16,16,192]{2,1,0:T(8,128)}, f32[16,16,192]{2,1,0:T(8,128)}, u32[]{:S(2)}, u32[]{:S(2)}) collective-permute-start(f32[16,16,192]{2,1,0:T(8,128)} %get-tuple-element.125), channel_id=1, source_target_pairs={{1,0},{2,1},{3,2},{4,3},{5,4},{6,5},{7,6},{0,7},{9,8},{10,9},{11,1... | collective-permute-start | bytes 589832 | tf_op jit(solution)/shard_map/ppermute | solution.py:28
  18.0 9.8 %all-to-all-start.2 = ((f32[4,1,256]{2,1,0:T(1,128)}), f32[4,1,256]{2,1,0:T(1,128)S(1)}, u32[]{:S(2)}, u32[]{:S(2)}) async-start(f32[4,1,256]{2,1,0:T(1,128)} %reshape.231), calls=%async_computation.2 | async-start | bytes 8192 | tf_op jit(solution)/shard_map/all_to_all | solution.py:159
  29.7 19.2 %all-to-all-start.3 = ((f32[1,4,4,64]{2,1,0,3:T(4,128)}), f32[1,4,4,64]{2,1,0,3:T(4,128)S(1)}, u32[]{:S(2)}, u32[]{:S(2)}) async-start(f32[1,4,4,64]{2,1,0,3:T(4,128)} %copy.162), calls=%async_computation.3 | async-start | bytes 262144 | tf_op jit(solution)/shard_map/all_to_all | solution.py:158
  48.9 10.2 %all-to-all-start = ((f32[4,1,4096]{2,1,0:T(1,128)}), f32[4,1,4096]{2,1,0:T(1,128)S(1)}, u32[]{:S(2)}, u32[]{:S(2)}) async-start(f32[4,1,4096]{2,1,0:T(1,128)} %reshape.227), calls=%async_computation | async-start | bytes 131072 | tf_op jit(solution)/shard_map/all_to_all | solution.py:168
  61.4 14.0 %all-to-all-start.1 = ((f32[64,1,256]{2,1,0:T(1,128)}), f32[64,1,256]{2,1,0:T(1,128)S(1)}, u32[]{:S(2)}, u32[]{:S(2)}) async-start(f32[64,1,256]{2,1,0:T(1,128)} %reshape.229), calls=%async_computation.1 | async-start | bytes 131072 | tf_op jit(solution)/shard_map/all_to_all | solution.py:167
  78.0 8.6 %collective-permute-start.2 = (f32[22,3,1024]{2,0,1:T(8,128)S(1)}, f32[22,3,1024]{2,0,1:T(8,128)S(1)}, u32[]{:S(2)}, u32[]{:S(2)}) collective-permute-start(f32[22,3,1024]{2,0,1:T(8,128)S(1)} %copy.142), channel_id=1, source_target_pairs={{0,8},{8,16},{16,24},{24,32},{32,40},{40,48},{48,56},{1,9},{9,17},... | collective-permute-start | bytes 811016 | tf_op jit(solution)/shard_map/ppermute | solution.py:26
  80.5 11.8 %collective-permute-start.3 = (f32[22,3,1024]{2,0,1:T(8,128)S(1)}, f32[22,3,1024]{2,0,1:T(8,128)}, u32[]{:S(2)}, u32[]{:S(2)}) collective-permute-start(f32[22,3,1024]{2,0,1:T(8,128)S(1)} %copy.143), channel_id=1, source_target_pairs={{8,0},{16,8},{24,16},{32,24},{40,32},{48,40},{56,48},{9,1},{17,9},... | collective-permute-start | bytes 811016 | tf_op jit(solution)/shard_map/ppermute | solution.py:28
  109.0 9.6 %collective-permute-start.6 = (f32[3,16,1024]{2,1,0:T(8,128)S(1)}, f32[3,16,1024]{2,1,0:T(8,128)S(1)}, u32[]{:S(2)}, u32[]{:S(2)}) collective-permute-start(f32[3,16,1024]{2,1,0:T(8,128)S(1)} %get-tuple-element.119), channel_id=1, source_target_pairs={{0,64},{64,128},{128,192},{1,65},{65,129},{129,193},{2,66},{66,130... | collective-permute-start | bytes 589832 | tf_op jit(solution)/shard_map/ppermute | solution.py:26
  115.8 11.7 %collective-permute-start.10 = (f32[16,16,192]{2,1,0:T(8,128)S(1)}, f32[16,16,192]{2,1,0:T(8,128)}, u32[]{:S(2)}, u32[]{:S(2)}) collective-permute-start(f32[16,16,192]{2,1,0:T(8,128)S(1)} %get-tuple-element.122), channel_id=1, source_target_pairs={{0,1},{1,2},{2,3},{3,4},{4,5},{5,6},{6,7},{7,0},{8,9},{9,10},{10,1... | collective-permute-start | bytes 589832 | tf_op jit(solution)/shard_map/ppermute | solution.py:26
  116.5 11.0 %collective-permute-start.11 = (f32[16,16,192]{2,1,0:T(8,128)S(1)}, f32[16,16,192]{2,1,0:T(8,128)}, u32[]{:S(2)}, u32[]{:S(2)}) collective-permute-start(f32[16,16,192]{2,1,0:T(8,128)S(1)} %get-tuple-element.121), channel_id=1, source_target_pairs={{1,0},{2,1},{3,2},{4,3},{5,4},{6,5},{7,6},{0,7},{9,8},{10,9},{11,1... | collective-permute-start | bytes 589832 | tf_op jit(solution)/shard_map/ppermute | solution.py:28
  122.7 9.5 %collective-permute-start.8 = (f32[22,3,1024]{2,0,1:T(8,128)S(1)}, f32[22,3,1024]{2,0,1:T(8,128)S(1)}, u32[]{:S(2)}, u32[]{:S(2)}) collective-permute-start(f32[22,3,1024]{2,0,1:T(8,128)S(1)} %copy.146), channel_id=1, source_target_pairs={{0,8},{8,16},{16,24},{24,32},{32,40},{40,48},{48,56},{1,9},{9,17},... | collective-permute-start | bytes 811016 | tf_op jit(solution)/shard_map/ppermute | solution.py:26
  126.2 10.9 %collective-permute-start.9 = (f32[22,3,1024]{2,0,1:T(8,128)}, f32[22,3,1024]{2,0,1:T(8,128)}, u32[]{:S(2)}, u32[]{:S(2)}) collective-permute-start(f32[22,3,1024]{2,0,1:T(8,128)} %copy.147), channel_id=1, source_target_pairs={{8,0},{16,8},{24,16},{32,24},{40,32},{48,40},{56,48},{9,1},{17,9},... | collective-permute-start | bytes 811016 | tf_op jit(solution)/shard_map/ppermute | solution.py:28
  158.2 12.4 %collective-permute-start.16 = (f32[16,16,192]{2,1,0:T(8,128)S(1)}, f32[16,16,192]{2,1,0:T(8,128)}, u32[]{:S(2)}, u32[]{:S(2)}) collective-permute-start(f32[16,16,192]{2,1,0:T(8,128)S(1)} %get-tuple-element.118), channel_id=1, source_target_pairs={{0,1},{1,2},{2,3},{3,4},{4,5},{5,6},{6,7},{7,0},{8,9},{9,10},{10,1... | collective-permute-start | bytes 589832 | tf_op jit(solution)/shard_map/ppermute | solution.py:26
  158.3 12.4 %collective-permute-start.17 = (f32[16,16,192]{2,1,0:T(8,128)S(1)}, f32[16,16,192]{2,1,0:T(8,128)}, u32[]{:S(2)}, u32[]{:S(2)}) collective-permute-start(f32[16,16,192]{2,1,0:T(8,128)S(1)} %get-tuple-element.117), channel_id=1, source_target_pairs={{1,0},{2,1},{3,2},{4,3},{5,4},{6,5},{7,6},{0,7},{9,8},{10,9},{11,1... | collective-permute-start | bytes 589832 | tf_op jit(solution)/shard_map/ppermute | solution.py:28
  165.0 10.4 %collective-permute-start.14 = (f32[22,3,1024]{2,0,1:T(8,128)S(1)}, f32[22,3,1024]{2,0,1:T(8,128)S(1)}, u32[]{:S(2)}, u32[]{:S(2)}) collective-permute-start(f32[22,3,1024]{2,0,1:T(8,128)S(1)} %copy.150), channel_id=1, source_target_pairs={{0,8},{8,16},{16,24},{24,32},{32,40},{40,48},{48,56},{1,9},{9,17},... | collective-permute-start | bytes 811016 | tf_op jit(solution)/shard_map/ppermute | solution.py:26
  169.3 10.0 %collective-permute-start.15 = (f32[22,3,1024]{2,0,1:T(8,128)}, f32[22,3,1024]{2,0,1:T(8,128)}, u32[]{:S(2)}, u32[]{:S(2)}) collective-permute-start(f32[22,3,1024]{2,0,1:T(8,128)} %copy.151), channel_id=1, source_target_pairs={{8,0},{16,8},{24,16},{32,24},{40,32},{48,40},{56,48},{9,1},{17,9},... | collective-permute-start | bytes 811016 | tf_op jit(solution)/shard_map/ppermute | solution.py:28
  201.2 11.9 %collective-permute-start.22 = (f32[16,16,192]{2,1,0:T(8,128)S(1)}, f32[16,16,192]{2,1,0:T(8,128)}, u32[]{:S(2)}, u32[]{:S(2)}) collective-permute-start(f32[16,16,192]{2,1,0:T(8,128)S(1)} %get-tuple-element.114), channel_id=1, source_target_pairs={{0,1},{1,2},{2,3},{3,4},{4,5},{5,6},{6,7},{7,0},{8,9},{9,10},{10,1... | collective-permute-start | bytes 589832 | tf_op jit(solution)/shard_map/ppermute | solution.py:26
  201.6 11.6 %collective-permute-start.23 = (f32[16,16,192]{2,1,0:T(8,128)S(1)}, f32[16,16,192]{2,1,0:T(8,128)}, u32[]{:S(2)}, u32[]{:S(2)}) collective-permute-start(f32[16,16,192]{2,1,0:T(8,128)S(1)} %get-tuple-element.113), channel_id=1, source_target_pairs={{1,0},{2,1},{3,2},{4,3},{5,4},{6,5},{7,6},{0,7},{9,8},{10,9},{11,1... | collective-permute-start | bytes 589832 | tf_op jit(solution)/shard_map/ppermute | solution.py:28
  208.2 9.7 %collective-permute-start.20 = (f32[22,3,1024]{2,0,1:T(8,128)S(1)}, f32[22,3,1024]{2,0,1:T(8,128)S(1)}, u32[]{:S(2)}, u32[]{:S(2)}) collective-permute-start(f32[22,3,1024]{2,0,1:T(8,128)S(1)} %copy.154), channel_id=1, source_target_pairs={{0,8},{8,16},{16,24},{24,32},{32,40},{40,48},{48,56},{1,9},{9,17},... | collective-permute-start | bytes 811016 | tf_op jit(solution)/shard_map/ppermute | solution.py:26
  211.9 9.9 %collective-permute-start.21 = (f32[22,3,1024]{2,0,1:T(8,128)}, f32[22,3,1024]{2,0,1:T(8,128)}, u32[]{:S(2)}, u32[]{:S(2)}) collective-permute-start(f32[22,3,1024]{2,0,1:T(8,128)} %copy.155), channel_id=1, source_target_pairs={{8,0},{16,8},{24,16},{32,24},{40,32},{48,40},{56,48},{9,1},{17,9},... | collective-permute-start | bytes 811016 | tf_op jit(solution)/shard_map/ppermute | solution.py:28
  277.2 14.6 %all-to-all-start.5 = ((f32[1,4,4,64]{2,1,0,3:T(4,128)}), f32[1,4,4,64]{2,1,0,3:T(4,128)S(1)}, u32[]{:S(2)}, u32[]{:S(2)}) async-start(f32[1,4,4,64]{2,1,0,3:T(4,128)} %copy.169), calls=%async_computation.5 | async-start | bytes 262144 | tf_op jit(solution)/shard_map/all_to_all | solution.py:177
  (14 other events, 255.9 us)
where the time goes:
time: 294 us; the launch traced here: 293 us
  other arithmetic  88.9 us (30%)
  starting transfers between devices  83.4 us (28%)
  waiting for transfers between devices  64.9 us (22%)
  local copies, waits for them, and re-layouts  37.3 us (13%)
  matrix products  8.72 us (3%)
  blocking collectives  7.56 us (3%)
    sub x4, other arithmetic, advance(): return level_set - time_step * jnp.maximum(hamiltonian, 0.0)  59.2 us
    ppermute x12, starting transfers between devices, extended(): lax.ppermute(tail, axis, [(i, (i + 1) % count) for i in range(ends)])  30.2 us
    ppermute x12, waiting for transfers between devices, extended(): lax.ppermute(head, axis, [((i + 1) % count, i) for i in range(ends)])  28.5 us
    ppermute x12, starting transfers between devices, extended(): lax.ppermute(head, axis, [((i + 1) % count, i) for i in range(ends)])  24.3 us
    sub x12, other arithmetic, weno_pair(): window_of(padded, 1, length_of + 5, along, stride)  10.3 us
    reduce_sum x8, other arithmetic, one_block(): jnp.sum(jnp.where(column_match[:, None, :, :], picked[:, :, None, :], 0.0...  9.95 us
    all_to_all x1, waiting for transfers between devices, local(): lax.all_to_all(lax.all_to_all(owner_sum, 'gx', split_axis=2, concat_axis=...  9.88 us
    concatenate x5, local copies, waits for them, and re-layouts, extended(): jnp.concatenate([lax.ppermute(tail, axis, [(i, (i + 1) % count) for i in...  9.49 us
  transfers between devices with their start and end apart: 29, of which 12 were waited for; matrix products, arithmetic and copies ran while one was open for 12% of the time, Pallas kernels for 0%

commit v1 on v0

v1 whole, which is shorter than its diff:
```python
import functools

import jax
import jax.numpy as jnp
import numpy as np
from jax import lax
from jax.experimental import pallas as pl
from jax.experimental.pallas import tpu as pltpu
from jax.sharding import PartitionSpec as P

NV = 64
STEPS = 4
EPS = 1e-06
DT = 0.15
CX = CY = CH = 16
PAIRS = CH // 2
ROWS = CX * CY * PAIRS
XROW = CY * PAIRS
YROW = PAIRS
F32 = jnp.float32
VMEM = pl.BlockSpec(memory_space=pltpu.VMEM)
SMEM = pl.BlockSpec(memory_space=pltpu.SMEM)
ALL = ("gx", "gy", "ha")

X0, XD, XFA, XFB, XHA, XHB, Y0, YD, YFA, YFB, YHA, YHB, HFA, HFB, HHA, HHB = range(16)


def smooth(low, high, turn):
    mid = (turn * (4.0 / 3.0)) * turn + low * high + EPS
    twice = turn + turn
    return mid + high * twice, mid, mid - low * twice


def inverse(d):
    r = pl.reciprocal(d, approx=True)
    return r * (2.0 - d * r)


def upwind(cells):
    count = len(cells) - 5
    diff = [cells[n + 1] - cells[n] for n in range(count + 4)]
    curve = [diff[n + 1] - diff[n] for n in range(count + 3)]
    turn = [curve[n + 1] - curve[n] for n in range(count + 2)]
    bend = [turn[n] - turn[n + 1] for n in range(count + 1)]
    terms = [smooth(curve[n], curve[n + 1], turn[n]) for n in range(count + 2)]
    slopes = []
    for n in range(count):
        a, b, c = terms[n][0], terms[n + 1][1], terms[n + 2][2]
        bc, ac, ab = b * c, a * c, a * b
        alpha, beta, gamma = bc * bc, ac * ac, ab * ab
        gamma3 = 3.0 * gamma
        down = alpha + 6.0 * beta + gamma3
        up = alpha * (bend[n] + bend[n]) + gamma3 * bend[n + 1]
        inner = curve[n + 1] + (curve[n + 2] + curve[n + 2]) + up * inverse(down)
        slopes.append(diff[n + 2] + inner * (1.0 / 6.0))
    return slopes


def heading_terms(pairs, first_half):
    def odd(low, high):
        return jnp.where(first_half, low, high)

    count = len(pairs)
    turned = [pltpu.roll(p, NV, 1) for p in pairs]
    between = [odd(turned[n], turned[n + 1]) for n in range(count - 1)]
    diff_e = [between[n] - pairs[n] for n in range(count - 1)]
    diff_o = [pairs[n + 1] - between[n] for n in range(count - 1)]
    curve_e = [diff_o[n] - diff_e[n] for n in range(count - 1)]
    curve_o = [diff_e[n + 1] - diff_o[n] for n in range(count - 2)]
    turn_e = [curve_o[n] - curve_e[n] for n in range(count - 2)]
    turn_o = [curve_e[n + 1] - curve_o[n] for n in range(count - 2)]
    terms = [smooth(curve_e[n], curve_o[n], turn_e[n]) for n in range(count - 2)]
    mid_turned = [pltpu.roll(t[1], NV, 1) for t in terms]
    minus, plus = [None], [None]
    for n in range(1, count - 2):
        a, c = terms[n - 1][0], terms[n][2]
        b = odd(mid_turned[n - 1], mid_turned[n])
        bc, ac, ab = b * c, a * c, a * b
        alpha, beta, gamma = bc * bc, ac * ac, ab * ab
        bend_a = alpha * (turn_e[n - 1] - turn_o[n - 1])
        bend_c = gamma * (turn_o[n - 1] - turn_e[n])
        both = alpha + gamma
        shared = both + 6.0 * beta
        bends = bend_a + bend_c
        bends = bends + bends
        before, here = curve_o[n - 1], curve_e[n]
        sums = before + here
        down = shared + (gamma + gamma)
        inner = sums + here + (bends + bend_c) * inverse(down)
        minus.append(pltpu.roll(diff_e[n] + inner * (1.0 / 6.0), NV, 1))
        if n >= 2:
            down = shared + (alpha + alpha)
            inner = sums + before + (bends + bend_a) * inverse(down)
            plus.append(inner * (1.0 / 6.0) - diff_e[n])
        else:
            plus.append(None)
    return [
        jnp.minimum(odd(minus[n - 1], minus[n]), plus[n]) for n in range(2, count - 2)
    ]


def tile(ref, row):
    return ref[pl.ds(pl.multiple_of(row, 8), 8), :]


def put(ref, row, value):
    ref[pl.ds(pl.multiple_of(row, 8), 8), :] = value


def lanes_first_half():
    return lax.broadcasted_iota(jnp.int32, (8, 128), 1) < NV


def write_faces(prm, v_ref, faces):
    fxa, fxb, fya, fyb, fha, fhb = faces

    def body(n, _):
        for l in range(3):
            put(fxa, l * XROW + n * YROW, tile(v_ref, (prm[XFA] + l) * XROW + n * YROW))
            put(fxb, l * XROW + n * YROW, tile(v_ref, (prm[XFB] + l) * XROW + n * YROW))
            put(fya, l * XROW + n * YROW, tile(v_ref, n * XROW + (prm[YFA] + l) * YROW))
            put(fyb, l * XROW + n * YROW, tile(v_ref, n * XROW + (prm[YFB] + l) * YROW))
        for l in range(2):
            for t in range(2):
                base = n * XROW + t * 64
                out = (l * 32 + n * 2 + t) * 8
                put(fha, out, v_ref[pl.ds(base + prm[HFA] + l, 8, stride=8), :])
                put(fhb, out, v_ref[pl.ds(base + prm[HFB] + l, 8, stride=8), :])
        return 0

    lax.fori_loop(0, 16, body, 0)


def faces_kernel(prm, v_ref, *faces):
    write_faces(prm, v_ref, faces)


def line_cells(prm, v_ref, start, direction, stride, offset, first, last):
    return [
        tile(v_ref, (prm[start] + prm[direction] * i) * stride + offset)
        for i in range(first, last)
    ]


def inner_kernel(prm, v_ref, adx_ref, ady_ref, h_ref):
    first_half = lanes_first_half()
    adx, ady = adx_ref[...], ady_ref[...]
    zero = jnp.zeros((8, 128), F32)

    def along_x(y, _):
        slopes = upwind(line_cells(prm, v_ref, X0, XD, XROW, y * YROW, 0, 16))
        for i in range(16):
            row = (prm[X0] + prm[XD] * i) * XROW + y * YROW
            put(h_ref, row, adx * slopes[i - 3] if 3 <= i <= 13 else zero)
        return 0

    lax.fori_loop(0, 16, along_x, 0)

    def along_y(x, _):
        slopes = upwind(line_cells(prm, v_ref, Y0, YD, YROW, x * XROW, 0, 16))
        for i in range(3, 14):
            row = (prm[Y0] + prm[YD] * i) * YROW + x * XROW
            put(h_ref, row, tile(h_ref, row) + ady * slopes[i - 3])
        return 0

    lax.fori_loop(0, 16, along_y, 0)

    def along_h(n, _):
        base = n * 64
        pairs = [v_ref[pl.ds(base + p, 8, stride=8), :] for p in range(8)]
        for p, term in enumerate(heading_terms(pairs, first_half)):
            at = pl.ds(base + 2 + p, 8, stride=8)
            h_ref[at, :] = h_ref[at, :] + term
        return 0

    lax.fori_loop(0, 32, along_h, 0)


def outer_kernel(
    last, prm, v_ref, h_in, adx_ref, ady_ref, rxa, rxb, rya, ryb, rha, rhb, out_ref, *rest
):
    faces, (xs, ys, hs, h_ref) = rest[:-4], rest[-4:]
    first_half = lanes_first_half()
    adx, ady = adx_ref[...], ady_ref[...]

    def halos(n, _):
        for l in range(3):
            src = l * XROW + n * YROW
            put(xs, (prm[XHA] + prm[XD] * l) * XROW + n * YROW, tile(rxa, src))
            put(xs, (prm[XHB] + prm[XD] * l) * XROW + n * YROW, tile(rxb, src))
            put(ys, (prm[YHA] + prm[YD] * l) * XROW + n * YROW, tile(rya, src))
            put(ys, (prm[YHB] + prm[YD] * l) * XROW + n * YROW, tile(ryb, src))
        for l in range(2):
            for t in range(2):
                at = (n * 2 + t) * 8
                put(hs, (prm[HHA] + l) * 256 + at, tile(rha, l * 256 + at))
                put(hs, (prm[HHB] + l) * 256 + at, tile(rhb, l * 256 + at))
        return 0

    lax.fori_loop(0, 16, halos, 0)

    def along_x(y, _):
        at = y * YROW
        cells = [tile(xs, l * XROW + at) for l in range(3)]
        cells += line_cells(prm, v_ref, X0, XD, XROW, at, 0, 5)
        low = upwind(cells)
        cells = line_cells(prm, v_ref, X0, XD, XROW, at, 11, 16)
        cells += [tile(xs, l * XROW + at) for l in range(3, 5)]
        high = upwind(cells)
        for i, slope in list(zip(range(3), low)) + list(zip(range(14, 16), high)):
            row = (prm[X0] + prm[XD] * i) * XROW + at
            put(h_ref, row, tile(h_in, row) + adx * slope)
        for i in range(3, 14):
            row = (prm[X0] + prm[XD] * i) * XROW + at
            put(h_ref, row, tile(h_in, row))
        return 0

    lax.fori_loop(0, 16, along_x, 0)

    def along_y(x, _):
        at = x * YROW
        cells = [tile(ys, l * XROW + at) for l in range(3)]
        cells += line_cells(prm, v_ref, Y0, YD, YROW, x * XROW, 0, 5)
        low = upwind(cells)
        cells = line_cells(prm, v_ref, Y0, YD, YROW, x * XROW, 11, 16)
        cells += [tile(ys, l * XROW + at) for l in range(3, 5)]
        high = upwind(cells)
        for i, slope in list(zip(range(3), low)) + list(zip(range(14, 16), high)):
            row = (prm[Y0] + prm[YD] * i) * YROW + x * XROW
            put(h_ref, row, tile(h_ref, row) + ady * slope)
        return 0

    lax.fori_loop(0, 16, along_y, 0)

    def along_h(n, _):
        base = n * 64
        own = [v_ref[pl.ds(base + p, 8, stride=8), :] for p in range(8)]
        ring = [tile(hs, l * 256 + n * 8) for l in range(4)]
        low = heading_terms(ring[:2] + own[:4], first_half)
        high = heading_terms(own[4:] + ring[2:], first_half)
        for p in range(8):
            at = pl.ds(base + p, 8, stride=8)
            total = h_ref[at, :]
            if p < 2:
                total = total + low[p]
            if p > 5:
                total = total + high[p - 6]
            out_ref[at, :] = own[p] - DT * jnp.maximum(total, 0.0)
        return 0

    lax.fori_loop(0, 32, along_h, 0)
    if not last:
        write_faces(prm, out_ref, faces)


def call(body, name, outs, in_specs, scratch=(), flops=0, moved=4 << 20):
    return pl.pallas_call(
        body,
        name=name,
        out_shape=[jax.ShapeDtypeStruct(s, F32) for s in outs],
        in_specs=in_specs,
        out_specs=[VMEM] * len(outs),
        scratch_shapes=[pltpu.VMEM(s, F32) for s in scratch],
        cost_estimate=pl.CostEstimate(flops=flops, bytes_accessed=moved, transcendentals=0),
        compiler_params=pltpu.CompilerParams(vmem_limit_bytes=40 << 20),
    )


FACES = [(3 * XROW, 128)] * 4 + [(512, 128)] * 2
BLOCK = (ROWS, 128)


def exchange(faces):
    sides = (("gx", 0, False), ("gx", 1, False), ("gy", 0, False), ("gy", 1, False), ("ha", 0, True), ("ha", 1, True))
    arrived = []
    for face, (axis, offset, closed) in zip(faces, sides):
        count = lax.axis_size(axis)
        pairs = []
        for i in range(offset, count if closed else count - 1, 2):
            pairs += [(i, (i + 1) % count), ((i + 1) % count, i)]
        arrived.append(lax.ppermute(face, axis, pairs))
    return arrived


def drift_tables(blocks):
    angle = np.arange(blocks * CH) * (2.0 * np.pi / (blocks * CH))
    speeds = 0.5 + np.arange(NV) / (NV - 1)
    tables, signs = [], []
    for part in (np.cos(angle), np.sin(angle)):
        part = np.where(np.abs(part) < 1e-12, 0.0, part).reshape(blocks, CH)
        positive = (part >= 0).all(axis=1)
        assert (positive | (part <= 0).all(axis=1)).all()
        tables.append(np.abs(part[:, :, None] * speeds).reshape(blocks, PAIRS, 2 * NV).astype(np.float32))
        signs.append(np.where(positive, 1, -1))
    return tables, signs


def parameters(signs):
    gx, gy, ha = (lax.axis_index(a) for a in ALL)
    table = []
    for index, sign in ((gx, signs[0]), (gy, signs[1])):
        even = index % 2 == 0
        wind = jnp.asarray(sign, jnp.int32)[ha]
        high = jnp.where(wind > 0, 3, 2)
        low = jnp.where(wind > 0, 0, 5)
        table += [
            jnp.where(wind > 0, 0, 15),
            wind,
            jnp.where(even, 13, 0),
            jnp.where(even, 0, 13),
            jnp.where(even, high, low),
            jnp.where(even, low, high),
        ]
    even = ha % 2 == 0
    table += [jnp.where(even, 6, 0), jnp.where(even, 0, 6), jnp.where(even, 2, 0), jnp.where(even, 0, 2)]
    return jnp.stack([jnp.asarray(t, jnp.int32) for t in table])


def steps(initial_value, request):
    tables, signs = drift_tables(lax.axis_size("ha"))
    ha = lax.axis_index("ha")
    adx, ady = (jnp.asarray(t)[ha] for t in tables)
    prm = parameters(signs)
    value = initial_value.reshape(BLOCK)
    faces = call(faces_kernel, "faces", FACES, [SMEM, VMEM])(prm, value)
    for step in range(STEPS):
        last = step == STEPS - 1
        arrived = exchange(faces)
        if step < 3:
            request = lax.all_to_all(request, ALL[step], split_axis=step, concat_axis=step, tiled=True)
            request, arrived = lax.optimization_barrier((request, arrived))
        (part,) = call(inner_kernel, "inner", [BLOCK], [SMEM] + [VMEM] * 3, flops=30_000_000)(prm, value, adx, ady)
        out = call(
            functools.partial(outer_kernel, last),
            "outer",
            [BLOCK] + ([] if last else FACES),
            [SMEM] + [VMEM] * 10,
            scratch=[(6 * XROW, 128), (6 * XROW, 128), (4 * 256, 128), BLOCK],
            flops=15_000_000,
        )(prm, value, part, adx, ady, *arrived)
        value, faces = out[0], out[1:]
        if step < 2:
            faces, request = lax.optimization_barrier((faces, request))
    return value, request


def sample_kernel(rows_ref, v_ref, w_ref, out_ref, table, picked):
    first_half = lanes_first_half()

    def fill(n, _):
        pair = tile(v_ref, n * 8)
        turned = pltpu.roll(pair, NV, 1)
        between = jnp.where(first_half, turned, pltpu.roll(turned, 7, 0))
        table[pl.ds(n * 16, 8, stride=2), :] = pair
        table[pl.ds(n * 16 + 1, 8, stride=2), :] = between
        return 0

    lax.fori_loop(0, CX * CY, fill, 0)

    def pick(n, _):
        for u in range(8):
            s = n * 8 + u
            for j in range(4):
                row = rows_ref[s * 4 + j]
                for q, shift in enumerate((0, CH, CY * CH, CY * CH + CH)):
                    picked[pl.ds((q * 4 + j) * 256 + s, 1), :] = table[pl.ds(row + shift, 1), :]
        return 0

    lax.fori_loop(0, 32, pick, 0)
    lane = lax.broadcasted_iota(jnp.int32, (8, 128), 1)
    slot = lane & 3
    corner_shift = ((lane >> 2) & 1) + NV * ((lane >> 3) & 1)

    def weigh(n, _):
        w = tile(w_ref, n * 8)
        speeds = jnp.maximum(jnp.take_along_axis(w, 64 + slot, axis=1), 0.0).astype(jnp.int32) & (NV - 1)
        total = jnp.zeros((8, 128), F32)
        for j in range(4):
            at = jnp.take_along_axis(speeds, jnp.full((8, 128), j, jnp.int32), axis=1) + corner_shift
            for q in range(4):
                read = jnp.take_along_axis(tile(picked, (q * 4 + j) * 256 + n * 8), at, axis=1)
                total = jnp.where((slot == j) & ((lane >> 4) == q), read, total)
        total = total * w
        total = jnp.where(lane < 64, total, 0.0)
        for shift in (96, 112, 120, 124):
            total = total + pltpu.roll(total, shift, 1)
        out_ref[pl.ds(n * 8, 8), :] = total[:, :4]
        return 0

    lax.fori_loop(0, 32, weigh, 0)


def local(initial_value, corner, weights):
    slots = corner.shape[1]
    owners = corner.shape[2]
    sizes = [lax.axis_size(a) for a in ALL]
    request = jnp.concatenate(
        [weights.reshape(16 * slots, owners), corner.reshape(slots, owners).astype(F32)], axis=0
    )
    request = jnp.pad(request.T, ((0, 0), (0, 128 - 17 * slots))).reshape(*sizes, 128)
    value, request = steps(initial_value, request)
    request = request.reshape(owners, 128)
    codes = jnp.maximum(request[:, 64 : 64 + slots], 0.0).astype(jnp.int32).reshape(-1)
    (sums,) = call(
        sample_kernel,
        "samples",
        [(owners, slots)],
        [SMEM, VMEM, VMEM],
        scratch=[(2 * ROWS, 128), (16 * owners, 128)],
    )(codes // NV, value, request)
    sampled = lax.all_to_all(sums, ALL, split_axis=0, concat_axis=0, tiled=True)
    sampled = jnp.where(corner >= 0, sampled.T.reshape(corner.shape), 0.0)
    return value.reshape(initial_value.shape), sampled


def solution(mesh):
    return jax.shard_map(
        local,
        mesh=mesh,
        in_specs=(
            P("gx", "gy", "ha"),
            P(("gx", "gy", "ha"), None, None),
            P(("gx", "gy", "ha"), None, None, None),
        ),
        out_specs=(P("gx", "gy", "ha"), P(("gx", "gy", "ha"), None, None)),
        check_vma=False,
    )
```

time: 294 us -> 256 us (0.87)
  Pallas kernels: 0 us -> 132 us
  other arithmetic: 88.9 us -> 0.73 us
  waiting for transfers between devices: 64.9 us -> 11.8 us
  matrix products: 8.72 us -> 0 us
  starting transfers between devices: 83.4 us -> 75.8 us
  blocking collectives: 7.56 us -> 0 us
  local copies, waits for them, and re-layouts: 37.3 us -> 32.5 us
    pallas_call x0 -> x10, Pallas kernels: none -> 132 us  [the longest x4 47.2 us: steps(): call(functools.partial(outer_kernel, last), 'outer', [BLOCK] + ([] if las...]
    sub x16 -> x0, other arithmetic: 69.5 us -> none  [the longest x4 59.2 us: advance(): return level_set - time_step * jnp.maximum(hamiltonian, 0.0)]
    ppermute x24, waiting for transfers between devices: 28.5 us -> 0.06 us  [exchange(): arrived.append(lax.ppermute(face, axis, pairs))]
    all_to_all x5 -> x4, waiting for transfers between devices: 36.4 us -> 11.7 us  [the longest x1 11.7 us: local(): sampled = lax.all_to_all(sums, ALL, split_axis=0, concat_axis=0, tiled=True)]
    unnamed x30 -> x73, local copies, waits for them, and re-layouts: 3.55 us -> 24.4 us
    reduce_sum x9 -> x0, other arithmetic: 10 us -> none  [the longest x8 9.95 us: one_block(): jnp.sum(jnp.where(column_match[:, None, :, :], picked[:, :, None, :], 0.0...]
    concatenate x5 -> x0, local copies, waits for them, and re-layouts: 9.49 us -> none  [extended(): jnp.concatenate([lax.ppermute(tail, axis, [(i, (i + 1) % count) for i in...]
    ppermute x24, starting transfers between devices: 54.4 us -> 45.1 us  [exchange(): arrived.append(lax.ppermute(face, axis, pairs))]
  transfers between devices with their start and end apart: 29 -> 28, of which waited for: 12 -> 1; matrix products, arithmetic and copies ran while one was open for 12% -> 2% of each run, Pallas kernels for 0% -> 18%
where the time goes in v1:
time: 256 us; the launch traced here: 255 us
  Pallas kernels  132 us (52%)
  starting transfers between devices  75.8 us (30%)
  local copies, waits for them, and re-layouts  32.5 us (13%)
  waiting for transfers between devices  11.8 us (5%)
    pallas_call x4, Pallas kernels, steps(): call(functools.partial(outer_kernel, last), 'outer', [BLOCK] + ([] if las...  47.2 us
    ppermute x24, starting transfers between devices, exchange(): arrived.append(lax.ppermute(face, axis, pairs))  45.1 us
    pallas_call x4, Pallas kernels, steps(): call(inner_kernel, 'inner', [BLOCK], [SMEM] + [VMEM] * 3, flops=30000000)  44.9 us
    pallas_call x1, Pallas kernels, local(): call(sample_kernel, 'samples', [(owners, slots)], [SMEM, VMEM, VMEM], scr...  37.9 us
    unnamed x73, local copies, waits for them, and re-layouts  24.4 us
    all_to_all x1, starting transfers between devices, local(): sampled = lax.all_to_all(sums, ALL, split_axis=0, concat_axis=0, tiled=True)  15.9 us
    all_to_all x3, starting transfers between devices, steps(): lax.all_to_all(request, ALL[step], split_axis=step, concat_axis=step, til...  14.8 us
    all_to_all x1, waiting for transfers between devices, local(): sampled = lax.all_to_all(sums, ALL, split_axis=0, concat_axis=0, tiled=True)  11.7 us
  transfers between devices with their start and end apart: 28, of which 1 were waited for; matrix products, arithmetic and copies ran while one was open for 2% of the time, Pallas kernels for 18%

profile of v1, /device:TPU:1, one launch (start us, length us, event | category | flops | bytes accessed | tf_op | source)
XLA Modules:
  0.0 255.0 jit_solution(354294248868231871)
XLA Ops:
  7.3 1.8 faces.1
  9.1 2.5 collective-permute-start.4
  11.5 4.7 %collective-permute-start.5 = (f32[512,128]{1,0:T(8,128)}, f32[512,128]{1,0:T(8,128)S(1)}, u32[]{:S(2)}, u32[]{:S(2)}) collective-permute-start(f32[512,128]{1,0:T(8,128)} %get-tuple-element.69), channel_id=1, source_target_pairs={{1,2},{2,1},{3,4},{4,3},{5,6},{6,5},{7,0},{0,7},{9,10},{10,9},{11,... | collective-permute-start | bytes 786440 | tf_op jit(solution)/shard_map/ppermute | solution.py:281
  17.4 4.5 %collective-permute-start.1 = (f32[384,128]{1,0:T(8,128)}, f32[384,128]{1,0:T(8,128)S(1)}, u32[]{:S(2)}, u32[]{:S(2)}) collective-permute-start(f32[384,128]{1,0:T(8,128)} %get-tuple-element.65), channel_id=1, source_target_pairs={{64,128},{128,64},{65,129},{129,65},{66,130},{130,66},{67,131},{13... | collective-permute-start | bytes 589832 | tf_op jit(solution)/shard_map/ppermute | solution.py:281
  23.9 4.1 %all-to-all-start = ((f32[4,8,8,128]{3,2,1,0:T(8,128)}), f32[4,8,8,128]{3,2,1,0:T(8,128)S(1)}, u32[]{:S(2)}, u32[]{:S(2)}) async-start(f32[4,8,8,128]{3,2,1,0:T(8,128)} %bitcast.20), calls=%async_computation | async-start | bytes 262144 | tf_op jit(solution)/shard_map/all_to_all | solution.py:330
  28.7 11.2 %inner.4.h_in = f32[2048,128]{1,0:T(8,128)S(1)} custom-call(s32[16]{0:T(128)S(1)} %stack.53.prm, f32[2048,128]{1,0:T(8,128)S(1)} %reshape.53.v_ref, f32[8,128]{1,0:T(8,128)S(1)} %get-tuple-element.137.adx_ref, f32[8,128]{1,0:T(8,128)S(1)} %get-tuple-element.136.ady_ref), custom_call_target="tpu_custom_call" | custom-call | flops 30000000 | bytes 4194304 | tf_op jit(solution)/shard_map/inner/pallas_call | solution.py:332
  47.4 12.1 %outer.4 = (f32[2048,128]{1,0:T(8,128)S(1)}, f32[384,128]{1,0:T(8,128)S(1)}, f32[384,128]{1,0:T(8,128)}, f32[384,128]{1,0:T(8,128)}, f32[384,128]{1,0:T(8,128)}, /*index=5*/f32[512,128]{1,0:T(8,128)}, f32[512,128]{1,0:T(8,128)}) custom-call(s32[16]{0:T(128)S(1)} %stack.53.prm, f32[2048,128]{1,0:T(8,128)S(1)} %reshape.53.v_ref, f32[2048,128]{1,0:T(8,128)S(1)} %inner.4.h_in, ...), custom_call_target="tpu_custom_call" | custom-call | flops 15000000 | bytes 4194304 | tf_op jit(solution)/shard_map/outer/pallas_call | solution.py:333
  60.9 5.8 %collective-permute-start.7 = (f32[384,128]{1,0:T(8,128)}, f32[384,128]{1,0:T(8,128)S(1)}, u32[]{:S(2)}, u32[]{:S(2)}) collective-permute-start(f32[384,128]{1,0:T(8,128)} %get-tuple-element.86), channel_id=1, source_target_pairs={{64,128},{128,64},{65,129},{129,65},{66,130},{130,66},{67,131},{13... | collective-permute-start | bytes 589832 | tf_op jit(solution)/shard_map/ppermute | solution.py:281
  66.7 3.5 %collective-permute-start.8 = (f32[384,128]{1,0:T(8,128)}, f32[384,128]{1,0:T(8,128)S(1)}, u32[]{:S(2)}, u32[]{:S(2)}) collective-permute-start(f32[384,128]{1,0:T(8,128)} %get-tuple-element.87), channel_id=1, source_target_pairs={{0,8},{8,0},{16,24},{24,16},{32,40},{40,32},{48,56},{56,48},{1,9},... | collective-permute-start | bytes 589832 | tf_op jit(solution)/shard_map/ppermute | solution.py:281
  71.5 5.7 %all-to-all-start.1 = ((f32[4,8,8,128]{3,2,0,1:T(8,128)}), f32[4,8,8,128]{3,2,0,1:T(8,128)S(1)}, u32[]{:S(2)}, u32[]{:S(2)}) async-start(f32[4,8,8,128]{3,2,0,1:T(8,128)} %copy.41), calls=%async_computation.1 | async-start | bytes 262144 | tf_op jit(solution)/shard_map/all_to_all | solution.py:330
  77.2 11.2 %inner.5.h_in = f32[2048,128]{1,0:T(8,128)S(1)} custom-call(s32[16]{0:T(128)S(1)} %stack.53.prm, f32[2048,128]{1,0:T(8,128)S(1)} %get-tuple-element.76.v_ref, f32[8,128]{1,0:T(8,128)S(1)} %get-tuple-element.137.adx_ref, f32[8,128]{1,0:T(8,128)S(1)} %get-tuple-element.136.ady_ref), custom_call_target="tpu_custom_call" | custom-call | flops 30000000 | bytes 4194304 | tf_op jit(solution)/shard_map/inner/pallas_call | solution.py:332
  95.9 12.2 %outer.5 = (f32[2048,128]{1,0:T(8,128)S(1)}, f32[384,128]{1,0:T(8,128)}, f32[384,128]{1,0:T(8,128)}, f32[384,128]{1,0:T(8,128)}, f32[384,128]{1,0:T(8,128)}, /*index=5*/f32[512,128]{1,0:T(8,128)}, f32[512,128]{1,0:T(8,128)}) custom-call(s32[16]{0:T(128)S(1)} %stack.53.prm, f32[2048,128]{1,0:T(8,128)S(1)} %get-tuple-element.76.v_ref, ...), custom_call_target="tpu_custom_call" | custom-call | flops 15000000 | bytes 4194304 | tf_op jit(solution)/shard_map/outer/pallas_call | solution.py:333
  109.9 5.0 %all-to-all-start.2 = ((f32[4,8,8,128]{3,1,0,2:T(8,128)}), f32[4,8,8,128]{3,1,0,2:T(8,128)S(1)}, u32[]{:S(2)}, u32[]{:S(2)}) async-start(f32[4,8,8,128]{3,1,0,2:T(8,128)} %copy.42), calls=%async_computation.2 | async-start | bytes 262144 | tf_op jit(solution)/shard_map/all_to_all | solution.py:330
  114.9 4.2 %collective-permute-start.13 = (f32[384,128]{1,0:T(8,128)}, f32[384,128]{1,0:T(8,128)S(1)}, u32[]{:S(2)}, u32[]{:S(2)}) collective-permute-start(f32[384,128]{1,0:T(8,128)} %get-tuple-element.107), channel_id=1, source_target_pairs={{64,128},{128,64},{65,129},{129,65},{66,130},{130,66},{67,131},{13... | collective-permute-start | bytes 589832 | tf_op jit(solution)/shard_map/ppermute | solution.py:281
  121.0 11.2 %inner.6.h_in = f32[2048,128]{1,0:T(8,128)S(1)} custom-call(s32[16]{0:T(128)S(1)} %stack.53.prm, f32[2048,128]{1,0:T(8,128)S(1)} %get-tuple-element.97.v_ref, f32[8,128]{1,0:T(8,128)S(1)} %get-tuple-element.137.adx_ref, f32[8,128]{1,0:T(8,128)S(1)} %get-tuple-element.136.ady_ref), custom_call_target="tpu_custom_call" | custom-call | flops 30000000 | bytes 4194304 | tf_op jit(solution)/shard_map/inner/pallas_call | solution.py:332
  139.7 12.1 %outer.6 = (f32[2048,128]{1,0:T(8,128)S(1)}, f32[384,128]{1,0:T(8,128)}, f32[384,128]{1,0:T(8,128)}, f32[384,128]{1,0:T(8,128)}, f32[384,128]{1,0:T(8,128)S(1)}, /*index=5*/f32[512,128]{1,0:T(8,128)}, f32[512,128]{1,0:T(8,128)}) custom-call(s32[16]{0:T(128)S(1)} %stack.53.prm, f32[2048,128]{1,0:T(8,128)S(1)} %get-tuple-element.97.v_ref, ...), custom_call_target="tpu_custom_call" | custom-call | flops 15000000 | bytes 4194304 | tf_op jit(solution)/shard_map/outer/pallas_call | solution.py:333
  154.3 2.4 collective-permute-start.23
  156.7 4.3 %collective-permute-start.19 = (f32[384,128]{1,0:T(8,128)}, f32[384,128]{1,0:T(8,128)S(1)}, u32[]{:S(2)}, u32[]{:S(2)}) collective-permute-start(f32[384,128]{1,0:T(8,128)} %get-tuple-element.120), channel_id=1, source_target_pairs={{64,128},{128,64},{65,129},{129,65},{66,130},{130,66},{67,131},{13... | collective-permute-start | bytes 589832 | tf_op jit(solution)/shard_map/ppermute | solution.py:281
  161.0 3.5 %collective-permute-start.20 = (f32[384,128]{1,0:T(8,128)}, f32[384,128]{1,0:T(8,128)S(1)}, u32[]{:S(2)}, u32[]{:S(2)}) collective-permute-start(f32[384,128]{1,0:T(8,128)} %get-tuple-element.121), channel_id=1, source_target_pairs={{0,8},{8,0},{16,24},{24,16},{32,40},{40,32},{48,56},{56,48},{1,9},... | collective-permute-start | bytes 589832 | tf_op jit(solution)/shard_map/ppermute | solution.py:281
  164.9 11.2 %inner.7.h_in = f32[2048,128]{1,0:T(8,128)S(1)} custom-call(s32[16]{0:T(128)S(1)} %stack.53.prm, f32[2048,128]{1,0:T(8,128)S(1)} %get-tuple-element.118.v_ref, f32[8,128]{1,0:T(8,128)S(1)} %get-tuple-element.137.adx_ref, f32[8,128]{1,0:T(8,128)S(1)} %get-tuple-element.136.ady_ref), custom_call_target="tpu_custom_call" | custom-call | flops 30000000 | bytes 4194304 | tf_op jit(solution)/shard_map/inner/pallas_call | solution.py:332
  176.9 10.8 %outer.7.v_ref = f32[2048,128]{1,0:T(8,128)S(1)} custom-call(s32[16]{0:T(128)S(1)} %stack.53.prm, f32[2048,128]{1,0:T(8,128)S(1)} %get-tuple-element.118.v_ref, f32[2048,128]{1,0:T(8,128)S(1)} %inner.7.h_in, f32[8,128]{1,0:T(8,128)S(1)} %get-tuple-element.137.adx_ref, f32[8,128]{1,0:T(8,128)S(1)} %get-tuple-element.136.ady_ref, ...), custom_call_target="tpu_custom_call" | custom-call | flops 15000000 | bytes 4194304 | tf_op jit(solution)/shard_map/outer/pallas_call | solution.py:333
  187.7 37.9 %samples.1 = f32[256,4]{1,0:T(8,128)} custom-call(s32[1024]{0:T(1024)S(1)} %add_select_fusion.rows_ref, f32[2048,128]{1,0:T(8,128)S(1)} %outer.7.v_ref, f32[256,128]{1,0:T(8,128)S(1)} %bitcast.36), custom_call_target="tpu_custom_call" | custom-call | bytes 4194304 | tf_op jit(solution)/shard_map/samples/pallas_call | solution.py:404
  225.6 15.9 %all-to-all-start.3 = ((f32[256,1,4]{2,1,0:T(1,128)}), f32[256,1,4]{2,1,0:T(1,128)S(1)}, u32[]{:S(2)}, u32[]{:S(2)}) async-start(f32[256,1,4]{2,1,0:T(1,128)} %bitcast.23), calls=%async_computation.3 | async-start | bytes 262144 | tf_op jit(solution)/shard_map/all_to_all | solution.py:411
  242.6 11.7 %all-to-all-done.3 = f32[256,1,4]{2,1,0:T(1,128)S(1)} async-done(((f32[256,1,4]{2,1,0:T(1,128)}), f32[256,1,4]{2,1,0:T(1,128)S(1)}, u32[]{:S(2)}, u32[]{:S(2)}) %all-to-all-start.3) | async-done | bytes 4128 | tf_op jit(solution)/shard_map/all_to_all | solution.py:411
  (133 shorter events, 43.1 us)
Async XLA Ops:
  9.1 32.9 %collective-permute-start.4 = (f32[512,128]{1,0:T(8,128)}, f32[512,128]{1,0:T(8,128)S(1)}, u32[]{:S(2)}, u32[]{:S(2)}) collective-permute-start(f32[512,128]{1,0:T(8,128)} %get-tuple-element.68), channel_id=1, source_target_pairs={{0,1},{1,0},{2,3},{3,2},{4,5},{5,4},{6,7},{7,6},{8,9},{9,8},{10,11... | collective-permute-start | bytes 786440 | tf_op jit(solution)/shard_map/ppermute | solution.py:281
  11.5 30.5 %collective-permute-start.5 = (f32[512,128]{1,0:T(8,128)}, f32[512,128]{1,0:T(8,128)S(1)}, u32[]{:S(2)}, u32[]{:S(2)}) collective-permute-start(f32[512,128]{1,0:T(8,128)} %get-tuple-element.69), channel_id=1, source_target_pairs={{1,2},{2,1},{3,4},{4,3},{5,6},{6,5},{7,0},{0,7},{9,10},{10,9},{11,... | collective-permute-start | bytes 786440 | tf_op jit(solution)/shard_map/ppermute | solution.py:281
  17.4 22.5 %collective-permute-start.1 = (f32[384,128]{1,0:T(8,128)}, f32[384,128]{1,0:T(8,128)S(1)}, u32[]{:S(2)}, u32[]{:S(2)}) collective-permute-start(f32[384,128]{1,0:T(8,128)} %get-tuple-element.65), channel_id=1, source_target_pairs={{64,128},{128,64},{65,129},{129,65},{66,130},{130,66},{67,131},{13... | collective-permute-start | bytes 589832 | tf_op jit(solution)/shard_map/ppermute | solution.py:281
  22.0 18.6 %collective-permute-start.2 = (f32[384,128]{1,0:T(8,128)}, f32[384,128]{1,0:T(8,128)S(1)}, u32[]{:S(2)}, u32[]{:S(2)}) collective-permute-start(f32[384,128]{1,0:T(8,128)} %get-tuple-element.66), channel_id=1, source_target_pairs={{0,8},{8,0},{16,24},{24,16},{32,40},{40,32},{48,56},{56,48},{1,9},... | collective-permute-start | bytes 589832 | tf_op jit(solution)/shard_map/ppermute | solution.py:281
  22.4 18.9 %collective-permute-start.3 = (f32[384,128]{1,0:T(8,128)}, f32[384,128]{1,0:T(8,128)S(1)}, u32[]{:S(2)}, u32[]{:S(2)}) collective-permute-start(f32[384,128]{1,0:T(8,128)} %get-tuple-element.67), channel_id=1, source_target_pairs={{8,16},{16,8},{24,32},{32,24},{40,48},{48,40},{9,17},{17,9},{25,33... | collective-permute-start | bytes 589832 | tf_op jit(solution)/shard_map/ppermute | solution.py:281
  23.9 16.0 %all-to-all-start = ((f32[4,8,8,128]{3,2,1,0:T(8,128)}), f32[4,8,8,128]{3,2,1,0:T(8,128)S(1)}, u32[]{:S(2)}, u32[]{:S(2)}) async-start(f32[4,8,8,128]{3,2,1,0:T(8,128)} %bitcast.20), calls=%async_computation | async-start | bytes 262144 | tf_op jit(solution)/shard_map/all_to_all | solution.py:330
  59.5 31.1 %collective-permute-start.10 = (f32[512,128]{1,0:T(8,128)}, f32[512,128]{1,0:T(8,128)S(1)}, u32[]{:S(2)}, u32[]{:S(2)}) collective-permute-start(f32[512,128]{1,0:T(8,128)} %get-tuple-element.89), channel_id=1, source_target_pairs={{0,1},{1,0},{2,3},{3,2},{4,5},{5,4},{6,7},{7,6},{8,9},{9,8},{10,11... | collective-permute-start | bytes 786440 | tf_op jit(solution)/shard_map/ppermute | solution.py:281
  59.5 31.1 %collective-permute-start.11 = (f32[512,128]{1,0:T(8,128)}, f32[512,128]{1,0:T(8,128)S(1)}, u32[]{:S(2)}, u32[]{:S(2)}) collective-permute-start(f32[512,128]{1,0:T(8,128)} %get-tuple-element.90), channel_id=1, source_target_pairs={{1,2},{2,1},{3,4},{4,3},{5,6},{6,5},{7,0},{0,7},{9,10},{10,9},{11,... | collective-permute-start | bytes 786440 | tf_op jit(solution)/shard_map/ppermute | solution.py:281
  60.9 27.5 %collective-permute-start.7 = (f32[384,128]{1,0:T(8,128)}, f32[384,128]{1,0:T(8,128)S(1)}, u32[]{:S(2)}, u32[]{:S(2)}) collective-permute-start(f32[384,128]{1,0:T(8,128)} %get-tuple-element.86), channel_id=1, source_target_pairs={{64,128},{128,64},{65,129},{129,65},{66,130},{130,66},{67,131},{13... | collective-permute-start | bytes 589832 | tf_op jit(solution)/shard_map/ppermute | solution.py:281
  66.7 22.5 %collective-permute-start.8 = (f32[384,128]{1,0:T(8,128)}, f32[384,128]{1,0:T(8,128)S(1)}, u32[]{:S(2)}, u32[]{:S(2)}) collective-permute-start(f32[384,128]{1,0:T(8,128)} %get-tuple-element.87), channel_id=1, source_target_pairs={{0,8},{8,0},{16,24},{24,16},{32,40},{40,32},{48,56},{56,48},{1,9},... | collective-permute-start | bytes 589832 | tf_op jit(solution)/shard_map/ppermute | solution.py:281
  70.2 19.7 %collective-permute-start.9 = (f32[384,128]{1,0:T(8,128)}, f32[384,128]{1,0:T(8,128)S(1)}, u32[]{:S(2)}, u32[]{:S(2)}) collective-permute-start(f32[384,128]{1,0:T(8,128)} %get-tuple-element.88), channel_id=1, source_target_pairs={{8,16},{16,8},{24,32},{32,24},{40,48},{48,40},{9,17},{17,9},{25,33... | collective-permute-start | bytes 589832 | tf_op jit(solution)/shard_map/ppermute | solution.py:281
  71.5 16.9 %all-to-all-start.1 = ((f32[4,8,8,128]{3,2,0,1:T(8,128)}), f32[4,8,8,128]{3,2,0,1:T(8,128)S(1)}, u32[]{:S(2)}, u32[]{:S(2)}) async-start(f32[4,8,8,128]{3,2,0,1:T(8,128)} %copy.41), calls=%async_computation.1 | async-start | bytes 262144 | tf_op jit(solution)/shard_map/all_to_all | solution.py:330
  108.1 26.2 %collective-permute-start.16 = (f32[512,128]{1,0:T(8,128)}, f32[512,128]{1,0:T(8,128)S(1)}, u32[]{:S(2)}, u32[]{:S(2)}) collective-permute-start(f32[512,128]{1,0:T(8,128)} %get-tuple-element.110), channel_id=1, source_target_pairs={{0,1},{1,0},{2,3},{3,2},{4,5},{5,4},{6,7},{7,6},{8,9},{9,8},{10,11... | collective-permute-start | bytes 786440 | tf_op jit(solution)/shard_map/ppermute | solution.py:281
  108.9 25.5 %collective-permute-start.17 = (f32[512,128]{1,0:T(8,128)}, f32[512,128]{1,0:T(8,128)S(1)}, u32[]{:S(2)}, u32[]{:S(2)}) collective-permute-start(f32[512,128]{1,0:T(8,128)} %get-tuple-element.111), channel_id=1, source_target_pairs={{1,2},{2,1},{3,4},{4,3},{5,6},{6,5},{7,0},{0,7},{9,10},{10,9},{11,... | collective-permute-start | bytes 786440 | tf_op jit(solution)/shard_map/ppermute | solution.py:281
  109.9 24.4 %all-to-all-start.2 = ((f32[4,8,8,128]{3,1,0,2:T(8,128)}), f32[4,8,8,128]{3,1,0,2:T(8,128)S(1)}, u32[]{:S(2)}, u32[]{:S(2)}) async-start(f32[4,8,8,128]{3,1,0,2:T(8,128)} %copy.42), calls=%async_computation.2 | async-start | bytes 262144 | tf_op jit(solution)/shard_map/all_to_all | solution.py:330
  114.9 17.3 %collective-permute-start.13 = (f32[384,128]{1,0:T(8,128)}, f32[384,128]{1,0:T(8,128)S(1)}, u32[]{:S(2)}, u32[]{:S(2)}) collective-permute-start(f32[384,128]{1,0:T(8,128)} %get-tuple-element.107), channel_id=1, source_target_pairs={{64,128},{128,64},{65,129},{129,65},{66,130},{130,66},{67,131},{13... | collective-permute-start | bytes 589832 | tf_op jit(solution)/shard_map/ppermute | solution.py:281
  119.1 13.8 %collective-permute-start.14 = (f32[384,128]{1,0:T(8,128)}, f32[384,128]{1,0:T(8,128)S(1)}, u32[]{:S(2)}, u32[]{:S(2)}) collective-permute-start(f32[384,128]{1,0:T(8,128)} %get-tuple-element.108), channel_id=1, source_target_pairs={{0,8},{8,0},{16,24},{24,16},{32,40},{40,32},{48,56},{56,48},{1,9},... | collective-permute-start | bytes 589832 | tf_op jit(solution)/shard_map/ppermute | solution.py:281
  120.3 13.3 %collective-permute-start.15 = (f32[384,128]{1,0:T(8,128)}, f32[384,128]{1,0:T(8,128)S(1)}, u32[]{:S(2)}, u32[]{:S(2)}) collective-permute-start(f32[384,128]{1,0:T(8,128)} %get-tuple-element.109), channel_id=1, source_target_pairs={{8,16},{16,8},{24,32},{32,24},{40,48},{48,40},{9,17},{17,9},{25,33... | collective-permute-start | bytes 589832 | tf_op jit(solution)/shard_map/ppermute | solution.py:281
  152.5 24.3 %collective-permute-start.22 = (f32[512,128]{1,0:T(8,128)}, f32[512,128]{1,0:T(8,128)S(1)}, u32[]{:S(2)}, u32[]{:S(2)}) collective-permute-start(f32[512,128]{1,0:T(8,128)} %get-tuple-element.123), channel_id=1, source_target_pairs={{0,1},{1,0},{2,3},{3,2},{4,5},{5,4},{6,7},{7,6},{8,9},{9,8},{10,11... | collective-permute-start | bytes 786440 | tf_op jit(solution)/shard_map/ppermute | solution.py:281
  154.3 22.6 %collective-permute-start.23 = (f32[512,128]{1,0:T(8,128)}, f32[512,128]{1,0:T(8,128)S(1)}, u32[]{:S(2)}, u32[]{:S(2)}) collective-permute-start(f32[512,128]{1,0:T(8,128)} %get-tuple-element.124), channel_id=1, source_target_pairs={{1,2},{2,1},{3,4},{4,3},{5,6},{6,5},{7,0},{0,7},{9,10},{10,9},{11,... | collective-permute-start | bytes 786440 | tf_op jit(solution)/shard_map/ppermute | solution.py:281
  156.7 19.4 %collective-permute-start.18 = (f32[384,128]{1,0:T(8,128)}, f32[384,128]{1,0:T(8,128)S(1)}, u32[]{:S(2)}, u32[]{:S(2)}) collective-permute-start(f32[384,128]{1,0:T(8,128)} %get-tuple-element.119), channel_id=1, source_target_pairs={{0,64},{64,0},{128,192},{192,128},{1,65},{65,1},{129,193},{193,129... | collective-permute-start | bytes 589832 | tf_op jit(solution)/shard_map/ppermute | solution.py:281
  156.7 20.2 %collective-permute-start.19 = (f32[384,128]{1,0:T(8,128)}, f32[384,128]{1,0:T(8,128)S(1)}, u32[]{:S(2)}, u32[]{:S(2)}) collective-permute-start(f32[384,128]{1,0:T(8,128)} %get-tuple-element.120), channel_id=1, source_target_pairs={{64,128},{128,64},{65,129},{129,65},{66,130},{130,66},{67,131},{13... | collective-permute-start | bytes 589832 | tf_op jit(solution)/shard_map/ppermute | solution.py:281
  161.0 15.8 %collective-permute-start.20 = (f32[384,128]{1,0:T(8,128)}, f32[384,128]{1,0:T(8,128)S(1)}, u32[]{:S(2)}, u32[]{:S(2)}) collective-permute-start(f32[384,128]{1,0:T(8,128)} %get-tuple-element.121), channel_id=1, source_target_pairs={{0,8},{8,0},{16,24},{24,16},{32,40},{40,32},{48,56},{56,48},{1,9},... | collective-permute-start | bytes 589832 | tf_op jit(solution)/shard_map/ppermute | solution.py:281
  225.6 28.7 %all-to-all-start.3 = ((f32[256,1,4]{2,1,0:T(1,128)}), f32[256,1,4]{2,1,0:T(1,128)S(1)}, u32[]{:S(2)}, u32[]{:S(2)}) async-start(f32[256,1,4]{2,1,0:T(1,128)} %bitcast.23), calls=%async_computation.3 | async-start | bytes 262144 | tf_op jit(solution)/shard_map/all_to_all | solution.py:411
  (40 other events, 108.5 us)

commit v2 on v1

v2 whole, which is shorter than its diff:
```python
import functools

import jax
import jax.numpy as jnp
import numpy as np
from jax import lax
from jax.experimental import pallas as pl
from jax.experimental.pallas import tpu as pltpu
from jax.sharding import PartitionSpec as P

NV = 64
STEPS = 4
EPS = 1e-06
DT = 0.15
CX = CY = CH = 16
PAIRS = CH // 2
ROWS = CX * CY * PAIRS
XROW = CY * PAIRS
YROW = PAIRS
F32 = jnp.float32
VMEM = pl.BlockSpec(memory_space=pltpu.VMEM)
SMEM = pl.BlockSpec(memory_space=pltpu.SMEM)
ALL = ("gx", "gy", "ha")

def smooth(low, high, turn):
    mid = (turn * (4.0 / 3.0)) * turn + low * high + EPS
    twice = turn + turn
    return mid + high * twice, mid, mid - low * twice


def inverse(d):
    r = pl.reciprocal(d, approx=True)
    return r * (2.0 - d * r)


def upwind(cells):
    count = len(cells) - 5
    diff = [cells[n + 1] - cells[n] for n in range(count + 4)]
    curve = [diff[n + 1] - diff[n] for n in range(count + 3)]
    turn = [curve[n + 1] - curve[n] for n in range(count + 2)]
    bend = [turn[n] - turn[n + 1] for n in range(count + 1)]
    terms = [smooth(curve[n], curve[n + 1], turn[n]) for n in range(count + 2)]
    slopes = []
    for n in range(count):
        a, b, c = terms[n][0], terms[n + 1][1], terms[n + 2][2]
        bc, ac, ab = b * c, a * c, a * b
        alpha, beta, gamma = bc * bc, ac * ac, ab * ab
        gamma3 = 3.0 * gamma
        down = alpha + 6.0 * beta + gamma3
        up = alpha * (bend[n] + bend[n]) + gamma3 * bend[n + 1]
        inner = curve[n + 1] + (curve[n + 2] + curve[n + 2]) + up * inverse(down)
        slopes.append(diff[n + 2] + inner * (1.0 / 6.0))
    return slopes


def heading_terms(pairs, turned, first_half):
    count = len(pairs)
    between = [jnp.where(first_half, turned[n], turned[n + 1]) for n in range(count - 1)]
    diff_e = [between[n] - pairs[n] for n in range(count - 1)]
    diff_o = [pairs[n + 1] - between[n] for n in range(count - 1)]
    curve_e = [diff_o[n] - diff_e[n] for n in range(count - 1)]
    curve_o = [diff_e[n + 1] - diff_o[n] for n in range(count - 2)]
    turn_e = [curve_o[n] - curve_e[n] for n in range(count - 2)]
    turn_o = [curve_e[n + 1] - curve_o[n] for n in range(count - 2)]
    even = [smooth(curve_e[n], curve_o[n], turn_e[n]) for n in range(count - 2)]
    odd = [smooth(curve_o[n], curve_e[n + 1], turn_o[n]) for n in range(count - 2)]

    def inner_sum(a, b, c, before, here, bend_a, bend_c):
        bc, ac, ab = b * c, a * c, a * b
        alpha, beta, gamma = bc * bc, ac * ac, ab * ab
        gamma3 = 3.0 * gamma
        down = alpha + 6.0 * beta + gamma3
        up = alpha * (bend_a + bend_a) + gamma3 * bend_c
        return before + (here + here) + up * inverse(down)

    result = []
    for n in range(2, count - 2):
        bend_m, bend_0, bend_p = (
            turn_o[n - 2] - turn_e[n - 1],
            turn_e[n - 1] - turn_o[n - 1],
            turn_o[n - 1] - turn_e[n],
        )
        minus = inner_sum(
            odd[n - 2][0], even[n - 1][1], odd[n - 1][2], curve_e[n - 1], curve_o[n - 1], bend_m, bend_0
        )
        plus = inner_sum(
            even[n][2], odd[n - 1][1], even[n - 1][0], curve_e[n], curve_o[n - 1], bend_p, bend_0
        )
        sixth = 1.0 / 6.0
        result.append(jnp.minimum(diff_o[n - 1] + minus * sixth, plus * sixth - diff_e[n]))
    return result


def tile(ref, row):
    return ref[pl.ds(pl.multiple_of(row, 8), 8), :]


def put(ref, row, value):
    ref[pl.ds(pl.multiple_of(row, 8), 8), :] = value


def lanes_first_half():
    return lax.broadcasted_iota(jnp.int32, (8, 128), 1) < NV


def scalars(signs):
    ha = lax.axis_index("ha")
    found = []
    for axis, sign in (("gx", signs[0]), ("gy", signs[1])):
        even = lax.rem(lax.axis_index(axis), 2) == 0
        wind = jnp.int32(int(sign[0]))
        for block in range(1, len(sign)):
            wind = jnp.where(ha == block, jnp.int32(int(sign[block])), wind)
        ahead = wind > 0
        high, low = jnp.where(ahead, 3, 2), jnp.where(ahead, 0, 5)
        found.append(
            (
                jnp.where(ahead, 0, 15),
                wind,
                jnp.where(even, 13, 0),
                jnp.where(even, 0, 13),
                jnp.where(even, high, low),
                jnp.where(even, low, high),
            )
        )
    even = lax.rem(ha, 2) == 0
    found.append(
        (jnp.where(even, 6, 0), jnp.where(even, 0, 6), jnp.where(even, 2, 0), jnp.where(even, 0, 2))
    )
    return found


def write_faces(where, v_ref, faces):
    (_, _, fx_a, fx_b, _, _), (_, _, fy_a, fy_b, _, _), (fh_a, fh_b, _, _) = where
    fxa, fxb, fya, fyb, fha, fhb = faces

    def body(n, _):
        for l in range(3):
            put(fxa, l * XROW + n * YROW, tile(v_ref, (fx_a + l) * XROW + n * YROW))
            put(fxb, l * XROW + n * YROW, tile(v_ref, (fx_b + l) * XROW + n * YROW))
            put(fya, l * XROW + n * YROW, tile(v_ref, n * XROW + (fy_a + l) * YROW))
            put(fyb, l * XROW + n * YROW, tile(v_ref, n * XROW + (fy_b + l) * YROW))
        for l in range(2):
            for t in range(2):
                base = n * XROW + t * 64
                out = (l * 32 + n * 2 + t) * 8
                put(fha, out, v_ref[pl.ds(base + fh_a + l, 8, stride=8), :])
                put(fhb, out, v_ref[pl.ds(base + fh_b + l, 8, stride=8), :])
        return 0

    lax.fori_loop(0, 16, body, 0, unroll=2)


def native(x, t, p):
    return x, pl.ds(8 * t, 8), pl.ds(128 * p, 128)


def first_kernel(signs, in_ref, v_ref, *faces):
    def body(x, _):
        for t in range(2):
            for p in range(8):
                v_ref[pl.ds(x * XROW + t * 64 + p, 8, stride=8), :] = in_ref[native(x, t, p)]
        return 0

    lax.fori_loop(0, 16, body, 0)
    write_faces(scalars(signs), v_ref, faces)


def inner_kernel(signs, v_ref, adx_ref, ady_ref, h_ref, turned_ref):
    (x_start, x_dir, *_), (y_start, y_dir, *_), _ = scalars(signs)
    first_half = lanes_first_half()
    adx, ady = adx_ref[...], ady_ref[...]
    zero = jnp.zeros((8, 128), F32)
    turned_ref[...] = pltpu.roll(v_ref[...], NV, 1)
    xs = [(x_start + x_dir * i) * XROW for i in range(16)]
    ys = [(y_start + y_dir * i) * YROW for i in range(16)]

    def along_x(y, _):
        slopes = upwind([tile(v_ref, row + y * YROW) for row in xs])
        for i in range(16):
            put(h_ref, xs[i] + y * YROW, adx * slopes[i - 3] if 3 <= i <= 13 else zero)
        return 0

    lax.fori_loop(0, 16, along_x, 0)

    def along_y(x, _):
        slopes = upwind([tile(v_ref, row + x * XROW) for row in ys])
        for i in range(3, 14):
            row = ys[i] + x * XROW
            put(h_ref, row, tile(h_ref, row) + ady * slopes[i - 3])
        return 0

    lax.fori_loop(0, 16, along_y, 0)

    def along_h(n, _):
        at = [pl.ds(n * 64 + p, 8, stride=8) for p in range(8)]
        terms = heading_terms([v_ref[a, :] for a in at], [turned_ref[a, :] for a in at], first_half)
        for a, term in zip(at[2:6], terms):
            h_ref[a, :] = h_ref[a, :] + term
        return 0

    lax.fori_loop(0, 32, along_h, 0)


def outer_kernel(
    signs, last, v_ref, h_in, turned_ref, adx_ref, ady_ref, rxa, rxb, rya, ryb, rha, rhb, *rest
):
    out_ref, others = rest[0], rest[1:-5]
    xs, ys, hs, hs_turned, h_ref = rest[-5:]
    where = scalars(signs)
    (x_start, x_dir, _, _, xh_a, xh_b), (y_start, y_dir, _, _, yh_a, yh_b), (_, _, hh_a, hh_b) = where
    first_half = lanes_first_half()
    adx, ady = adx_ref[...], ady_ref[...]
    for l in range(2):
        hs[pl.ds(pl.multiple_of((hh_a + l) * 256, 256), 256), :] = rha[pl.ds(l * 256, 256), :]
        hs[pl.ds(pl.multiple_of((hh_b + l) * 256, 256), 256), :] = rhb[pl.ds(l * 256, 256), :]
    hs_turned[...] = pltpu.roll(hs[...], NV, 1)
    for l in range(3):
        part = pl.ds(l * XROW, XROW)
        for ref, got, base, step in (
            (xs, rxa, xh_a, x_dir),
            (xs, rxb, xh_b, x_dir),
            (ys, rya, yh_a, y_dir),
            (ys, ryb, yh_b, y_dir),
        ):
            ref[pl.ds(pl.multiple_of((base + step * l) * XROW, XROW), XROW), :] = got[part, :]
    x_rows = [(x_start + x_dir * i) * XROW for i in range(16)]
    y_rows = [(y_start + y_dir * i) * YROW for i in range(16)]

    def edges(halo, at, rows, offset):
        own = {i: tile(v_ref, rows[i] + offset) for i in (0, 1, 2, 3, 4, 11, 12, 13, 14, 15)}
        ring = [tile(halo, l * XROW + at) for l in range(5)]
        low = upwind(ring[:3] + [own[i] for i in range(5)])
        high = upwind([own[i] for i in range(11, 16)] + ring[3:])
        return list(zip(range(3), low)) + list(zip(range(14, 16), high))

    def along_x(y, _):
        at = y * YROW
        for i, slope in edges(xs, at, x_rows, at):
            put(h_ref, x_rows[i] + at, tile(h_in, x_rows[i] + at) + adx * slope)
        for i in range(3, 14):
            put(h_ref, x_rows[i] + at, tile(h_in, x_rows[i] + at))
        return 0

    lax.fori_loop(0, 16, along_x, 0)

    def along_y(x, _):
        for i, slope in edges(ys, x * YROW, y_rows, x * XROW):
            row = y_rows[i] + x * XROW
            put(h_ref, row, tile(h_ref, row) + ady * slope)
        return 0

    lax.fori_loop(0, 16, along_y, 0)

    def along_h(n, _):
        at = [pl.ds(n * 64 + p, 8, stride=8) for p in range(8)]
        own = [v_ref[a, :] for a in at]
        own_turned = [turned_ref[a, :] for a in at]
        ring = [tile(hs, l * 256 + n * 8) for l in range(4)]
        ring_turned = [tile(hs_turned, l * 256 + n * 8) for l in range(4)]
        low = heading_terms(ring[:2] + own[:4], ring_turned[:2] + own_turned[:4], first_half)
        high = heading_terms(own[4:] + ring[2:], own_turned[4:] + ring_turned[2:], first_half)
        for p in range(8):
            total = h_ref[at[p], :]
            if p < 2:
                total = total + low[p]
            if p > 5:
                total = total + high[p - 6]
            value = own[p] - DT * jnp.maximum(total, 0.0)
            out_ref[at[p], :] = value
            if last:
                others[0][native(n // 2, lax.rem(n, 2), p)] = value
        return 0

    lax.fori_loop(0, 32, along_h, 0)
    if not last:
        write_faces(where, out_ref, others)


def call(body, name, outs, in_specs, scratch=(), flops=0, moved=4 << 20):
    return pl.pallas_call(
        body,
        name=name,
        out_shape=[jax.ShapeDtypeStruct(s, F32) for s in outs],
        in_specs=in_specs,
        out_specs=[VMEM] * len(outs),
        scratch_shapes=[pltpu.VMEM(s, F32) for s in scratch],
        cost_estimate=pl.CostEstimate(flops=flops, bytes_accessed=moved, transcendentals=0),
        compiler_params=pltpu.CompilerParams(vmem_limit_bytes=40 << 20),
    )


FACES = [(3 * XROW, 128)] * 4 + [(512, 128)] * 2
BLOCK = (ROWS, 128)


def exchange(faces):
    sides = (("gx", 0, False), ("gx", 1, False), ("gy", 0, False), ("gy", 1, False), ("ha", 0, True), ("ha", 1, True))
    arrived = []
    for face, (axis, offset, closed) in zip(faces, sides):
        count = lax.axis_size(axis)
        pairs = []
        for i in range(offset, count if closed else count - 1, 2):
            pairs += [(i, (i + 1) % count), ((i + 1) % count, i)]
        arrived.append(lax.ppermute(face, axis, pairs))
    return arrived


def drift_tables(blocks):
    angle = np.arange(blocks * CH) * (2.0 * np.pi / (blocks * CH))
    speeds = 0.5 + np.arange(NV) / (NV - 1)
    tables, signs = [], []
    for part in (np.cos(angle), np.sin(angle)):
        part = np.where(np.abs(part) < 1e-12, 0.0, part).reshape(blocks, CH)
        positive = (part >= 0).all(axis=1)
        assert (positive | (part <= 0).all(axis=1)).all()
        tables.append(np.abs(part[:, :, None] * speeds).reshape(blocks, PAIRS, 2 * NV).astype(np.float32))
        signs.append(np.where(positive, 1, -1))
    return tables, signs


def steps(initial_value, request):
    tables, signs = drift_tables(lax.axis_size("ha"))
    ha = lax.axis_index("ha")
    adx, ady = (jnp.asarray(t)[ha] for t in tables)
    value, *faces = call(functools.partial(first_kernel, signs), "first", [BLOCK] + FACES, [VMEM])(initial_value)
    for step in range(STEPS):
        last = step == STEPS - 1
        arrived = exchange(faces)
        if step < 3:
            request = lax.all_to_all(request, ALL[step], split_axis=step, concat_axis=step, tiled=True)
        part, turned = call(
            functools.partial(inner_kernel, signs), "inner", [BLOCK] * 2, [VMEM] * 3, flops=30_000_000
        )(value, adx, ady)
        if step < 3:
            request, ady = lax.optimization_barrier((request, ady))
        value, *faces = call(
            functools.partial(outer_kernel, signs, last),
            "outer",
            [BLOCK] + ([initial_value.shape] if last else FACES),
            [VMEM] * 11,
            scratch=[(6 * XROW, 128), (6 * XROW, 128), (1024, 128), (1024, 128), BLOCK],
            flops=15_000_000,
        )(value, part, turned, adx, ady, *arrived)
    return value, faces[0], request


def sample_kernel(rows_ref, v_ref, at_ref, w_ref, out_ref, table, picked):
    first_half = lanes_first_half()

    def fill(n, _):
        tiles = [tile(v_ref, n * 256 + 8 * u) for u in range(32)]
        turned = [pltpu.roll(t, NV, 1) for t in tiles]
        for u in range(32):
            between = jnp.where(first_half, turned[u], pltpu.roll(turned[u], 7, 0))
            table[pl.ds(n * 512 + u * 16, 8, stride=2), :] = tiles[u]
            table[pl.ds(n * 512 + u * 16 + 1, 8, stride=2), :] = between
        return 0

    lax.fori_loop(0, 8, fill, 0)

    def pick(n, _):
        for u in range(8):
            s = n * 8 + u
            for j in range(4):
                row = rows_ref[s * 4 + j]
                for q, shift in enumerate((0, CH, CY * CH, CY * CH + CH)):
                    picked[pl.ds((q * 4 + j) * 256 + s, 1), :] = table[pl.ds(row + shift, 1), :]
        return 0

    lax.fori_loop(0, 32, pick, 0)
    lane = lax.broadcasted_iota(jnp.int32, (8, 128), 1)
    masks = [[((lane & 3) == j) & ((lane >> 4) == q) for q in range(4)] for j in range(4)]

    def weigh(n, _):
        for u in range(8):
            group = n * 8 + u
            total = jnp.zeros((8, 128), F32)
            for j in range(4):
                at = tile(at_ref, j * 256 + group * 8)
                for q in range(4):
                    read = jnp.take_along_axis(tile(picked, (q * 4 + j) * 256 + group * 8), at, axis=1)
                    total = jnp.where(masks[j][q], read, total)
            put(table, group * 8, total * tile(w_ref, group * 8))
        return 0

    lax.fori_loop(0, 4, weigh, 0)
    spread = lax.broadcasted_iota(jnp.int32, (128, 128), 0)
    slot = lax.broadcasted_iota(jnp.int32, (128, 128), 1)
    adder = ((spread < 64) & ((spread & 3) == slot)).astype(F32)
    sums = jnp.dot(
        table[pl.ds(0, 256), :], adder, precision=lax.Precision.HIGHEST, preferred_element_type=F32
    )
    out_ref[...] = sums[:, :4]


def local(initial_value, corner, weights):
    slots = corner.shape[1]
    owners = corner.shape[2]
    sizes = [lax.axis_size(a) for a in ALL]
    request = jnp.concatenate(
        [weights.reshape(16 * slots, owners), corner.reshape(slots, owners).astype(F32)], axis=0
    )
    request = jnp.pad(request.T, ((0, 0), (0, 128 - 17 * slots))).reshape(*sizes, 128)
    value, final, request = steps(initial_value, request)
    request = request.reshape(owners, 128)
    codes = jnp.maximum(request[:, 64 : 64 + slots], 0.0).astype(jnp.int32)
    lane = jnp.arange(128, dtype=jnp.int32)
    reads = (codes.T % NV)[:, :, None] + (((lane >> 2) & 1) + NV * ((lane >> 3) & 1))[None, None, :]
    (sums,) = call(
        sample_kernel,
        "samples",
        [(owners, slots)],
        [SMEM, VMEM, VMEM, VMEM],
        scratch=[(2 * ROWS, 128), (16 * owners, 128)],
    )(codes.reshape(-1) // NV, value, reads.reshape(slots * owners, 128), request)
    sampled = lax.all_to_all(sums, ALL, split_axis=0, concat_axis=0, tiled=True)
    sampled = jnp.where(corner >= 0, sampled.T.reshape(corner.shape), 0.0)
    return final, sampled


def solution(mesh):
    return jax.shard_map(
        local,
        mesh=mesh,
        in_specs=(
            P("gx", "gy", "ha"),
            P(("gx", "gy", "ha"), None, None),
            P(("gx", "gy", "ha"), None, None, None),
        ),
        out_specs=(P("gx", "gy", "ha"), P(("gx", "gy", "ha"), None, None)),
        check_vma=False,
    )
```

time: 256 us -> 171 us (0.67)
  Pallas kernels: 132 us -> 49.1 us
  blocking collectives: 0 us -> 23 us
  starting transfers between devices: 75.8 us -> 59.2 us
  local copies, waits for them, and re-layouts: 32.5 us -> 28.4 us
  waiting for transfers between devices: 11.8 us -> 7.97 us
    pallas_call x10, Pallas kernels: 132 us -> 49.1 us  [the longest x4 22.5 us: steps(): call(functools.partial(outer_kernel, signs, last), 'outer', [BLOCK] + ([i...]
    all_to_all x0 -> x1, blocking collectives: none -> 23 us  [local(): sampled = lax.all_to_all(sums, ALL, split_axis=0, concat_axis=0, tiled=True)]
    all_to_all x1 -> x0, starting transfers between devices: 15.9 us -> none  [local(): sampled = lax.all_to_all(sums, ALL, split_axis=0, concat_axis=0, tiled=True)]
    all_to_all x1 -> x0, waiting for transfers between devices: 11.7 us -> none  [local(): sampled = lax.all_to_all(sums, ALL, split_axis=0, concat_axis=0, tiled=True)]
    all_to_all x3, waiting for transfers between devices: 0.01 us -> 4.15 us  [steps(): lax.all_to_all(request, ALL[step], split_axis=step, concat_axis=step, til...]
    ppermute x24, waiting for transfers between devices: 0.06 us -> 3.82 us  [exchange(): arrived.append(lax.ppermute(face, axis, pairs))]
    unnamed x73 -> x76, local copies, waits for them, and re-layouts: 24.4 us -> 23.7 us
  transfers between devices with their start and end apart: 28 -> 27, of which waited for: 1 -> 4; matrix products, arithmetic and copies ran while one was open for 2% -> 3% of each run, Pallas kernels for 18% -> 12%
where the time goes in v2:
time: 171 us; the launch traced here: 170 us
  starting transfers between devices  59.2 us (35%)
  Pallas kernels  49.1 us (29%)
  local copies, waits for them, and re-layouts  28.4 us (17%)
  blocking collectives  23 us (13%)
  waiting for transfers between devices  7.97 us (5%)
    ppermute x24, starting transfers between devices, exchange(): arrived.append(lax.ppermute(face, axis, pairs))  43.4 us
    unnamed x76, local copies, waits for them, and re-layouts  23.7 us
    all_to_all x1, blocking collectives, local(): sampled = lax.all_to_all(sums, ALL, split_axis=0, concat_axis=0, tiled=True)  23 us
    pallas_call x4, Pallas kernels, steps(): call(functools.partial(outer_kernel, signs, last), 'outer', [BLOCK] + ([i...  22.5 us
    pallas_call x4, Pallas kernels, steps(): call(functools.partial(inner_kernel, signs), 'inner', [BLOCK] * 2, [VMEM]...  20.1 us
    all_to_all x3, starting transfers between devices, steps(): lax.all_to_all(request, ALL[step], split_axis=step, concat_axis=step, til...  15.7 us
    pallas_call x1, Pallas kernels, local(): call(sample_kernel, 'samples', [(owners, slots)], [SMEM, VMEM, VMEM, VMEM...  5.09 us
    all_to_all x3, waiting for transfers between devices, steps(): lax.all_to_all(request, ALL[step], split_axis=step, concat_axis=step, til...  4.15 us
  transfers between devices with their start and end apart: 27, of which 4 were waited for; matrix products, arithmetic and copies ran while one was open for 3% of the time, Pallas kernels for 12%

profile of v2, /device:TPU:1, one launch (start us, length us, event | category | flops | bytes accessed | tf_op | source)
XLA Modules:
  0.0 169.6 jit_solution(17357935879120277902)
XLA Ops:
  3.3 2.5 %collective-permute-start.4 = (f32[512,128]{1,0:T(8,128)}, f32[512,128]{1,0:T(8,128)S(1)}, u32[]{:S(2)}, u32[]{:S(2)}) collective-permute-start(f32[512,128]{1,0:T(8,128)} %get-tuple-element.54), channel_id=1, source_target_pairs={{0,1},{1,0},{2,3},{3,2},{4,5},{5,4},{6,7},{7,6},{8,9},{9,8},{10,11... | collective-permute-start | bytes 786440 | tf_op jit(solution)/shard_map/ppermute | solution.py:305
  5.7 4.7 %collective-permute-start.5 = (f32[512,128]{1,0:T(8,128)}, f32[512,128]{1,0:T(8,128)S(1)}, u32[]{:S(2)}, u32[]{:S(2)}) collective-permute-start(f32[512,128]{1,0:T(8,128)} %get-tuple-element.55), channel_id=1, source_target_pairs={{1,2},{2,1},{3,4},{4,3},{5,6},{6,5},{7,0},{0,7},{9,10},{10,9},{11,... | collective-permute-start | bytes 786440 | tf_op jit(solution)/shard_map/ppermute | solution.py:305
  12.4 4.4 %all-to-all-start = ((f32[4,8,8,128]{3,2,1,0:T(8,128)}), f32[4,8,8,128]{3,2,1,0:T(8,128)S(1)}, u32[]{:S(2)}, u32[]{:S(2)}) async-start(f32[4,8,8,128]{3,2,1,0:T(8,128)} %bitcast.4), calls=%async_computation | async-start | bytes 262144 | tf_op jit(solution)/shard_map/all_to_all | solution.py:331
  16.8 5.0 %collective-permute-start.1 = (f32[384,128]{1,0:T(8,128)}, f32[384,128]{1,0:T(8,128)S(1)}, u32[]{:S(2)}, u32[]{:S(2)}) collective-permute-start(f32[384,128]{1,0:T(8,128)} %get-tuple-element.51), channel_id=1, source_target_pairs={{64,128},{128,64},{65,129},{129,65},{66,130},{130,66},{67,131},{13... | collective-permute-start | bytes 589832 | tf_op jit(solution)/shard_map/ppermute | solution.py:305
  24.3 5.0 %inner.4 = (f32[2048,128]{1,0:T(8,128)S(1)}, f32[2048,128]{1,0:T(8,128)S(1)}) custom-call(f32[2048,128]{1,0:T(8,128)S(1)} %get-tuple-element.46.v_ref, f32[8,128]{1,0:T(8,128)S(1)} %dynamic-slice_bitcast_fusion.1.adx_ref, f32[8,128]{1,0:T(8,128)S(1)} %dynamic-slice_bitcast_fusion.ady_ref), custom_call_target="tpu_custom_call" | custom-call | flops 30000000 | bytes 4194304 | tf_op jit(solution)/shard_map/inner/pallas_call | solution.py:332
  39.0 5.8 %outer.4 = (f32[2048,128]{1,0:T(8,128)S(1)}, f32[384,128]{1,0:T(8,128)}, f32[384,128]{1,0:T(8,128)}, f32[384,128]{1,0:T(8,128)}, f32[384,128]{1,0:T(8,128)}, /*index=5*/f32[512,128]{1,0:T(8,128)}, f32[512,128]{1,0:T(8,128)}) custom-call(f32[2048,128]{1,0:T(8,128)S(1)} %get-tuple-element.46.v_ref, f32[2048,128]{1,0:T(8,128)S(1)} %get-tuple-element.47.h_in, ...), custom_call_target="tpu_custom_call" | custom-call | flops 15000000 | bytes 4194304 | tf_op jit(solution)/shard_map/outer/pallas_call | solution.py:337
  45.4 7.3 %all-to-all-start.1 = ((f32[4,8,8,128]{3,2,0,1:T(8,128)}), f32[4,8,8,128]{3,2,0,1:T(8,128)S(1)}, u32[]{:S(2)}, u32[]{:S(2)}) async-start(f32[4,8,8,128]{3,2,0,1:T(8,128)} %copy.43), calls=%async_computation.1 | async-start | bytes 262144 | tf_op jit(solution)/shard_map/all_to_all | solution.py:331
  54.2 4.1 %all-to-all-done.1 = f32[4,8,8,128]{3,2,0,1:T(8,128)S(1)} async-done(((f32[4,8,8,128]{3,2,0,1:T(8,128)}), f32[4,8,8,128]{3,2,0,1:T(8,128)S(1)}, u32[]{:S(2)}, u32[]{:S(2)}) %all-to-all-start.1) | async-done | bytes 131104 | tf_op jit(solution)/shard_map/all_to_all | solution.py:331
  59.1 4.0 %all-to-all-start.2 = ((f32[4,8,8,128]{3,1,0,2:T(8,128)}), f32[4,8,8,128]{3,1,0,2:T(8,128)}, u32[]{:S(2)}, u32[]{:S(2)}) async-start(f32[4,8,8,128]{3,1,0,2:T(8,128)} %copy.44), calls=%async_computation.2 | async-start | bytes 262144 | tf_op jit(solution)/shard_map/all_to_all | solution.py:331
  63.1 4.6 %collective-permute-start.7 = (f32[384,128]{1,0:T(8,128)}, f32[384,128]{1,0:T(8,128)S(1)}, u32[]{:S(2)}, u32[]{:S(2)}) collective-permute-start(f32[384,128]{1,0:T(8,128)} %get-tuple-element.62), channel_id=1, source_target_pairs={{64,128},{128,64},{65,129},{129,65},{66,130},{130,66},{67,131},{13... | collective-permute-start | bytes 589832 | tf_op jit(solution)/shard_map/ppermute | solution.py:305
  68.5 5.0 %inner.5 = (f32[2048,128]{1,0:T(8,128)S(1)}, f32[2048,128]{1,0:T(8,128)S(1)}) custom-call(f32[2048,128]{1,0:T(8,128)S(1)} %get-tuple-element.56.v_ref, f32[8,128]{1,0:T(8,128)S(1)} %dynamic-slice_bitcast_fusion.1.adx_ref, f32[8,128]{1,0:T(8,128)S(1)} %dynamic-slice_bitcast_fusion.ady_ref), custom_call_target="tpu_custom_call" | custom-call | flops 30000000 | bytes 4194304 | tf_op jit(solution)/shard_map/inner/pallas_call | solution.py:332
  83.9 5.6 %outer.5 = (f32[2048,128]{1,0:T(8,128)S(1)}, f32[384,128]{1,0:T(8,128)}, f32[384,128]{1,0:T(8,128)S(1)}, f32[384,128]{1,0:T(8,128)S(1)}, f32[384,128]{1,0:T(8,12...) custom-call(f32[2048,128]{1,0:T(8,128)S(1)} %get-tuple-element.56.v_ref, f32[2048,128]{1,0:T(8,128)S(1)} %get-tuple-element.57.h_in, ...), custom_call_target="tpu_custom_call" | custom-call | flops 15000000 | bytes 4194304 | tf_op jit(solution)/shard_map/outer/pallas_call | solution.py:337
  93.2 2.4 %collective-permute-start.17 = (f32[512,128]{1,0:T(8,128)}, f32[512,128]{1,0:T(8,128)S(1)}, u32[]{:S(2)}, u32[]{:S(2)}) collective-permute-start(f32[512,128]{1,0:T(8,128)} %get-tuple-element.77), channel_id=1, source_target_pairs={{1,2},{2,1},{3,4},{4,3},{5,6},{6,5},{7,0},{0,7},{9,10},{10,9},{11,... | collective-permute-start | bytes 786440 | tf_op jit(solution)/shard_map/ppermute | solution.py:305
  95.8 3.3 %collective-permute-start.13 = (f32[384,128]{1,0:T(8,128)}, f32[384,128]{1,0:T(8,128)S(1)}, u32[]{:S(2)}, u32[]{:S(2)}) collective-permute-start(f32[384,128]{1,0:T(8,128)} %copy-done.31), channel_id=1, source_target_pairs={{64,128},{128,64},{65,129},{129,65},{66,130},{130,66},{67,131},{13... | collective-permute-start | bytes 589832 | tf_op jit(solution)/shard_map/ppermute | solution.py:305
  99.2 2.8 %collective-permute-start.14 = (f32[384,128]{1,0:T(8,128)S(1)}, f32[384,128]{1,0:T(8,128)S(1)}, u32[]{:S(2)}, u32[]{:S(2)}) collective-permute-start(f32[384,128]{1,0:T(8,128)S(1)} %copy-done.28), channel_id=1, source_target_pairs={{0,8},{8,0},{16,24},{24,16},{32,40},{40,32},{48,56},{56,48},{1,9},... | collective-permute-start | bytes 589832 | tf_op jit(solution)/shard_map/ppermute | solution.py:305
  102.8 5.0 %inner.6 = (f32[2048,128]{1,0:T(8,128)S(1)}, f32[2048,128]{1,0:T(8,128)S(1)}) custom-call(f32[2048,128]{1,0:T(8,128)S(1)} %get-tuple-element.67.v_ref, f32[8,128]{1,0:T(8,128)S(1)} %dynamic-slice_bitcast_fusion.1.adx_ref, f32[8,128]{1,0:T(8,128)S(1)} %dynamic-slice_bitcast_fusion.ady_ref), custom_call_target="tpu_custom_call" | custom-call | flops 30000000 | bytes 4194304 | tf_op jit(solution)/shard_map/inner/pallas_call | solution.py:332
  109.3 5.6 %outer.6 = (f32[2048,128]{1,0:T(8,128)S(1)}, f32[384,128]{1,0:T(8,128)}, f32[384,128]{1,0:T(8,128)S(1)}, f32[384,128]{1,0:T(8,128)S(1)}, f32[384,128]{1,0:T(8,12...) custom-call(f32[2048,128]{1,0:T(8,128)S(1)} %get-tuple-element.67.v_ref, f32[2048,128]{1,0:T(8,128)S(1)} %get-tuple-element.68.h_in, ...), custom_call_target="tpu_custom_call" | custom-call | flops 15000000 | bytes 4194304 | tf_op jit(solution)/shard_map/outer/pallas_call | solution.py:337
  117.0 2.3 %collective-permute-start.23 = (f32[512,128]{1,0:T(8,128)}, f32[512,128]{1,0:T(8,128)S(1)}, u32[]{:S(2)}, u32[]{:S(2)}) collective-permute-start(f32[512,128]{1,0:T(8,128)} %get-tuple-element.86), channel_id=1, source_target_pairs={{1,2},{2,1},{3,4},{4,3},{5,6},{6,5},{7,0},{0,7},{9,10},{10,9},{11,... | collective-permute-start | bytes 786440 | tf_op jit(solution)/shard_map/ppermute | solution.py:305
  119.6 5.3 %collective-permute-start.19 = (f32[384,128]{1,0:T(8,128)}, f32[384,128]{1,0:T(8,128)S(1)}, u32[]{:S(2)}, u32[]{:S(2)}) collective-permute-start(f32[384,128]{1,0:T(8,128)} %copy-done.34), channel_id=1, source_target_pairs={{64,128},{128,64},{65,129},{129,65},{66,130},{130,66},{67,131},{13... | collective-permute-start | bytes 589832 | tf_op jit(solution)/shard_map/ppermute | solution.py:305
  124.9 3.1 %collective-permute-start.20 = (f32[384,128]{1,0:T(8,128)S(1)}, f32[384,128]{1,0:T(8,128)S(1)}, u32[]{:S(2)}, u32[]{:S(2)}) collective-permute-start(f32[384,128]{1,0:T(8,128)S(1)} %copy-done.33), channel_id=1, source_target_pairs={{0,8},{8,0},{16,24},{24,16},{32,40},{40,32},{48,56},{56,48},{1,9},... | collective-permute-start | bytes 589832 | tf_op jit(solution)/shard_map/ppermute | solution.py:305
  128.7 5.0 %inner.7 = (f32[2048,128]{1,0:T(8,128)S(1)}, f32[2048,128]{1,0:T(8,128)S(1)}) custom-call(f32[2048,128]{1,0:T(8,128)S(1)} %get-tuple-element.78.v_ref, f32[8,128]{1,0:T(8,128)S(1)} %dynamic-slice_bitcast_fusion.1.adx_ref, f32[8,128]{1,0:T(8,128)S(1)} %dynamic-slice_bitcast_fusion.ady_ref), custom_call_target="tpu_custom_call" | custom-call | flops 30000000 | bytes 4194304 | tf_op jit(solution)/shard_map/inner/pallas_call | solution.py:332
  135.4 5.5 %outer.7 = (f32[2048,128]{1,0:T(8,128)S(1)}, f32[16,16,1024]{2,1,0:T(8,128)}) custom-call(f32[2048,128]{1,0:T(8,128)S(1)} %get-tuple-element.78.v_ref, f32[2048,128]{1,0:T(8,128)S(1)} %get-tuple-element.79.h_in, f32[2048,128]{1,0:T(8,128)S(1)} %get-tuple-element.80.turned_ref, f32[8,128]{1,0:T(8,128)S(1)} %dynamic-slice_bitcast_fusion.1.adx_ref, ...), custom_call_target="tpu_custom_call" | custom-call | flops 15000000 | bytes 4194304 | tf_op jit(solution)/shard_map/outer/pallas_call | solution.py:337
  140.8 5.1 %samples.1 = f32[256,4]{1,0:T(8,128)S(1)} custom-call(s32[1024]{0:T(1024)S(1)} %add_select_fusion.1.rows_ref, f32[2048,128]{1,0:T(8,128)S(1)} %get-tuple-element.89.v_ref, s32[1024,128]{1,0:T(8,128)S(1)} %broadcast_add_fusion.at_ref, f32[256,128]{1,0:T(8,128)S(1)} %bitcast.27), custom_call_target="tpu_custom_call" | custom-call | bytes 4194304 | tf_op jit(solution)/shard_map/samples/pallas_call | solution.py:410
  145.9 23.0 %all_to_all.27 = f32[256,1,4]{2,1,0:T(1,128)S(1)} all-to-all(f32[256,1,4]{2,1,0:T(1,128)S(1)} %bitcast.28), channel_id=1, replica_groups=mesh['gx'=4,'gy'=8,'ha'=8] {'gx','gy','ha'}, dimensions={0} | all-to-all | bytes 8192 | tf_op jit(solution)/shard_map/all_to_all | solution.py:417
  (135 shorter events, 42.1 us)
Async XLA Ops:
  3.3 29.1 %collective-permute-start.4 = (f32[512,128]{1,0:T(8,128)}, f32[512,128]{1,0:T(8,128)S(1)}, u32[]{:S(2)}, u32[]{:S(2)}) collective-permute-start(f32[512,128]{1,0:T(8,128)} %get-tuple-element.54), channel_id=1, source_target_pairs={{0,1},{1,0},{2,3},{3,2},{4,5},{5,4},{6,7},{7,6},{8,9},{9,8},{10,11... | collective-permute-start | bytes 786440 | tf_op jit(solution)/shard_map/ppermute | solution.py:305
  5.7 26.7 %collective-permute-start.5 = (f32[512,128]{1,0:T(8,128)}, f32[512,128]{1,0:T(8,128)S(1)}, u32[]{:S(2)}, u32[]{:S(2)}) collective-permute-start(f32[512,128]{1,0:T(8,128)} %get-tuple-element.55), channel_id=1, source_target_pairs={{1,2},{2,1},{3,4},{4,3},{5,6},{6,5},{7,0},{0,7},{9,10},{10,9},{11,... | collective-permute-start | bytes 786440 | tf_op jit(solution)/shard_map/ppermute | solution.py:305
  10.4 11.9 %collective-permute-start = (f32[384,128]{1,0:T(8,128)S(1)}, f32[384,128]{1,0:T(8,128)S(1)}, u32[]{:S(2)}, u32[]{:S(2)}) collective-permute-start(f32[384,128]{1,0:T(8,128)S(1)} %get-tuple-element.50), channel_id=1, source_target_pairs={{0,64},{64,0},{128,192},{192,128},{1,65},{65,1},{129,193},{193,129... | collective-permute-start | bytes 589832 | tf_op jit(solution)/shard_map/ppermute | solution.py:305
  12.4 17.9 %all-to-all-start = ((f32[4,8,8,128]{3,2,1,0:T(8,128)}), f32[4,8,8,128]{3,2,1,0:T(8,128)S(1)}, u32[]{:S(2)}, u32[]{:S(2)}) async-start(f32[4,8,8,128]{3,2,1,0:T(8,128)} %bitcast.4), calls=%async_computation | async-start | bytes 262144 | tf_op jit(solution)/shard_map/all_to_all | solution.py:331
  16.8 13.5 %collective-permute-start.1 = (f32[384,128]{1,0:T(8,128)}, f32[384,128]{1,0:T(8,128)S(1)}, u32[]{:S(2)}, u32[]{:S(2)}) collective-permute-start(f32[384,128]{1,0:T(8,128)} %get-tuple-element.51), channel_id=1, source_target_pairs={{64,128},{128,64},{65,129},{129,65},{66,130},{130,66},{67,131},{13... | collective-permute-start | bytes 589832 | tf_op jit(solution)/shard_map/ppermute | solution.py:305
  21.9 9.2 %collective-permute-start.2 = (f32[384,128]{1,0:T(8,128)}, f32[384,128]{1,0:T(8,128)S(1)}, u32[]{:S(2)}, u32[]{:S(2)}) collective-permute-start(f32[384,128]{1,0:T(8,128)} %get-tuple-element.52), channel_id=1, source_target_pairs={{0,8},{8,0},{16,24},{24,16},{32,40},{40,32},{48,56},{56,48},{1,9},... | collective-permute-start | bytes 589832 | tf_op jit(solution)/shard_map/ppermute | solution.py:305
  22.3 9.4 %collective-permute-start.3 = (f32[384,128]{1,0:T(8,128)}, f32[384,128]{1,0:T(8,128)S(1)}, u32[]{:S(2)}, u32[]{:S(2)}) collective-permute-start(f32[384,128]{1,0:T(8,128)} %get-tuple-element.53), channel_id=1, source_target_pairs={{8,16},{16,8},{24,32},{32,24},{40,48},{48,40},{9,17},{17,9},{25,33... | collective-permute-start | bytes 589832 | tf_op jit(solution)/shard_map/ppermute | solution.py:305
  44.8 23.0 %collective-permute-start.6 = (f32[384,128]{1,0:T(8,128)}, f32[384,128]{1,0:T(8,128)S(1)}, u32[]{:S(2)}, u32[]{:S(2)}) collective-permute-start(f32[384,128]{1,0:T(8,128)} %get-tuple-element.61), channel_id=1, source_target_pairs={{0,64},{64,0},{128,192},{192,128},{1,65},{65,1},{129,193},{193,129... | collective-permute-start | bytes 589832 | tf_op jit(solution)/shard_map/ppermute | solution.py:305
  45.4 12.9 %all-to-all-start.1 = ((f32[4,8,8,128]{3,2,0,1:T(8,128)}), f32[4,8,8,128]{3,2,0,1:T(8,128)S(1)}, u32[]{:S(2)}, u32[]{:S(2)}) async-start(f32[4,8,8,128]{3,2,0,1:T(8,128)} %copy.43), calls=%async_computation.1 | async-start | bytes 262144 | tf_op jit(solution)/shard_map/all_to_all | solution.py:331
  52.7 25.5 %collective-permute-start.10 = (f32[512,128]{1,0:T(8,128)}, f32[512,128]{1,0:T(8,128)S(1)}, u32[]{:S(2)}, u32[]{:S(2)}) collective-permute-start(f32[512,128]{1,0:T(8,128)} %get-tuple-element.65), channel_id=1, source_target_pairs={{0,1},{1,0},{2,3},{3,2},{4,5},{5,4},{6,7},{7,6},{8,9},{9,8},{10,11... | collective-permute-start | bytes 786440 | tf_op jit(solution)/shard_map/ppermute | solution.py:305
  52.7 25.5 %collective-permute-start.11 = (f32[512,128]{1,0:T(8,128)}, f32[512,128]{1,0:T(8,128)S(1)}, u32[]{:S(2)}, u32[]{:S(2)}) collective-permute-start(f32[512,128]{1,0:T(8,128)} %get-tuple-element.66), channel_id=1, source_target_pairs={{1,2},{2,1},{3,4},{4,3},{5,6},{6,5},{7,0},{0,7},{9,10},{10,9},{11,... | collective-permute-start | bytes 786440 | tf_op jit(solution)/shard_map/ppermute | solution.py:305
  59.1 15.4 %all-to-all-start.2 = ((f32[4,8,8,128]{3,1,0,2:T(8,128)}), f32[4,8,8,128]{3,1,0,2:T(8,128)}, u32[]{:S(2)}, u32[]{:S(2)}) async-start(f32[4,8,8,128]{3,1,0,2:T(8,128)} %copy.44), calls=%async_computation.2 | async-start | bytes 262144 | tf_op jit(solution)/shard_map/all_to_all | solution.py:331
  63.1 12.4 %collective-permute-start.7 = (f32[384,128]{1,0:T(8,128)}, f32[384,128]{1,0:T(8,128)S(1)}, u32[]{:S(2)}, u32[]{:S(2)}) collective-permute-start(f32[384,128]{1,0:T(8,128)} %get-tuple-element.62), channel_id=1, source_target_pairs={{64,128},{128,64},{65,129},{129,65},{66,130},{130,66},{67,131},{13... | collective-permute-start | bytes 589832 | tf_op jit(solution)/shard_map/ppermute | solution.py:305
  67.6 9.2 %collective-permute-start.8 = (f32[384,128]{1,0:T(8,128)}, f32[384,128]{1,0:T(8,128)S(1)}, u32[]{:S(2)}, u32[]{:S(2)}) collective-permute-start(f32[384,128]{1,0:T(8,128)} %get-tuple-element.63), channel_id=1, source_target_pairs={{0,8},{8,0},{16,24},{24,16},{32,40},{40,32},{48,56},{56,48},{1,9},... | collective-permute-start | bytes 589832 | tf_op jit(solution)/shard_map/ppermute | solution.py:305
  67.8 9.8 %collective-permute-start.9 = (f32[384,128]{1,0:T(8,128)}, f32[384,128]{1,0:T(8,128)S(1)}, u32[]{:S(2)}, u32[]{:S(2)}) collective-permute-start(f32[384,128]{1,0:T(8,128)} %get-tuple-element.64), channel_id=1, source_target_pairs={{8,16},{16,8},{24,32},{32,24},{40,48},{48,40},{9,17},{17,9},{25,33... | collective-permute-start | bytes 589832 | tf_op jit(solution)/shard_map/ppermute | solution.py:305
  91.6 17.7 %collective-permute-start.16 = (f32[512,128]{1,0:T(8,128)}, f32[512,128]{1,0:T(8,128)S(1)}, u32[]{:S(2)}, u32[]{:S(2)}) collective-permute-start(f32[512,128]{1,0:T(8,128)} %get-tuple-element.76), channel_id=1, source_target_pairs={{0,1},{1,0},{2,3},{3,2},{4,5},{5,4},{6,7},{7,6},{8,9},{9,8},{10,11... | collective-permute-start | bytes 786440 | tf_op jit(solution)/shard_map/ppermute | solution.py:305
  93.2 16.1 %collective-permute-start.17 = (f32[512,128]{1,0:T(8,128)}, f32[512,128]{1,0:T(8,128)S(1)}, u32[]{:S(2)}, u32[]{:S(2)}) collective-permute-start(f32[512,128]{1,0:T(8,128)} %get-tuple-element.77), channel_id=1, source_target_pairs={{1,2},{2,1},{3,4},{4,3},{5,6},{6,5},{7,0},{0,7},{9,10},{10,9},{11,... | collective-permute-start | bytes 786440 | tf_op jit(solution)/shard_map/ppermute | solution.py:305
  95.8 12.0 %collective-permute-start.13 = (f32[384,128]{1,0:T(8,128)}, f32[384,128]{1,0:T(8,128)S(1)}, u32[]{:S(2)}, u32[]{:S(2)}) collective-permute-start(f32[384,128]{1,0:T(8,128)} %copy-done.31), channel_id=1, source_target_pairs={{64,128},{128,64},{65,129},{129,65},{66,130},{130,66},{67,131},{13... | collective-permute-start | bytes 589832 | tf_op jit(solution)/shard_map/ppermute | solution.py:305
  99.2 10.1 %collective-permute-start.14 = (f32[384,128]{1,0:T(8,128)S(1)}, f32[384,128]{1,0:T(8,128)S(1)}, u32[]{:S(2)}, u32[]{:S(2)}) collective-permute-start(f32[384,128]{1,0:T(8,128)S(1)} %copy-done.28), channel_id=1, source_target_pairs={{0,8},{8,0},{16,24},{24,16},{32,40},{40,32},{48,56},{56,48},{1,9},... | collective-permute-start | bytes 589832 | tf_op jit(solution)/shard_map/ppermute | solution.py:305
  117.0 18.4 %collective-permute-start.22 = (f32[512,128]{1,0:T(8,128)}, f32[512,128]{1,0:T(8,128)S(1)}, u32[]{:S(2)}, u32[]{:S(2)}) collective-permute-start(f32[512,128]{1,0:T(8,128)} %get-tuple-element.85), channel_id=1, source_target_pairs={{0,1},{1,0},{2,3},{3,2},{4,5},{5,4},{6,7},{7,6},{8,9},{9,8},{10,11... | collective-permute-start | bytes 786440 | tf_op jit(solution)/shard_map/ppermute | solution.py:305
  117.0 18.4 %collective-permute-start.23 = (f32[512,128]{1,0:T(8,128)}, f32[512,128]{1,0:T(8,128)S(1)}, u32[]{:S(2)}, u32[]{:S(2)}) collective-permute-start(f32[512,128]{1,0:T(8,128)} %get-tuple-element.86), channel_id=1, source_target_pairs={{1,2},{2,1},{3,4},{4,3},{5,6},{6,5},{7,0},{0,7},{9,10},{10,9},{11,... | collective-permute-start | bytes 786440 | tf_op jit(solution)/shard_map/ppermute | solution.py:305
  119.4 8.6 %collective-permute-start.18 = (f32[384,128]{1,0:T(8,128)}, f32[384,128]{1,0:T(8,128)S(1)}, u32[]{:S(2)}, u32[]{:S(2)}) collective-permute-start(f32[384,128]{1,0:T(8,128)} %get-tuple-element.81), channel_id=1, source_target_pairs={{0,64},{64,0},{128,192},{192,128},{1,65},{65,1},{129,193},{193,129... | collective-permute-start | bytes 589832 | tf_op jit(solution)/shard_map/ppermute | solution.py:305
  119.6 14.1 %collective-permute-start.19 = (f32[384,128]{1,0:T(8,128)}, f32[384,128]{1,0:T(8,128)S(1)}, u32[]{:S(2)}, u32[]{:S(2)}) collective-permute-start(f32[384,128]{1,0:T(8,128)} %copy-done.34), channel_id=1, source_target_pairs={{64,128},{128,64},{65,129},{129,65},{66,130},{130,66},{67,131},{13... | collective-permute-start | bytes 589832 | tf_op jit(solution)/shard_map/ppermute | solution.py:305
  124.9 10.4 %collective-permute-start.20 = (f32[384,128]{1,0:T(8,128)S(1)}, f32[384,128]{1,0:T(8,128)S(1)}, u32[]{:S(2)}, u32[]{:S(2)}) collective-permute-start(f32[384,128]{1,0:T(8,128)S(1)} %copy-done.33), channel_id=1, source_target_pairs={{0,8},{8,0},{16,24},{24,16},{32,40},{40,32},{48,56},{56,48},{1,9},... | collective-permute-start | bytes 589832 | tf_op jit(solution)/shard_map/ppermute | solution.py:305
  (40 other events, 104.2 us)

commit v3 on v2

--- a/solution.py
+++ b/solution.py
@@ -155,7 +155,7 @@
     return x, pl.ds(8 * t, 8), pl.ds(128 * p, 128)
 
 
-def first_kernel(signs, in_ref, v_ref, *faces):
+def first_kernel(signs, in_ref, _, v_ref, *faces):
     def body(x, _):
         for t in range(2):
             for p in range(8):
@@ -286,7 +286,7 @@
         out_specs=[VMEM] * len(outs),
         scratch_shapes=[pltpu.VMEM(s, F32) for s in scratch],
         cost_estimate=pl.CostEstimate(flops=flops, bytes_accessed=moved, transcendentals=0),
-        compiler_params=pltpu.CompilerParams(vmem_limit_bytes=40 << 20),
+        compiler_params=pltpu.CompilerParams(vmem_limit_bytes=16 << 20),
     )
 
 
@@ -323,17 +323,16 @@
     tables, signs = drift_tables(lax.axis_size("ha"))
     ha = lax.axis_index("ha")
     adx, ady = (jnp.asarray(t)[ha] for t in tables)
-    value, *faces = call(functools.partial(first_kernel, signs), "first", [BLOCK] + FACES, [VMEM])(initial_value)
+    request = lax.all_to_all(request, ALL, split_axis=0, concat_axis=0, tiled=True)
+    value, *faces = call(
+        functools.partial(first_kernel, signs), "first", [BLOCK] + FACES, [VMEM, pl.BlockSpec(memory_space=pl.ANY)]
+    )(initial_value, request)
     for step in range(STEPS):
         last = step == STEPS - 1
         arrived = exchange(faces)
-        if step < 3:
-            request = lax.all_to_all(request, ALL[step], split_axis=step, concat_axis=step, tiled=True)
         part, turned = call(
             functools.partial(inner_kernel, signs), "inner", [BLOCK] * 2, [VMEM] * 3, flops=30_000_000
         )(value, adx, ady)
-        if step < 3:
-            request, ady = lax.optimization_barrier((request, ady))
         value, *faces = call(
             functools.partial(outer_kernel, signs, last),
             "outer",
@@ -397,13 +396,11 @@
 def local(initial_value, corner, weights):
     slots = corner.shape[1]
     owners = corner.shape[2]
-    sizes = [lax.axis_size(a) for a in ALL]
     request = jnp.concatenate(
         [weights.reshape(16 * slots, owners), corner.reshape(slots, owners).astype(F32)], axis=0
     )
-    request = jnp.pad(request.T, ((0, 0), (0, 128 - 17 * slots))).reshape(*sizes, 128)
+    request = jnp.pad(request.T, ((0, 0), (0, 128 - 17 * slots)))
     value, final, request = steps(initial_value, request)
-    request = request.reshape(owners, 128)
     codes = jnp.maximum(request[:, 64 : 64 + slots], 0.0).astype(jnp.int32)
     lane = jnp.arange(128, dtype=jnp.int32)
     reads = (codes.T % NV)[:, :, None] + (((lane >> 2) & 1) + NV * ((lane >> 3) & 1))[None, None, :]

time: 171 us -> 154 us (0.901)
  blocking collectives: 23 us -> 52.9 us
  starting transfers between devices: 59.2 us -> 36.4 us
  local copies, waits for them, and re-layouts: 28.4 us -> 7.25 us
    all_to_all x0 -> x1, blocking collectives: none -> 28.3 us  [steps(): lax.all_to_all(request, ALL, split_axis=0, concat_axis=0, tiled=True)]
    unnamed x76 -> x25, local copies, waits for them, and re-layouts: 23.7 us -> 5.31 us
    all_to_all x3 -> x0, starting transfers between devices: 15.7 us -> none  [steps(): lax.all_to_all(request, ALL[step], split_axis=step, concat_axis=step, til...]
    ppermute x24, starting transfers between devices: 43.4 us -> 36.4 us  [exchange(): arrived.append(lax.ppermute(face, axis, pairs))]
    all_to_all x3 -> x0, waiting for transfers between devices: 4.15 us -> none  [steps(): lax.all_to_all(request, ALL[step], split_axis=step, concat_axis=step, til...]
    ppermute x24, waiting for transfers between devices: 3.82 us -> 7.15 us  [exchange(): arrived.append(lax.ppermute(face, axis, pairs))]
    optimization_barrier x3 -> x0, local copies, waits for them, and re-layouts: 2.4 us -> none  [steps(): request, ady = lax.optimization_barrier((request, ady))]
  transfers between devices with their start and end apart: 27 -> 24, of which waited for: 4 -> 4; matrix products, arithmetic and copies ran while one was open for 3% -> 1% of each run, Pallas kernels for 12% -> 13%
where the time goes in v3:
time: 154 us
  blocking collectives  52.9 us (34%)
  Pallas kernels  48 us (31%)
  starting transfers between devices  36.4 us (24%)
  local copies, waits for them, and re-layouts  7.25 us (5%)
  waiting for transfers between devices  7.15 us (5%)
    ppermute x24, starting transfers between devices, exchange(): arrived.append(lax.ppermute(face, axis, pairs))  36.4 us
    all_to_all x1, blocking collectives, steps(): lax.all_to_all(request, ALL, split_axis=0, concat_axis=0, tiled=True)  28.3 us
    all_to_all x1, blocking collectives, local(): sampled = lax.all_to_all(sums, ALL, split_axis=0, concat_axis=0, tiled=True)  24.6 us
    pallas_call x4, Pallas kernels, steps(): call(functools.partial(outer_kernel, signs, last), 'outer', [BLOCK] + ([i...  21.4 us
    pallas_call x4, Pallas kernels, steps(): call(functools.partial(inner_kernel, signs), 'inner', [BLOCK] * 2, [VMEM]...  20.1 us
    ppermute x24, waiting for transfers between devices, exchange(): arrived.append(lax.ppermute(face, axis, pairs))  7.15 us
    unnamed x25, local copies, waits for them, and re-layouts  5.31 us
    pallas_call x1, Pallas kernels, local(): call(sample_kernel, 'samples', [(owners, slots)], [SMEM, VMEM, VMEM, VMEM...  5.1 us
  transfers between devices with their start and end apart: 24, of which 4 were waited for; matrix products, arithmetic and copies ran while one was open for 1% of the time, Pallas kernels for 13%

profile of v3, /device:TPU:1, one launch (start us, length us, event | category | flops | bytes accessed | tf_op | source)
XLA Modules:
  0.0 153.7 jit_solution(5925305906846686149)
XLA Ops:
  1.7 28.3 %all_to_all.23 = f32[256,1,128]{2,1,0:T(1,128)S(1)} all-to-all(f32[256,1,128]{2,1,0:T(1,128)S(1)} %copy.24), channel_id=1, replica_groups=mesh['gx'=4,'gy'=8,'ha'=8] {'gx','gy','ha'}, dimensions={0} | all-to-all | bytes 262144 | tf_op jit(solution)/shard_map/all_to_all | solution.py:326
  34.2 3.0 %collective-permute-start.1 = (f32[384,128]{1,0:T(8,128)}, f32[384,128]{1,0:T(8,128)S(1)}, u32[]{:S(2)}, u32[]{:S(2)}) collective-permute-start(f32[384,128]{1,0:T(8,128)} %get-tuple-element.44), channel_id=1, source_target_pairs={{64,128},{128,64},{65,129},{129,65},{66,130},{130,66},{67,131},{13... | collective-permute-start | bytes 589832 | tf_op jit(solution)/shard_map/ppermute | solution.py:305
  39.2 5.0 %inner.4 = (f32[2048,128]{1,0:T(8,128)S(1)}, f32[2048,128]{1,0:T(8,128)S(1)}) custom-call(f32[2048,128]{1,0:T(8,128)S(1)} %get-tuple-element.40.v_ref, f32[8,128]{1,0:T(8,128)S(1)} %get-tuple-element.85.adx_ref, f32[8,128]{1,0:T(8,128)S(1)} %get-tuple-element.84.ady_ref), custom_call_target="tpu_custom_call" | custom-call | flops 30000000 | bytes 4194304 | tf_op jit(solution)/shard_map/inner/pallas_call | solution.py:333
  44.3 2.5 %collective-permute-done.2.rya = f32[384,128]{1,0:T(8,128)S(1)} collective-permute-done((f32[384,128]{1,0:T(8,128)}, f32[384,128]{1,0:T(8,128)S(1)}, u32[]{:S(2)}, u32[]{:S(2)}) %collective-permute-start.2) | collective-permute-done | bytes 196640 | tf_op jit(solution)/shard_map/ppermute | solution.py:305
  46.8 4.7 %outer.4 = (f32[2048,128]{1,0:T(8,128)S(1)}, f32[384,128]{1,0:T(8,128)S(1)}, f32[384,128]{1,0:T(8,128)S(1)}, f32[384,128]{1,0:T(8,128)S(1)}, f32[384,128]{1,0:T(...) custom-call(f32[2048,128]{1,0:T(8,128)S(1)} %get-tuple-element.40.v_ref, ...), custom_call_target="tpu_custom_call" | custom-call | flops 15000000 | bytes 4194304 | tf_op jit(solution)/shard_map/outer/pallas_call | solution.py:336
  52.7 2.1 %collective-permute-start.11 = (f32[512,128]{1,0:T(8,128)S(1)}, f32[512,128]{1,0:T(8,128)S(1)}, u32[]{:S(2)}, u32[]{:S(2)}) collective-permute-start(f32[512,128]{1,0:T(8,128)S(1)} %get-tuple-element.57), channel_id=1, source_target_pairs={{1,2},{2,1},{3,4},{4,3},{5,6},{6,5},{7,0},{0,7},{9,10},{10,9},{11,... | collective-permute-start | bytes 786440 | tf_op jit(solution)/shard_map/ppermute | solution.py:305
  54.7 2.9 %collective-permute-start.7 = (f32[384,128]{1,0:T(8,128)S(1)}, f32[384,128]{1,0:T(8,128)S(1)}, u32[]{:S(2)}, u32[]{:S(2)}) collective-permute-start(f32[384,128]{1,0:T(8,128)S(1)} %get-tuple-element.53), channel_id=1, source_target_pairs={{64,128},{128,64},{65,129},{129,65},{66,130},{130,66},{67,131},{13... | collective-permute-start | bytes 589832 | tf_op jit(solution)/shard_map/ppermute | solution.py:305
  57.7 2.2 %collective-permute-start.8 = (f32[384,128]{1,0:T(8,128)S(1)}, f32[384,128]{1,0:T(8,128)S(1)}, u32[]{:S(2)}, u32[]{:S(2)}) collective-permute-start(f32[384,128]{1,0:T(8,128)S(1)} %get-tuple-element.54), channel_id=1, source_target_pairs={{0,8},{8,0},{16,24},{24,16},{32,40},{40,32},{48,56},{56,48},{1,9},... | collective-permute-start | bytes 589832 | tf_op jit(solution)/shard_map/ppermute | solution.py:305
  60.5 5.0 %inner.5 = (f32[2048,128]{1,0:T(8,128)S(1)}, f32[2048,128]{1,0:T(8,128)S(1)}) custom-call(f32[2048,128]{1,0:T(8,128)S(1)} %get-tuple-element.49.v_ref, f32[8,128]{1,0:T(8,128)S(1)} %get-tuple-element.85.adx_ref, f32[8,128]{1,0:T(8,128)S(1)} %get-tuple-element.84.ady_ref), custom_call_target="tpu_custom_call" | custom-call | flops 30000000 | bytes 4194304 | tf_op jit(solution)/shard_map/inner/pallas_call | solution.py:333
  67.0 5.6 %outer.5 = (f32[2048,128]{1,0:T(8,128)S(1)}, f32[384,128]{1,0:T(8,128)}, f32[384,128]{1,0:T(8,128)S(1)}, f32[384,128]{1,0:T(8,128)S(1)}, f32[384,128]{1,0:T(8,12...) custom-call(f32[2048,128]{1,0:T(8,128)S(1)} %get-tuple-element.49.v_ref, f32[2048,128]{1,0:T(8,128)S(1)} %get-tuple-element.50.h_in, ...), custom_call_target="tpu_custom_call" | custom-call | flops 15000000 | bytes 4194304 | tf_op jit(solution)/shard_map/outer/pallas_call | solution.py:336
  74.7 2.2 %collective-permute-start.17 = (f32[512,128]{1,0:T(8,128)}, f32[512,128]{1,0:T(8,128)S(1)}, u32[]{:S(2)}, u32[]{:S(2)}) collective-permute-start(f32[512,128]{1,0:T(8,128)} %get-tuple-element.66), channel_id=1, source_target_pairs={{1,2},{2,1},{3,4},{4,3},{5,6},{6,5},{7,0},{0,7},{9,10},{10,9},{11,... | collective-permute-start | bytes 786440 | tf_op jit(solution)/shard_map/ppermute | solution.py:305
  77.2 5.3 %collective-permute-start.13 = (f32[384,128]{1,0:T(8,128)}, f32[384,128]{1,0:T(8,128)S(1)}, u32[]{:S(2)}, u32[]{:S(2)}) collective-permute-start(f32[384,128]{1,0:T(8,128)} %copy-done.7), channel_id=1, source_target_pairs={{64,128},{128,64},{65,129},{129,65},{66,130},{130,66},{67,131},{13... | collective-permute-start | bytes 589832 | tf_op jit(solution)/shard_map/ppermute | solution.py:305
  82.5 2.9 %collective-permute-start.14 = (f32[384,128]{1,0:T(8,128)S(1)}, f32[384,128]{1,0:T(8,128)S(1)}, u32[]{:S(2)}, u32[]{:S(2)}) collective-permute-start(f32[384,128]{1,0:T(8,128)S(1)} %copy-done.4), channel_id=1, source_target_pairs={{0,8},{8,0},{16,24},{24,16},{32,40},{40,32},{48,56},{56,48},{1,9},... | collective-permute-start | bytes 589832 | tf_op jit(solution)/shard_map/ppermute | solution.py:305
  86.3 5.0 %inner.6 = (f32[2048,128]{1,0:T(8,128)S(1)}, f32[2048,128]{1,0:T(8,128)S(1)}) custom-call(f32[2048,128]{1,0:T(8,128)S(1)} %get-tuple-element.58.v_ref, f32[8,128]{1,0:T(8,128)S(1)} %get-tuple-element.85.adx_ref, f32[8,128]{1,0:T(8,128)S(1)} %get-tuple-element.84.ady_ref), custom_call_target="tpu_custom_call" | custom-call | flops 30000000 | bytes 4194304 | tf_op jit(solution)/shard_map/inner/pallas_call | solution.py:333
  91.3 1.5 collective-permute-done.14.rya
  92.8 5.6 %outer.6 = (f32[2048,128]{1,0:T(8,128)S(1)}, f32[384,128]{1,0:T(8,128)}, f32[384,128]{1,0:T(8,128)S(1)}, f32[384,128]{1,0:T(8,128)S(1)}, f32[384,128]{1,0:T(8,12...) custom-call(f32[2048,128]{1,0:T(8,128)S(1)} %get-tuple-element.58.v_ref, f32[2048,128]{1,0:T(8,128)S(1)} %get-tuple-element.59.h_in, ...), custom_call_target="tpu_custom_call" | custom-call | flops 15000000 | bytes 4194304 | tf_op jit(solution)/shard_map/outer/pallas_call | solution.py:336
  100.5 1.7 %collective-permute-start.23 = (f32[512,128]{1,0:T(8,128)}, f32[512,128]{1,0:T(8,128)S(1)}, u32[]{:S(2)}, u32[]{:S(2)}) collective-permute-start(f32[512,128]{1,0:T(8,128)} %get-tuple-element.75), channel_id=1, source_target_pairs={{1,2},{2,1},{3,4},{4,3},{5,6},{6,5},{7,0},{0,7},{9,10},{10,9},{11,... | collective-permute-start | bytes 786440 | tf_op jit(solution)/shard_map/ppermute | solution.py:305
  102.4 6.0 %collective-permute-start.19 = (f32[384,128]{1,0:T(8,128)}, f32[384,128]{1,0:T(8,128)S(1)}, u32[]{:S(2)}, u32[]{:S(2)}) collective-permute-start(f32[384,128]{1,0:T(8,128)} %copy-done.10), channel_id=1, source_target_pairs={{64,128},{128,64},{65,129},{129,65},{66,130},{130,66},{67,131},{13... | collective-permute-start | bytes 589832 | tf_op jit(solution)/shard_map/ppermute | solution.py:305
  108.4 2.0 %collective-permute-start.20 = (f32[384,128]{1,0:T(8,128)S(1)}, f32[384,128]{1,0:T(8,128)S(1)}, u32[]{:S(2)}, u32[]{:S(2)}) collective-permute-start(f32[384,128]{1,0:T(8,128)S(1)} %copy-done.9), channel_id=1, source_target_pairs={{0,8},{8,0},{16,24},{24,16},{32,40},{40,32},{48,56},{56,48},{1,9},... | collective-permute-start | bytes 589832 | tf_op jit(solution)/shard_map/ppermute | solution.py:305
  111.1 5.0 %inner.7 = (f32[2048,128]{1,0:T(8,128)S(1)}, f32[2048,128]{1,0:T(8,128)S(1)}) custom-call(f32[2048,128]{1,0:T(8,128)S(1)} %get-tuple-element.67.v_ref, f32[8,128]{1,0:T(8,128)S(1)} %get-tuple-element.85.adx_ref, f32[8,128]{1,0:T(8,128)S(1)} %get-tuple-element.84.ady_ref), custom_call_target="tpu_custom_call" | custom-call | flops 30000000 | bytes 4194304 | tf_op jit(solution)/shard_map/inner/pallas_call | solution.py:333
  116.1 1.7 %collective-permute-done.20.rya = f32[384,128]{1,0:T(8,128)S(1)} collective-permute-done((f32[384,128]{1,0:T(8,128)S(1)}, f32[384,128]{1,0:T(8,128)S(1)}, u32[]{:S(2)}, u32[]{:S(2)}) %collective-permute-start.20) | collective-permute-done | bytes 196640 | tf_op jit(solution)/shard_map/ppermute | solution.py:305
  117.8 5.5 %outer.7 = (f32[2048,128]{1,0:T(8,128)S(1)}, f32[16,16,1024]{2,1,0:T(8,128)}) custom-call(f32[2048,128]{1,0:T(8,128)S(1)} %get-tuple-element.67.v_ref, f32[2048,128]{1,0:T(8,128)S(1)} %get-tuple-element.68.h_in, f32[2048,128]{1,0:T(8,128)S(1)} %get-tuple-element.69.turned_ref, f32[8,128]{1,0:T(8,128)S(1)} %get-tuple-element.85.adx_ref, ...), custom_call_target="tpu_custom_call" | custom-call | flops 15000000 | bytes 4194304 | tf_op jit(solution)/shard_map/outer/pallas_call | solution.py:336
  123.3 5.1 %samples.1 = f32[256,4]{1,0:T(8,128)S(1)} custom-call(s32[1024]{0:T(1024)S(1)} %add_select_fusion.1.rows_ref, f32[2048,128]{1,0:T(8,128)S(1)} %get-tuple-element.77.v_ref, s32[1024,128]{1,0:T(8,128)S(1)} %broadcast_add_fusion.at_ref, f32[256,128]{1,0:T(8,128)S(1)} %bitcast.29), custom_call_target="tpu_custom_call" | custom-call | bytes 4194304 | tf_op jit(solution)/shard_map/samples/pallas_call | solution.py:407
  128.4 24.6 %all_to_all.24 = f32[256,1,4]{2,1,0:T(1,128)S(1)} all-to-all(f32[256,1,4]{2,1,0:T(1,128)S(1)} %bitcast.30), channel_id=1, replica_groups=mesh['gx'=4,'gy'=8,'ha'=8] {'gx','gy','ha'}, dimensions={0} | all-to-all | bytes 8192 | tf_op jit(solution)/shard_map/all_to_all | solution.py:414
  (76 shorter events, 17.3 us)
Async XLA Ops:
  32.6 5.3 %collective-permute-start = (f32[384,128]{1,0:T(8,128)S(1)}, f32[384,128]{1,0:T(8,128)S(1)}, u32[]{:S(2)}, u32[]{:S(2)}) collective-permute-start(f32[384,128]{1,0:T(8,128)S(1)} %get-tuple-element.43), channel_id=1, source_target_pairs={{0,64},{64,0},{128,192},{192,128},{1,65},{65,1},{129,193},{193,129... | collective-permute-start | bytes 589832 | tf_op jit(solution)/shard_map/ppermute | solution.py:305
  33.4 13.4 %collective-permute-start.4 = (f32[512,128]{1,0:T(8,128)}, f32[512,128]{1,0:T(8,128)S(1)}, u32[]{:S(2)}, u32[]{:S(2)}) collective-permute-start(f32[512,128]{1,0:T(8,128)} %get-tuple-element.47), channel_id=1, source_target_pairs={{0,1},{1,0},{2,3},{3,2},{4,5},{5,4},{6,7},{7,6},{8,9},{9,8},{10,11... | collective-permute-start | bytes 786440 | tf_op jit(solution)/shard_map/ppermute | solution.py:305
  34.2 12.6 %collective-permute-start.5 = (f32[512,128]{1,0:T(8,128)}, f32[512,128]{1,0:T(8,128)S(1)}, u32[]{:S(2)}, u32[]{:S(2)}) collective-permute-start(f32[512,128]{1,0:T(8,128)} %get-tuple-element.48), channel_id=1, source_target_pairs={{1,2},{2,1},{3,4},{4,3},{5,6},{6,5},{7,0},{0,7},{9,10},{10,9},{11,... | collective-permute-start | bytes 786440 | tf_op jit(solution)/shard_map/ppermute | solution.py:305
  34.2 10.0 %collective-permute-start.1 = (f32[384,128]{1,0:T(8,128)}, f32[384,128]{1,0:T(8,128)S(1)}, u32[]{:S(2)}, u32[]{:S(2)}) collective-permute-start(f32[384,128]{1,0:T(8,128)} %get-tuple-element.44), channel_id=1, source_target_pairs={{64,128},{128,64},{65,129},{129,65},{66,130},{130,66},{67,131},{13... | collective-permute-start | bytes 589832 | tf_op jit(solution)/shard_map/ppermute | solution.py:305
  37.2 9.6 %collective-permute-start.2 = (f32[384,128]{1,0:T(8,128)}, f32[384,128]{1,0:T(8,128)S(1)}, u32[]{:S(2)}, u32[]{:S(2)}) collective-permute-start(f32[384,128]{1,0:T(8,128)} %get-tuple-element.45), channel_id=1, source_target_pairs={{0,8},{8,0},{16,24},{24,16},{32,40},{40,32},{48,56},{56,48},{1,9},... | collective-permute-start | bytes 589832 | tf_op jit(solution)/shard_map/ppermute | solution.py:305
  37.9 8.9 %collective-permute-start.3 = (f32[384,128]{1,0:T(8,128)}, f32[384,128]{1,0:T(8,128)S(1)}, u32[]{:S(2)}, u32[]{:S(2)}) collective-permute-start(f32[384,128]{1,0:T(8,128)} %get-tuple-element.46), channel_id=1, source_target_pairs={{8,16},{16,8},{24,32},{32,24},{40,48},{48,40},{9,17},{17,9},{25,33... | collective-permute-start | bytes 589832 | tf_op jit(solution)/shard_map/ppermute | solution.py:305
  51.5 8.3 %collective-permute-start.6 = (f32[384,128]{1,0:T(8,128)S(1)}, f32[384,128]{1,0:T(8,128)S(1)}, u32[]{:S(2)}, u32[]{:S(2)}) collective-permute-start(f32[384,128]{1,0:T(8,128)S(1)} %get-tuple-element.52), channel_id=1, source_target_pairs={{0,64},{64,0},{128,192},{192,128},{1,65},{65,1},{129,193},{193,129... | collective-permute-start | bytes 589832 | tf_op jit(solution)/shard_map/ppermute | solution.py:305
  51.6 15.4 %collective-permute-start.10 = (f32[512,128]{1,0:T(8,128)S(1)}, f32[512,128]{1,0:T(8,128)S(1)}, u32[]{:S(2)}, u32[]{:S(2)}) collective-permute-start(f32[512,128]{1,0:T(8,128)S(1)} %get-tuple-element.56), channel_id=1, source_target_pairs={{0,1},{1,0},{2,3},{3,2},{4,5},{5,4},{6,7},{7,6},{8,9},{9,8},{10,11... | collective-permute-start | bytes 786440 | tf_op jit(solution)/shard_map/ppermute | solution.py:305
  52.7 14.3 %collective-permute-start.11 = (f32[512,128]{1,0:T(8,128)S(1)}, f32[512,128]{1,0:T(8,128)S(1)}, u32[]{:S(2)}, u32[]{:S(2)}) collective-permute-start(f32[512,128]{1,0:T(8,128)S(1)} %get-tuple-element.57), channel_id=1, source_target_pairs={{1,2},{2,1},{3,4},{4,3},{5,6},{6,5},{7,0},{0,7},{9,10},{10,9},{11,... | collective-permute-start | bytes 786440 | tf_op jit(solution)/shard_map/ppermute | solution.py:305
  54.7 10.8 %collective-permute-start.7 = (f32[384,128]{1,0:T(8,128)S(1)}, f32[384,128]{1,0:T(8,128)S(1)}, u32[]{:S(2)}, u32[]{:S(2)}) collective-permute-start(f32[384,128]{1,0:T(8,128)S(1)} %get-tuple-element.53), channel_id=1, source_target_pairs={{64,128},{128,64},{65,129},{129,65},{66,130},{130,66},{67,131},{13... | collective-permute-start | bytes 589832 | tf_op jit(solution)/shard_map/ppermute | solution.py:305
  57.7 9.3 %collective-permute-start.8 = (f32[384,128]{1,0:T(8,128)S(1)}, f32[384,128]{1,0:T(8,128)S(1)}, u32[]{:S(2)}, u32[]{:S(2)}) collective-permute-start(f32[384,128]{1,0:T(8,128)S(1)} %get-tuple-element.54), channel_id=1, source_target_pairs={{0,8},{8,0},{16,24},{24,16},{32,40},{40,32},{48,56},{56,48},{1,9},... | collective-permute-start | bytes 589832 | tf_op jit(solution)/shard_map/ppermute | solution.py:305
  59.9 7.1 %collective-permute-start.9 = (f32[384,128]{1,0:T(8,128)S(1)}, f32[384,128]{1,0:T(8,128)S(1)}, u32[]{:S(2)}, u32[]{:S(2)}) collective-permute-start(f32[384,128]{1,0:T(8,128)S(1)} %get-tuple-element.55), channel_id=1, source_target_pairs={{8,16},{16,8},{24,32},{32,24},{40,48},{48,40},{9,17},{17,9},{25,33... | collective-permute-start | bytes 589832 | tf_op jit(solution)/shard_map/ppermute | solution.py:305
  74.7 18.2 %collective-permute-start.16 = (f32[512,128]{1,0:T(8,128)}, f32[512,128]{1,0:T(8,128)S(1)}, u32[]{:S(2)}, u32[]{:S(2)}) collective-permute-start(f32[512,128]{1,0:T(8,128)} %get-tuple-element.65), channel_id=1, source_target_pairs={{0,1},{1,0},{2,3},{3,2},{4,5},{5,4},{6,7},{7,6},{8,9},{9,8},{10,11... | collective-permute-start | bytes 786440 | tf_op jit(solution)/shard_map/ppermute | solution.py:305
  74.7 18.1 %collective-permute-start.17 = (f32[512,128]{1,0:T(8,128)}, f32[512,128]{1,0:T(8,128)S(1)}, u32[]{:S(2)}, u32[]{:S(2)}) collective-permute-start(f32[512,128]{1,0:T(8,128)} %get-tuple-element.66), channel_id=1, source_target_pairs={{1,2},{2,1},{3,4},{4,3},{5,6},{6,5},{7,0},{0,7},{9,10},{10,9},{11,... | collective-permute-start | bytes 786440 | tf_op jit(solution)/shard_map/ppermute | solution.py:305
  76.9 8.5 %collective-permute-start.12 = (f32[384,128]{1,0:T(8,128)}, f32[384,128]{1,0:T(8,128)S(1)}, u32[]{:S(2)}, u32[]{:S(2)}) collective-permute-start(f32[384,128]{1,0:T(8,128)} %get-tuple-element.61), channel_id=1, source_target_pairs={{0,64},{64,0},{128,192},{192,128},{1,65},{65,1},{129,193},{193,129... | collective-permute-start | bytes 589832 | tf_op jit(solution)/shard_map/ppermute | solution.py:305
  77.2 14.2 %collective-permute-start.13 = (f32[384,128]{1,0:T(8,128)}, f32[384,128]{1,0:T(8,128)S(1)}, u32[]{:S(2)}, u32[]{:S(2)}) collective-permute-start(f32[384,128]{1,0:T(8,128)} %copy-done.7), channel_id=1, source_target_pairs={{64,128},{128,64},{65,129},{129,65},{66,130},{130,66},{67,131},{13... | collective-permute-start | bytes 589832 | tf_op jit(solution)/shard_map/ppermute | solution.py:305
  82.5 10.3 %collective-permute-start.14 = (f32[384,128]{1,0:T(8,128)S(1)}, f32[384,128]{1,0:T(8,128)S(1)}, u32[]{:S(2)}, u32[]{:S(2)}) collective-permute-start(f32[384,128]{1,0:T(8,128)S(1)} %copy-done.4), channel_id=1, source_target_pairs={{0,8},{8,0},{16,24},{24,16},{32,40},{40,32},{48,56},{56,48},{1,9},... | collective-permute-start | bytes 589832 | tf_op jit(solution)/shard_map/ppermute | solution.py:305
  85.4 7.4 %collective-permute-start.15 = (f32[384,128]{1,0:T(8,128)S(1)}, f32[384,128]{1,0:T(8,128)S(1)}, u32[]{:S(2)}, u32[]{:S(2)}) collective-permute-start(f32[384,128]{1,0:T(8,128)S(1)} %copy-done.2), channel_id=1, source_target_pairs={{8,16},{16,8},{24,32},{32,24},{40,48},{48,40},{9,17},{17,9},{25,33... | collective-permute-start | bytes 589832 | tf_op jit(solution)/shard_map/ppermute | solution.py:305
  100.5 17.3 %collective-permute-start.22 = (f32[512,128]{1,0:T(8,128)}, f32[512,128]{1,0:T(8,128)S(1)}, u32[]{:S(2)}, u32[]{:S(2)}) collective-permute-start(f32[512,128]{1,0:T(8,128)} %get-tuple-element.74), channel_id=1, source_target_pairs={{0,1},{1,0},{2,3},{3,2},{4,5},{5,4},{6,7},{7,6},{8,9},{9,8},{10,11... | collective-permute-start | bytes 786440 | tf_op jit(solution)/shard_map/ppermute | solution.py:305
  100.5 17.3 %collective-permute-start.23 = (f32[512,128]{1,0:T(8,128)}, f32[512,128]{1,0:T(8,128)S(1)}, u32[]{:S(2)}, u32[]{:S(2)}) collective-permute-start(f32[512,128]{1,0:T(8,128)} %get-tuple-element.75), channel_id=1, source_target_pairs={{1,2},{2,1},{3,4},{4,3},{5,6},{6,5},{7,0},{0,7},{9,10},{10,9},{11,... | collective-permute-start | bytes 786440 | tf_op jit(solution)/shard_map/ppermute | solution.py:305
  102.2 8.2 %collective-permute-start.18 = (f32[384,128]{1,0:T(8,128)}, f32[384,128]{1,0:T(8,128)S(1)}, u32[]{:S(2)}, u32[]{:S(2)}) collective-permute-start(f32[384,128]{1,0:T(8,128)} %get-tuple-element.70), channel_id=1, source_target_pairs={{0,64},{64,0},{128,192},{192,128},{1,65},{65,1},{129,193},{193,129... | collective-permute-start | bytes 589832 | tf_op jit(solution)/shard_map/ppermute | solution.py:305
  102.4 13.7 %collective-permute-start.19 = (f32[384,128]{1,0:T(8,128)}, f32[384,128]{1,0:T(8,128)S(1)}, u32[]{:S(2)}, u32[]{:S(2)}) collective-permute-start(f32[384,128]{1,0:T(8,128)} %copy-done.10), channel_id=1, source_target_pairs={{64,128},{128,64},{65,129},{129,65},{66,130},{130,66},{67,131},{13... | collective-permute-start | bytes 589832 | tf_op jit(solution)/shard_map/ppermute | solution.py:305
  108.4 9.4 %collective-permute-start.20 = (f32[384,128]{1,0:T(8,128)S(1)}, f32[384,128]{1,0:T(8,128)S(1)}, u32[]{:S(2)}, u32[]{:S(2)}) collective-permute-start(f32[384,128]{1,0:T(8,128)S(1)} %copy-done.9), channel_id=1, source_target_pairs={{0,8},{8,0},{16,24},{24,16},{32,40},{40,32},{48,56},{56,48},{1,9},... | collective-permute-start | bytes 589832 | tf_op jit(solution)/shard_map/ppermute | solution.py:305
  110.4 7.4 %collective-permute-start.21 = (f32[384,128]{1,0:T(8,128)S(1)}, f32[384,128]{1,0:T(8,128)S(1)}, u32[]{:S(2)}, u32[]{:S(2)}) collective-permute-start(f32[384,128]{1,0:T(8,128)S(1)} %copy-done.6), channel_id=1, source_target_pairs={{8,16},{16,8},{24,32},{32,24},{40,48},{48,40},{9,17},{17,9},{25,33... | collective-permute-start | bytes 589832 | tf_op jit(solution)/shard_map/ppermute | solution.py:305
  (12 other events, 34.6 us)

commit v4 on v3

--- a/solution.py
+++ b/solution.py
@@ -19,13 +19,13 @@
 YROW = PAIRS
 F32 = jnp.float32
 VMEM = pl.BlockSpec(memory_space=pltpu.VMEM)
+ANY = pl.BlockSpec(memory_space=pl.ANY)
 SMEM = pl.BlockSpec(memory_space=pltpu.SMEM)
 ALL = ("gx", "gy", "ha")
 
-def smooth(low, high, turn):
+def smooth(low, high, low2, high2, turn):
     mid = (turn * (4.0 / 3.0)) * turn + low * high + EPS
-    twice = turn + turn
-    return mid + high * twice, mid, mid - low * twice
+    return mid + high2 * turn, mid, mid - low2 * turn
 
 
 def inverse(d):
@@ -39,7 +39,8 @@
     curve = [diff[n + 1] - diff[n] for n in range(count + 3)]
     turn = [curve[n + 1] - curve[n] for n in range(count + 2)]
     bend = [turn[n] - turn[n + 1] for n in range(count + 1)]
-    terms = [smooth(curve[n], curve[n + 1], turn[n]) for n in range(count + 2)]
+    curve2 = [c + c for c in curve]
+    terms = [smooth(curve[n], curve[n + 1], curve2[n], curve2[n + 1], turn[n]) for n in range(count + 2)]
     slopes = []
     for n in range(count):
         a, b, c = terms[n][0], terms[n + 1][1], terms[n + 2][2]
@@ -48,7 +49,7 @@
         gamma3 = 3.0 * gamma
         down = alpha + 6.0 * beta + gamma3
         up = alpha * (bend[n] + bend[n]) + gamma3 * bend[n + 1]
-        inner = curve[n + 1] + (curve[n + 2] + curve[n + 2]) + up * inverse(down)
+        inner = curve[n + 1] + curve2[n + 2] + up * inverse(down)
         slopes.append(diff[n + 2] + inner * (1.0 / 6.0))
     return slopes
 
@@ -62,16 +63,19 @@
     curve_o = [diff_e[n + 1] - diff_o[n] for n in range(count - 2)]
     turn_e = [curve_o[n] - curve_e[n] for n in range(count - 2)]
     turn_o = [curve_e[n + 1] - curve_o[n] for n in range(count - 2)]
-    even = [smooth(curve_e[n], curve_o[n], turn_e[n]) for n in range(count - 2)]
-    odd = [smooth(curve_o[n], curve_e[n + 1], turn_o[n]) for n in range(count - 2)]
-
-    def inner_sum(a, b, c, before, here, bend_a, bend_c):
+    two_e, two_o = [c + c for c in curve_e], [c + c for c in curve_o]
+    even = [smooth(curve_e[n], curve_o[n], two_e[n], two_o[n], turn_e[n]) for n in range(count - 2)]
+    odd = [
+        smooth(curve_o[n], curve_e[n + 1], two_o[n], two_e[n + 1], turn_o[n]) for n in range(count - 2)
+    ]
+
+    def inner_sum(a, b, c, before, here2, bend_a, bend_c):
         bc, ac, ab = b * c, a * c, a * b
         alpha, beta, gamma = bc * bc, ac * ac, ab * ab
         gamma3 = 3.0 * gamma
         down = alpha + 6.0 * beta + gamma3
         up = alpha * (bend_a + bend_a) + gamma3 * bend_c
-        return before + (here + here) + up * inverse(down)
+        return before + here2 + up * inverse(down)
 
     result = []
     for n in range(2, count - 2):
@@ -81,10 +85,10 @@
             turn_o[n - 1] - turn_e[n],
         )
         minus = inner_sum(
-            odd[n - 2][0], even[n - 1][1], odd[n - 1][2], curve_e[n - 1], curve_o[n - 1], bend_m, bend_0
+            odd[n - 2][0], even[n - 1][1], odd[n - 1][2], curve_e[n - 1], two_o[n - 1], bend_m, bend_0
         )
         plus = inner_sum(
-            even[n][2], odd[n - 1][1], even[n - 1][0], curve_e[n], curve_o[n - 1], bend_p, bend_0
+            even[n][2], odd[n - 1][1], even[n - 1][0], curve_e[n], two_o[n - 1], bend_p, bend_0
         )
         sixth = 1.0 / 6.0
         result.append(jnp.minimum(diff_o[n - 1] + minus * sixth, plus * sixth - diff_e[n]))
@@ -155,7 +159,7 @@
     return x, pl.ds(8 * t, 8), pl.ds(128 * p, 128)
 
 
-def first_kernel(signs, in_ref, _, v_ref, *faces):
+def first_kernel(signs, in_ref, rows_ref, reads_ref, v_ref, *faces):
     def body(x, _):
         for t in range(2):
             for p in range(8):
@@ -169,7 +173,7 @@
 def inner_kernel(signs, v_ref, adx_ref, ady_ref, h_ref, turned_ref):
     (x_start, x_dir, *_), (y_start, y_dir, *_), _ = scalars(signs)
     first_half = lanes_first_half()
-    adx, ady = adx_ref[...], ady_ref[...]
+    adx, ady = adx_ref[lax.axis_index("ha")], ady_ref[lax.axis_index("ha")]
     zero = jnp.zeros((8, 128), F32)
     turned_ref[...] = pltpu.roll(v_ref[...], NV, 1)
     xs = [(x_start + x_dir * i) * XROW for i in range(16)]
@@ -210,7 +214,7 @@
     where = scalars(signs)
     (x_start, x_dir, _, _, xh_a, xh_b), (y_start, y_dir, _, _, yh_a, yh_b), (_, _, hh_a, hh_b) = where
     first_half = lanes_first_half()
-    adx, ady = adx_ref[...], ady_ref[...]
+    adx, ady = adx_ref[lax.axis_index("ha")], ady_ref[lax.axis_index("ha")]
     for l in range(2):
         hs[pl.ds(pl.multiple_of((hh_a + l) * 256, 256), 256), :] = rha[pl.ds(l * 256, 256), :]
         hs[pl.ds(pl.multiple_of((hh_b + l) * 256, 256), 256), :] = rhb[pl.ds(l * 256, 256), :]
@@ -286,7 +290,7 @@
         out_specs=[VMEM] * len(outs),
         scratch_shapes=[pltpu.VMEM(s, F32) for s in scratch],
         cost_estimate=pl.CostEstimate(flops=flops, bytes_accessed=moved, transcendentals=0),
-        compiler_params=pltpu.CompilerParams(vmem_limit_bytes=16 << 20),
+        compiler_params=pltpu.CompilerParams(vmem_limit_bytes=8 << 20),
     )
 
 
@@ -319,14 +323,12 @@
     return tables, signs
 
 
-def steps(initial_value, request):
+def steps(initial_value, rows, reads):
     tables, signs = drift_tables(lax.axis_size("ha"))
-    ha = lax.axis_index("ha")
-    adx, ady = (jnp.asarray(t)[ha] for t in tables)
-    request = lax.all_to_all(request, ALL, split_axis=0, concat_axis=0, tiled=True)
+    adx, ady = (jnp.asarray(t) for t in tables)
     value, *faces = call(
-        functools.partial(first_kernel, signs), "first", [BLOCK] + FACES, [VMEM, pl.BlockSpec(memory_space=pl.ANY)]
-    )(initial_value, request)
+        functools.partial(first_kernel, signs), "first", [BLOCK] + FACES, [VMEM, ANY, ANY]
+    )(initial_value, rows, reads)
     for step in range(STEPS):
         last = step == STEPS - 1
         arrived = exchange(faces)
@@ -341,7 +343,7 @@
             scratch=[(6 * XROW, 128), (6 * XROW, 128), (1024, 128), (1024, 128), BLOCK],
             flops=15_000_000,
         )(value, part, turned, adx, ady, *arrived)
-    return value, faces[0], request
+    return value, faces[0]
 
 
 def sample_kernel(rows_ref, v_ref, at_ref, w_ref, out_ref, table, picked):
@@ -400,17 +402,20 @@
         [weights.reshape(16 * slots, owners), corner.reshape(slots, owners).astype(F32)], axis=0
     )
     request = jnp.pad(request.T, ((0, 0), (0, 128 - 17 * slots)))
-    value, final, request = steps(initial_value, request)
+    request = lax.all_to_all(request, ALL, split_axis=0, concat_axis=0, tiled=True)
     codes = jnp.maximum(request[:, 64 : 64 + slots], 0.0).astype(jnp.int32)
     lane = jnp.arange(128, dtype=jnp.int32)
     reads = (codes.T % NV)[:, :, None] + (((lane >> 2) & 1) + NV * ((lane >> 3) & 1))[None, None, :]
+    rows = codes.reshape(-1) // NV
+    reads = reads.reshape(slots * owners, 128)
+    value, final = steps(initial_value, rows, reads)
     (sums,) = call(
         sample_kernel,
         "samples",
         [(owners, slots)],
         [SMEM, VMEM, VMEM, VMEM],
         scratch=[(2 * ROWS, 128), (16 * owners, 128)],
-    )(codes.reshape(-1) // NV, value, reads.reshape(slots * owners, 128), request)
+    )(rows, value, reads, request)
     sampled = lax.all_to_all(sums, ALL, split_axis=0, concat_axis=0, tiled=True)
     sampled = jnp.where(corner >= 0, sampled.T.reshape(corner.shape), 0.0)
     return final, sampled

time: 154 us -> 148 us (0.961)
  blocking collectives: 52.9 us -> 23.3 us
  waiting for transfers between devices: 7.15 us -> 22.8 us
  starting transfers between devices: 36.4 us -> 51.5 us
  local copies, waits for them, and re-layouts: 7.25 us -> 2.54 us
  Pallas kernels: 48 us -> 44.9 us
    all_to_all x1 -> x0, blocking collectives: 28.3 us -> none  [steps(): lax.all_to_all(request, ALL, split_axis=0, concat_axis=0, tiled=True)]
    all_to_all x0 -> x1, starting transfers between devices: none -> 15.7 us  [local(): lax.all_to_all(request, ALL, split_axis=0, concat_axis=0, tiled=True)]
    all_to_all x0 -> x1, waiting for transfers between devices: none -> 12.7 us  [local(): lax.all_to_all(request, ALL, split_axis=0, concat_axis=0, tiled=True)]
    unnamed x25 -> x9, local copies, waits for them, and re-layouts: 5.31 us -> 0.64 us
    ppermute x24, waiting for transfers between devices: 7.15 us -> 10 us  [exchange(): arrived.append(lax.ppermute(face, axis, pairs))]
    pallas_call x4, Pallas kernels: 21.4 us -> 19.4 us  [steps(): call(functools.partial(outer_kernel, signs, last), 'outer', [BLOCK] + ([i...]
  transfers between devices with their start and end apart: 24 -> 25, of which waited for: 4 -> 5; matrix products, arithmetic and copies ran while one was open for 1% -> 0% of each run, Pallas kernels for 13% -> 14%
where the time goes in v4:
time: 148 us
  starting transfers between devices  51.5 us (35%)
  Pallas kernels  44.9 us (30%)
  blocking collectives  23.3 us (16%)
  waiting for transfers between devices  22.8 us (15%)
  local copies, waits for them, and re-layouts  2.54 us (2%)
  other arithmetic  1.74 us (1%)
    ppermute x24, starting transfers between devices, exchange(): arrived.append(lax.ppermute(face, axis, pairs))  35.8 us
    all_to_all x1, blocking collectives, local(): sampled = lax.all_to_all(sums, ALL, split_axis=0, concat_axis=0, tiled=True)  23.3 us
    pallas_call x4, Pallas kernels, steps(): call(functools.partial(inner_kernel, signs), 'inner', [BLOCK] * 2, [VMEM]...  20 us
    pallas_call x4, Pallas kernels, steps(): call(functools.partial(outer_kernel, signs, last), 'outer', [BLOCK] + ([i...  19.4 us
    all_to_all x1, starting transfers between devices, local(): lax.all_to_all(request, ALL, split_axis=0, concat_axis=0, tiled=True)  15.7 us
    all_to_all x1, waiting for transfers between devices, local(): lax.all_to_all(request, ALL, split_axis=0, concat_axis=0, tiled=True)  12.7 us
    ppermute x24, waiting for transfers between devices, exchange(): arrived.append(lax.ppermute(face, axis, pairs))  10 us
    pallas_call x1, Pallas kernels, local(): call(sample_kernel, 'samples', [(owners, slots)], [SMEM, VMEM, VMEM, VMEM...  5.1 us
  transfers between devices with their start and end apart: 25, of which 5 were waited for; matrix products, arithmetic and copies ran while one was open for 0% of the time, Pallas kernels for 14%

profile of v4, /device:TPU:1, one launch (start us, length us, event | category | flops | bytes accessed | tf_op | source)
XLA Modules:
  0.0 147.7 jit_solution(3338904746313203303)
XLA Ops:
  3.0 15.7 %all-to-all-start = ((f32[256,1,128]{2,1,0:T(1,128)}), f32[256,1,128]{2,1,0:T(1,128)S(1)}, u32[]{:S(2)}, u32[]{:S(2)}) async-start(f32[256,1,128]{2,1,0:T(1,128)} %copy.24), calls=%async_computation | async-start | bytes 262144 | tf_op jit(solution)/shard_map/all_to_all | solution.py:405
  18.7 12.7 %all-to-all-done = f32[256,1,128]{2,1,0:T(1,128)S(1)} async-done(((f32[256,1,128]{2,1,0:T(1,128)}), f32[256,1,128]{2,1,0:T(1,128)S(1)}, u32[]{:S(2)}, u32[]{:S(2)}) %all-to-all-start) | async-done | bytes 131104 | tf_op jit(solution)/shard_map/all_to_all | solution.py:405
  34.3 3.0 %collective-permute-start.1 = (f32[384,128]{1,0:T(8,128)S(1)}, f32[384,128]{1,0:T(8,128)S(1)}, u32[]{:S(2)}, u32[]{:S(2)}) collective-permute-start(f32[384,128]{1,0:T(8,128)S(1)} %get-tuple-element.44), channel_id=1, source_target_pairs={{64,128},{128,64},{65,129},{129,65},{66,130},{130,66},{67,131},{13... | collective-permute-start | bytes 589832 | tf_op jit(solution)/shard_map/ppermute | solution.py:309
  38.7 5.0 %inner.4 = (f32[2048,128]{1,0:T(8,128)S(1)}, f32[2048,128]{1,0:T(8,128)S(1)}) custom-call(f32[2048,128]{1,0:T(8,128)S(1)} %get-tuple-element.40.v_ref, f32[8,8,128]{2,1,0:T(8,128)S(1)} %copy-done.1, f32[8,8,128]{2,1,0:T(8,128)S(1)} %copy-done), custom_call_target="tpu_custom_call" | custom-call | flops 30000000 | bytes 4194304 | tf_op jit(solution)/shard_map/inner/pallas_call | solution.py:335
  43.7 3.0 %collective-permute-done.2.rya = f32[384,128]{1,0:T(8,128)S(1)} collective-permute-done((f32[384,128]{1,0:T(8,128)S(1)}, f32[384,128]{1,0:T(8,128)S(1)}, u32[]{:S(2)}, u32[]{:S(2)}) %collective-permute-start.2) | collective-permute-done | bytes 196640 | tf_op jit(solution)/shard_map/ppermute | solution.py:309
  46.7 4.7 %outer.4 = (f32[2048,128]{1,0:T(8,128)S(1)}, f32[384,128]{1,0:T(8,128)S(1)}, f32[384,128]{1,0:T(8,128)S(1)}, f32[384,128]{1,0:T(8,128)S(1)}, f32[384,128]{1,0:T(...) custom-call(f32[2048,128]{1,0:T(8,128)S(1)} %get-tuple-element.40.v_ref, ...), custom_call_target="tpu_custom_call" | custom-call | flops 15000000 | bytes 4194304 | tf_op jit(solution)/shard_map/outer/pallas_call | solution.py:338
  52.6 2.1 %collective-permute-start.11 = (f32[512,128]{1,0:T(8,128)S(1)}, f32[512,128]{1,0:T(8,128)S(1)}, u32[]{:S(2)}, u32[]{:S(2)}) collective-permute-start(f32[512,128]{1,0:T(8,128)S(1)} %get-tuple-element.57), channel_id=1, source_target_pairs={{1,2},{2,1},{3,4},{4,3},{5,6},{6,5},{7,0},{0,7},{9,10},{10,9},{11,... | collective-permute-start | bytes 786440 | tf_op jit(solution)/shard_map/ppermute | solution.py:309
  54.6 2.8 %collective-permute-start.7 = (f32[384,128]{1,0:T(8,128)S(1)}, f32[384,128]{1,0:T(8,128)S(1)}, u32[]{:S(2)}, u32[]{:S(2)}) collective-permute-start(f32[384,128]{1,0:T(8,128)S(1)} %get-tuple-element.53), channel_id=1, source_target_pairs={{64,128},{128,64},{65,129},{129,65},{66,130},{130,66},{67,131},{13... | collective-permute-start | bytes 589832 | tf_op jit(solution)/shard_map/ppermute | solution.py:309
  57.4 2.2 %collective-permute-start.8 = (f32[384,128]{1,0:T(8,128)S(1)}, f32[384,128]{1,0:T(8,128)S(1)}, u32[]{:S(2)}, u32[]{:S(2)}) collective-permute-start(f32[384,128]{1,0:T(8,128)S(1)} %get-tuple-element.54), channel_id=1, source_target_pairs={{0,8},{8,0},{16,24},{24,16},{32,40},{40,32},{48,56},{56,48},{1,9},... | collective-permute-start | bytes 589832 | tf_op jit(solution)/shard_map/ppermute | solution.py:309
  60.3 5.0 %inner.5 = (f32[2048,128]{1,0:T(8,128)S(1)}, f32[2048,128]{1,0:T(8,128)S(1)}) custom-call(f32[2048,128]{1,0:T(8,128)S(1)} %get-tuple-element.49.v_ref, f32[8,8,128]{2,1,0:T(8,128)S(1)} %copy-done.1, f32[8,8,128]{2,1,0:T(8,128)S(1)} %copy-done), custom_call_target="tpu_custom_call" | custom-call | flops 30000000 | bytes 4194304 | tf_op jit(solution)/shard_map/inner/pallas_call | solution.py:335
  66.9 4.7 %outer.5 = (f32[2048,128]{1,0:T(8,128)S(1)}, f32[384,128]{1,0:T(8,128)S(1)}, f32[384,128]{1,0:T(8,128)S(1)}, f32[384,128]{1,0:T(8,128)S(1)}, f32[384,128]{1,0:T(...) custom-call(f32[2048,128]{1,0:T(8,128)S(1)} %get-tuple-element.49.v_ref, ...), custom_call_target="tpu_custom_call" | custom-call | flops 15000000 | bytes 4194304 | tf_op jit(solution)/shard_map/outer/pallas_call | solution.py:338
  71.8 2.1 %collective-permute-start.17 = (f32[512,128]{1,0:T(8,128)S(1)}, f32[512,128]{1,0:T(8,128)S(1)}, u32[]{:S(2)}, u32[]{:S(2)}) collective-permute-start(f32[512,128]{1,0:T(8,128)S(1)} %get-tuple-element.66), channel_id=1, source_target_pairs={{1,2},{2,1},{3,4},{4,3},{5,6},{6,5},{7,0},{0,7},{9,10},{10,9},{11,... | collective-permute-start | bytes 786440 | tf_op jit(solution)/shard_map/ppermute | solution.py:309
  73.9 5.4 %collective-permute-start.13 = (f32[384,128]{1,0:T(8,128)S(1)}, f32[384,128]{1,0:T(8,128)S(1)}, u32[]{:S(2)}, u32[]{:S(2)}) collective-permute-start(f32[384,128]{1,0:T(8,128)S(1)} %get-tuple-element.62), channel_id=1, source_target_pairs={{64,128},{128,64},{65,129},{129,65},{66,130},{130,66},{67,131},{13... | collective-permute-start | bytes 589832 | tf_op jit(solution)/shard_map/ppermute | solution.py:309
  79.3 2.9 %collective-permute-start.14 = (f32[384,128]{1,0:T(8,128)S(1)}, f32[384,128]{1,0:T(8,128)S(1)}, u32[]{:S(2)}, u32[]{:S(2)}) collective-permute-start(f32[384,128]{1,0:T(8,128)S(1)} %get-tuple-element.63), channel_id=1, source_target_pairs={{0,8},{8,0},{16,24},{24,16},{32,40},{40,32},{48,56},{56,48},{1,9},... | collective-permute-start | bytes 589832 | tf_op jit(solution)/shard_map/ppermute | solution.py:309
  82.9 5.0 %inner.6 = (f32[2048,128]{1,0:T(8,128)S(1)}, f32[2048,128]{1,0:T(8,128)S(1)}) custom-call(f32[2048,128]{1,0:T(8,128)S(1)} %get-tuple-element.58.v_ref, f32[8,8,128]{2,1,0:T(8,128)S(1)} %copy-done.1, f32[8,8,128]{2,1,0:T(8,128)S(1)} %copy-done), custom_call_target="tpu_custom_call" | custom-call | flops 30000000 | bytes 4194304 | tf_op jit(solution)/shard_map/inner/pallas_call | solution.py:335
  87.9 2.3 %collective-permute-done.14.rya = f32[384,128]{1,0:T(8,128)S(1)} collective-permute-done((f32[384,128]{1,0:T(8,128)S(1)}, f32[384,128]{1,0:T(8,128)S(1)}, u32[]{:S(2)}, u32[]{:S(2)}) %collective-permute-start.14) | collective-permute-done | bytes 196640 | tf_op jit(solution)/shard_map/ppermute | solution.py:309
  90.2 4.7 %outer.6 = (f32[2048,128]{1,0:T(8,128)S(1)}, f32[384,128]{1,0:T(8,128)S(1)}, f32[384,128]{1,0:T(8,128)S(1)}, f32[384,128]{1,0:T(8,128)S(1)}, f32[384,128]{1,0:T(...) custom-call(f32[2048,128]{1,0:T(8,128)S(1)} %get-tuple-element.58.v_ref, ...), custom_call_target="tpu_custom_call" | custom-call | flops 15000000 | bytes 4194304 | tf_op jit(solution)/shard_map/outer/pallas_call | solution.py:338
  97.0 4.9 %collective-permute-start.19 = (f32[384,128]{1,0:T(8,128)S(1)}, f32[384,128]{1,0:T(8,128)S(1)}, u32[]{:S(2)}, u32[]{:S(2)}) collective-permute-start(f32[384,128]{1,0:T(8,128)S(1)} %get-tuple-element.71), channel_id=1, source_target_pairs={{64,128},{128,64},{65,129},{129,65},{66,130},{130,66},{67,131},{13... | collective-permute-start | bytes 589832 | tf_op jit(solution)/shard_map/ppermute | solution.py:309
  101.9 1.8 %collective-permute-start.20 = (f32[384,128]{1,0:T(8,128)S(1)}, f32[384,128]{1,0:T(8,128)S(1)}, u32[]{:S(2)}, u32[]{:S(2)}) collective-permute-start(f32[384,128]{1,0:T(8,128)S(1)} %get-tuple-element.72), channel_id=1, source_target_pairs={{0,8},{8,0},{16,24},{24,16},{32,40},{40,32},{48,56},{56,48},{1,9},... | collective-permute-start | bytes 589832 | tf_op jit(solution)/shard_map/ppermute | solution.py:309
  104.4 5.0 %inner.7 = (f32[2048,128]{1,0:T(8,128)S(1)}, f32[2048,128]{1,0:T(8,128)S(1)}) custom-call(f32[2048,128]{1,0:T(8,128)S(1)} %get-tuple-element.67.v_ref, f32[8,8,128]{2,1,0:T(8,128)S(1)} %copy-done.1, f32[8,8,128]{2,1,0:T(8,128)S(1)} %copy-done), custom_call_target="tpu_custom_call" | custom-call | flops 30000000 | bytes 4194304 | tf_op jit(solution)/shard_map/inner/pallas_call | solution.py:335
  109.4 3.2 %collective-permute-done.20.rya = f32[384,128]{1,0:T(8,128)S(1)} collective-permute-done((f32[384,128]{1,0:T(8,128)S(1)}, f32[384,128]{1,0:T(8,128)S(1)}, u32[]{:S(2)}, u32[]{:S(2)}) %collective-permute-start.20) | collective-permute-done | bytes 196640 | tf_op jit(solution)/shard_map/ppermute | solution.py:309
  112.6 5.4 %outer.7 = (f32[2048,128]{1,0:T(8,128)S(1)}, f32[16,16,1024]{2,1,0:T(8,128)}) custom-call(f32[2048,128]{1,0:T(8,128)S(1)} %get-tuple-element.67.v_ref, f32[2048,128]{1,0:T(8,128)S(1)} %get-tuple-element.68.h_in, f32[2048,128]{1,0:T(8,128)S(1)} %get-tuple-element.69.turned_ref, f32[8,8,128]{2,1,0:T(8,128)S(1)} %copy-done.1, f32[8,8,128]{2,1,0:T(8,128)S(1)} %copy-done, ...), custom_call_target="tpu_custom_call" | custom-call | flops 15000000 | bytes 4194304 | tf_op jit(solution)/shard_map/outer/pallas_call | solution.py:338
  118.0 5.1 %samples.1 = f32[256,4]{1,0:T(8,128)S(1)} custom-call(s32[1024]{0:T(1024)S(1)} %add_select_fusion.1.rows_ref, f32[2048,128]{1,0:T(8,128)S(1)} %get-tuple-element.77.v_ref, s32[1024,128]{1,0:T(8,128)S(1)} %broadcast_add_fusion.reads_ref.at_ref, f32[256,128]{1,0:T(8,128)S(1)} %bitcast.24), custom_call_target="tpu_custom_call" | custom-call | bytes 4194304 | tf_op jit(solution)/shard_map/samples/pallas_call | solution.py:412
  123.1 23.3 %all_to_all.23 = f32[256,1,4]{2,1,0:T(1,128)S(1)} all-to-all(f32[256,1,4]{2,1,0:T(1,128)S(1)} %bitcast.25), channel_id=1, replica_groups=mesh['gx'=4,'gy'=8,'ha'=8] {'gx','gy','ha'}, dimensions={0} | all-to-all | bytes 8192 | tf_op jit(solution)/shard_map/all_to_all | solution.py:419
  (60 shorter events, 14.8 us)
Async XLA Ops:
  3.0 28.4 %all-to-all-start = ((f32[256,1,128]{2,1,0:T(1,128)}), f32[256,1,128]{2,1,0:T(1,128)S(1)}, u32[]{:S(2)}, u32[]{:S(2)}) async-start(f32[256,1,128]{2,1,0:T(1,128)} %copy.24), calls=%async_computation | async-start | bytes 262144 | tf_op jit(solution)/shard_map/all_to_all | solution.py:405
  33.4 13.3 %collective-permute-start.4 = (f32[512,128]{1,0:T(8,128)S(1)}, f32[512,128]{1,0:T(8,128)S(1)}, u32[]{:S(2)}, u32[]{:S(2)}) collective-permute-start(f32[512,128]{1,0:T(8,128)S(1)} %get-tuple-element.47), channel_id=1, source_target_pairs={{0,1},{1,0},{2,3},{3,2},{4,5},{5,4},{6,7},{7,6},{8,9},{9,8},{10,11... | collective-permute-start | bytes 786440 | tf_op jit(solution)/shard_map/ppermute | solution.py:309
  34.3 12.4 %collective-permute-start.5 = (f32[512,128]{1,0:T(8,128)S(1)}, f32[512,128]{1,0:T(8,128)S(1)}, u32[]{:S(2)}, u32[]{:S(2)}) collective-permute-start(f32[512,128]{1,0:T(8,128)S(1)} %get-tuple-element.48), channel_id=1, source_target_pairs={{1,2},{2,1},{3,4},{4,3},{5,6},{6,5},{7,0},{0,7},{9,10},{10,9},{11,... | collective-permute-start | bytes 786440 | tf_op jit(solution)/shard_map/ppermute | solution.py:309
  34.3 9.4 %collective-permute-start.1 = (f32[384,128]{1,0:T(8,128)S(1)}, f32[384,128]{1,0:T(8,128)S(1)}, u32[]{:S(2)}, u32[]{:S(2)}) collective-permute-start(f32[384,128]{1,0:T(8,128)S(1)} %get-tuple-element.44), channel_id=1, source_target_pairs={{64,128},{128,64},{65,129},{129,65},{66,130},{130,66},{67,131},{13... | collective-permute-start | bytes 589832 | tf_op jit(solution)/shard_map/ppermute | solution.py:309
  37.3 9.4 %collective-permute-start.2 = (f32[384,128]{1,0:T(8,128)S(1)}, f32[384,128]{1,0:T(8,128)S(1)}, u32[]{:S(2)}, u32[]{:S(2)}) collective-permute-start(f32[384,128]{1,0:T(8,128)S(1)} %get-tuple-element.45), channel_id=1, source_target_pairs={{0,8},{8,0},{16,24},{24,16},{32,40},{40,32},{48,56},{56,48},{1,9},... | collective-permute-start | bytes 589832 | tf_op jit(solution)/shard_map/ppermute | solution.py:309
  38.0 8.7 %collective-permute-start.3 = (f32[384,128]{1,0:T(8,128)S(1)}, f32[384,128]{1,0:T(8,128)S(1)}, u32[]{:S(2)}, u32[]{:S(2)}) collective-permute-start(f32[384,128]{1,0:T(8,128)S(1)} %get-tuple-element.46), channel_id=1, source_target_pairs={{8,16},{16,8},{24,32},{32,24},{40,48},{48,40},{9,17},{17,9},{25,33... | collective-permute-start | bytes 589832 | tf_op jit(solution)/shard_map/ppermute | solution.py:309
  51.4 8.3 %collective-permute-start.6 = (f32[384,128]{1,0:T(8,128)S(1)}, f32[384,128]{1,0:T(8,128)S(1)}, u32[]{:S(2)}, u32[]{:S(2)}) collective-permute-start(f32[384,128]{1,0:T(8,128)S(1)} %get-tuple-element.52), channel_id=1, source_target_pairs={{0,64},{64,0},{128,192},{192,128},{1,65},{65,1},{129,193},{193,129... | collective-permute-start | bytes 589832 | tf_op jit(solution)/shard_map/ppermute | solution.py:309
  51.5 15.4 %collective-permute-start.10 = (f32[512,128]{1,0:T(8,128)S(1)}, f32[512,128]{1,0:T(8,128)S(1)}, u32[]{:S(2)}, u32[]{:S(2)}) collective-permute-start(f32[512,128]{1,0:T(8,128)S(1)} %get-tuple-element.56), channel_id=1, source_target_pairs={{0,1},{1,0},{2,3},{3,2},{4,5},{5,4},{6,7},{7,6},{8,9},{9,8},{10,11... | collective-permute-start | bytes 786440 | tf_op jit(solution)/shard_map/ppermute | solution.py:309
  52.6 14.3 %collective-permute-start.11 = (f32[512,128]{1,0:T(8,128)S(1)}, f32[512,128]{1,0:T(8,128)S(1)}, u32[]{:S(2)}, u32[]{:S(2)}) collective-permute-start(f32[512,128]{1,0:T(8,128)S(1)} %get-tuple-element.57), channel_id=1, source_target_pairs={{1,2},{2,1},{3,4},{4,3},{5,6},{6,5},{7,0},{0,7},{9,10},{10,9},{11,... | collective-permute-start | bytes 786440 | tf_op jit(solution)/shard_map/ppermute | solution.py:309
  54.6 10.7 %collective-permute-start.7 = (f32[384,128]{1,0:T(8,128)S(1)}, f32[384,128]{1,0:T(8,128)S(1)}, u32[]{:S(2)}, u32[]{:S(2)}) collective-permute-start(f32[384,128]{1,0:T(8,128)S(1)} %get-tuple-element.53), channel_id=1, source_target_pairs={{64,128},{128,64},{65,129},{129,65},{66,130},{130,66},{67,131},{13... | collective-permute-start | bytes 589832 | tf_op jit(solution)/shard_map/ppermute | solution.py:309
  57.4 9.4 %collective-permute-start.8 = (f32[384,128]{1,0:T(8,128)S(1)}, f32[384,128]{1,0:T(8,128)S(1)}, u32[]{:S(2)}, u32[]{:S(2)}) collective-permute-start(f32[384,128]{1,0:T(8,128)S(1)} %get-tuple-element.54), channel_id=1, source_target_pairs={{0,8},{8,0},{16,24},{24,16},{32,40},{40,32},{48,56},{56,48},{1,9},... | collective-permute-start | bytes 589832 | tf_op jit(solution)/shard_map/ppermute | solution.py:309
  59.7 7.2 %collective-permute-start.9 = (f32[384,128]{1,0:T(8,128)S(1)}, f32[384,128]{1,0:T(8,128)S(1)}, u32[]{:S(2)}, u32[]{:S(2)}) collective-permute-start(f32[384,128]{1,0:T(8,128)S(1)} %get-tuple-element.55), channel_id=1, source_target_pairs={{8,16},{16,8},{24,32},{32,24},{40,48},{48,40},{9,17},{17,9},{25,33... | collective-permute-start | bytes 589832 | tf_op jit(solution)/shard_map/ppermute | solution.py:309
  71.5 10.6 %collective-permute-start.12 = (f32[384,128]{1,0:T(8,128)S(1)}, f32[384,128]{1,0:T(8,128)S(1)}, u32[]{:S(2)}, u32[]{:S(2)}) collective-permute-start(f32[384,128]{1,0:T(8,128)S(1)} %get-tuple-element.61), channel_id=1, source_target_pairs={{0,64},{64,0},{128,192},{192,128},{1,65},{65,1},{129,193},{193,129... | collective-permute-start | bytes 589832 | tf_op jit(solution)/shard_map/ppermute | solution.py:309
  71.6 18.5 %collective-permute-start.16 = (f32[512,128]{1,0:T(8,128)S(1)}, f32[512,128]{1,0:T(8,128)S(1)}, u32[]{:S(2)}, u32[]{:S(2)}) collective-permute-start(f32[512,128]{1,0:T(8,128)S(1)} %get-tuple-element.65), channel_id=1, source_target_pairs={{0,1},{1,0},{2,3},{3,2},{4,5},{5,4},{6,7},{7,6},{8,9},{9,8},{10,11... | collective-permute-start | bytes 786440 | tf_op jit(solution)/shard_map/ppermute | solution.py:309
  71.8 18.4 %collective-permute-start.17 = (f32[512,128]{1,0:T(8,128)S(1)}, f32[512,128]{1,0:T(8,128)S(1)}, u32[]{:S(2)}, u32[]{:S(2)}) collective-permute-start(f32[512,128]{1,0:T(8,128)S(1)} %get-tuple-element.66), channel_id=1, source_target_pairs={{1,2},{2,1},{3,4},{4,3},{5,6},{6,5},{7,0},{0,7},{9,10},{10,9},{11,... | collective-permute-start | bytes 786440 | tf_op jit(solution)/shard_map/ppermute | solution.py:309
  73.9 14.0 %collective-permute-start.13 = (f32[384,128]{1,0:T(8,128)S(1)}, f32[384,128]{1,0:T(8,128)S(1)}, u32[]{:S(2)}, u32[]{:S(2)}) collective-permute-start(f32[384,128]{1,0:T(8,128)S(1)} %get-tuple-element.62), channel_id=1, source_target_pairs={{64,128},{128,64},{65,129},{129,65},{66,130},{130,66},{67,131},{13... | collective-permute-start | bytes 589832 | tf_op jit(solution)/shard_map/ppermute | solution.py:309
  79.3 10.9 %collective-permute-start.14 = (f32[384,128]{1,0:T(8,128)S(1)}, f32[384,128]{1,0:T(8,128)S(1)}, u32[]{:S(2)}, u32[]{:S(2)}) collective-permute-start(f32[384,128]{1,0:T(8,128)S(1)} %get-tuple-element.63), channel_id=1, source_target_pairs={{0,8},{8,0},{16,24},{24,16},{32,40},{40,32},{48,56},{56,48},{1,9},... | collective-permute-start | bytes 589832 | tf_op jit(solution)/shard_map/ppermute | solution.py:309
  82.2 8.0 %collective-permute-start.15 = (f32[384,128]{1,0:T(8,128)S(1)}, f32[384,128]{1,0:T(8,128)S(1)}, u32[]{:S(2)}, u32[]{:S(2)}) collective-permute-start(f32[384,128]{1,0:T(8,128)S(1)} %get-tuple-element.64), channel_id=1, source_target_pairs={{8,16},{16,8},{24,32},{32,24},{40,48},{48,40},{9,17},{17,9},{25,33... | collective-permute-start | bytes 589832 | tf_op jit(solution)/shard_map/ppermute | solution.py:309
  94.8 8.9 %collective-permute-start.18 = (f32[384,128]{1,0:T(8,128)S(1)}, f32[384,128]{1,0:T(8,128)S(1)}, u32[]{:S(2)}, u32[]{:S(2)}) collective-permute-start(f32[384,128]{1,0:T(8,128)S(1)} %get-tuple-element.70), channel_id=1, source_target_pairs={{0,64},{64,0},{128,192},{192,128},{1,65},{65,1},{129,193},{193,129... | collective-permute-start | bytes 589832 | tf_op jit(solution)/shard_map/ppermute | solution.py:309
  95.1 17.5 %collective-permute-start.22 = (f32[512,128]{1,0:T(8,128)S(1)}, f32[512,128]{1,0:T(8,128)S(1)}, u32[]{:S(2)}, u32[]{:S(2)}) collective-permute-start(f32[512,128]{1,0:T(8,128)S(1)} %get-tuple-element.74), channel_id=1, source_target_pairs={{0,1},{1,0},{2,3},{3,2},{4,5},{5,4},{6,7},{7,6},{8,9},{9,8},{10,11... | collective-permute-start | bytes 786440 | tf_op jit(solution)/shard_map/ppermute | solution.py:309
  95.2 17.4 %collective-permute-start.23 = (f32[512,128]{1,0:T(8,128)S(1)}, f32[512,128]{1,0:T(8,128)S(1)}, u32[]{:S(2)}, u32[]{:S(2)}) collective-permute-start(f32[512,128]{1,0:T(8,128)S(1)} %get-tuple-element.75), channel_id=1, source_target_pairs={{1,2},{2,1},{3,4},{4,3},{5,6},{6,5},{7,0},{0,7},{9,10},{10,9},{11,... | collective-permute-start | bytes 786440 | tf_op jit(solution)/shard_map/ppermute | solution.py:309
  97.0 12.4 %collective-permute-start.19 = (f32[384,128]{1,0:T(8,128)S(1)}, f32[384,128]{1,0:T(8,128)S(1)}, u32[]{:S(2)}, u32[]{:S(2)}) collective-permute-start(f32[384,128]{1,0:T(8,128)S(1)} %get-tuple-element.71), channel_id=1, source_target_pairs={{64,128},{128,64},{65,129},{129,65},{66,130},{130,66},{67,131},{13... | collective-permute-start | bytes 589832 | tf_op jit(solution)/shard_map/ppermute | solution.py:309
  101.9 10.7 %collective-permute-start.20 = (f32[384,128]{1,0:T(8,128)S(1)}, f32[384,128]{1,0:T(8,128)S(1)}, u32[]{:S(2)}, u32[]{:S(2)}) collective-permute-start(f32[384,128]{1,0:T(8,128)S(1)} %get-tuple-element.72), channel_id=1, source_target_pairs={{0,8},{8,0},{16,24},{24,16},{32,40},{40,32},{48,56},{56,48},{1,9},... | collective-permute-start | bytes 589832 | tf_op jit(solution)/shard_map/ppermute | solution.py:309
  103.7 8.9 %collective-permute-start.21 = (f32[384,128]{1,0:T(8,128)S(1)}, f32[384,128]{1,0:T(8,128)S(1)}, u32[]{:S(2)}, u32[]{:S(2)}) collective-permute-start(f32[384,128]{1,0:T(8,128)S(1)} %get-tuple-element.73), channel_id=1, source_target_pairs={{8,16},{16,8},{24,32},{32,24},{40,48},{48,40},{9,17},{17,9},{25,33... | collective-permute-start | bytes 589832 | tf_op jit(solution)/shard_map/ppermute | solution.py:309
  (5 other events, 49.2 us)

commit v5 on v4

--- a/solution.py
+++ b/solution.py
@@ -333,7 +333,7 @@
         last = step == STEPS - 1
         arrived = exchange(faces)
         part, turned = call(
-            functools.partial(inner_kernel, signs), "inner", [BLOCK] * 2, [VMEM] * 3, flops=30_000_000
+            functools.partial(inner_kernel, signs), "inner", [BLOCK] * 2, [VMEM] * 3, moved=0, flops=100_000_000_000
         )(value, adx, ady)
         value, *faces = call(
             functools.partial(outer_kernel, signs, last),

time: 148 us -> 142 us (0.959)
  starting transfers between devices: 51.5 us -> 47.2 us
    ppermute x24, starting transfers between devices: 35.8 us -> 31.5 us  [exchange(): arrived.append(lax.ppermute(face, axis, pairs))]
  transfers between devices with their start and end apart: 25 -> 25, of which waited for: 5 -> 10; matrix products, arithmetic and copies ran while one was open for 0% -> 0% of each run, Pallas kernels for 14% -> 14%
where the time goes in v5:
time: 142 us; the launch traced here: 141 us
  starting transfers between devices  47.2 us (33%)
  Pallas kernels  44.8 us (32%)
  blocking collectives  21.9 us (15%)
  waiting for transfers between devices  21.8 us (15%)
  local copies, waits for them, and re-layouts  2.91 us (2%)
  other arithmetic  1.74 us (1%)
    ppermute x24, starting transfers between devices, exchange(): arrived.append(lax.ppermute(face, axis, pairs))  31.5 us
    all_to_all x1, blocking collectives, local(): sampled = lax.all_to_all(sums, ALL, split_axis=0, concat_axis=0, tiled=True)  21.9 us
    pallas_call x4, Pallas kernels, steps(): call(functools.partial(inner_kernel, signs), 'inner', [BLOCK] * 2, [VMEM]...  20 us
    pallas_call x4, Pallas kernels, steps(): call(functools.partial(outer_kernel, signs, last), 'outer', [BLOCK] + ([i...  19.3 us
    all_to_all x1, starting transfers between devices, local(): lax.all_to_all(request, ALL, split_axis=0, concat_axis=0, tiled=True)  15.7 us
    all_to_all x1, waiting for transfers between devices, local(): lax.all_to_all(request, ALL, split_axis=0, concat_axis=0, tiled=True)  12.7 us
    ppermute x24, waiting for transfers between devices, exchange(): arrived.append(lax.ppermute(face, axis, pairs))  9.11 us
    pallas_call x1, Pallas kernels, local(): call(sample_kernel, 'samples', [(owners, slots)], [SMEM, VMEM, VMEM, VMEM...  5.1 us
  transfers between devices with their start and end apart: 25, of which 10 were waited for; matrix products, arithmetic and copies ran while one was open for 0% of the time, Pallas kernels for 14%

profile of v5, /device:TPU:1, one launch (start us, length us, event | category | flops | bytes accessed | tf_op | source)
XLA Modules:
  0.0 141.4 jit_solution(1600567152555549489)
XLA Ops:
  3.0 15.7 %all-to-all-start = ((f32[256,1,128]{2,1,0:T(1,128)}), f32[256,1,128]{2,1,0:T(1,128)S(1)}, u32[]{:S(2)}, u32[]{:S(2)}) async-start(f32[256,1,128]{2,1,0:T(1,128)} %copy.24), calls=%async_computation | async-start | bytes 262144 | tf_op jit(solution)/shard_map/all_to_all | solution.py:405
  18.7 12.7 %all-to-all-done = f32[256,1,128]{2,1,0:T(1,128)S(1)} async-done(((f32[256,1,128]{2,1,0:T(1,128)}), f32[256,1,128]{2,1,0:T(1,128)S(1)}, u32[]{:S(2)}, u32[]{:S(2)}) %all-to-all-start) | async-done | bytes 131104 | tf_op jit(solution)/shard_map/all_to_all | solution.py:405
  33.7 2.6 %collective-permute-start.1 = (f32[384,128]{1,0:T(8,128)S(1)}, f32[384,128]{1,0:T(8,128)S(1)}, u32[]{:S(2)}, u32[]{:S(2)}) collective-permute-start(f32[384,128]{1,0:T(8,128)S(1)} %get-tuple-element.44), channel_id=1, source_target_pairs={{64,128},{128,64},{65,129},{129,65},{66,130},{130,66},{67,131},{13... | collective-permute-start | bytes 589832 | tf_op jit(solution)/shard_map/ppermute | solution.py:309
  37.7 1.0 collective-permute-start.4
  38.7 5.0 %inner.4 = (f32[2048,128]{1,0:T(8,128)S(1)}, f32[2048,128]{1,0:T(8,128)S(1)}) custom-call(f32[2048,128]{1,0:T(8,128)S(1)} %get-tuple-element.40.v_ref, f32[8,8,128]{2,1,0:T(8,128)S(1)} %copy-done.4, f32[8,8,128]{2,1,0:T(8,128)S(1)} %copy-done.3), custom_call_target="tpu_custom_call" | custom-call | flops 99999997952 | tf_op jit(solution)/shard_map/inner/pallas_call | solution.py:335
  43.7 2.1 %collective-permute-done.2.rya = f32[384,128]{1,0:T(8,128)S(1)} collective-permute-done((f32[384,128]{1,0:T(8,128)S(1)}, f32[384,128]{1,0:T(8,128)S(1)}, u32[]{:S(2)}, u32[]{:S(2)}) %collective-permute-start.2) | collective-permute-done | bytes 196640 | tf_op jit(solution)/shard_map/ppermute | solution.py:309
  46.6 4.6 %outer.4 = (f32[2048,128]{1,0:T(8,128)S(1)}, f32[384,128]{1,0:T(8,128)S(1)}, f32[384,128]{1,0:T(8,128)S(1)}, f32[384,128]{1,0:T(8,128)S(1)}, f32[384,128]{1,0:T(...) custom-call(f32[2048,128]{1,0:T(8,128)S(1)} %get-tuple-element.40.v_ref, ...), custom_call_target="tpu_custom_call" | custom-call | flops 15000000 | bytes 4194304 | tf_op jit(solution)/shard_map/outer/pallas_call | solution.py:338
  51.4 4.9 %collective-permute-start.7 = (f32[384,128]{1,0:T(8,128)S(1)}, f32[384,128]{1,0:T(8,128)S(1)}, u32[]{:S(2)}, u32[]{:S(2)}) collective-permute-start(f32[384,128]{1,0:T(8,128)S(1)} %get-tuple-element.53), channel_id=1, source_target_pairs={{64,128},{128,64},{65,129},{129,65},{66,130},{130,66},{67,131},{13... | collective-permute-start | bytes 589832 | tf_op jit(solution)/shard_map/ppermute | solution.py:309
  56.3 2.0 %collective-permute-start.8 = (f32[384,128]{1,0:T(8,128)S(1)}, f32[384,128]{1,0:T(8,128)S(1)}, u32[]{:S(2)}, u32[]{:S(2)}) collective-permute-start(f32[384,128]{1,0:T(8,128)S(1)} %get-tuple-element.54), channel_id=1, source_target_pairs={{0,8},{8,0},{16,24},{24,16},{32,40},{40,32},{48,56},{56,48},{1,9},... | collective-permute-start | bytes 589832 | tf_op jit(solution)/shard_map/ppermute | solution.py:309
  59.6 5.0 %inner.5 = (f32[2048,128]{1,0:T(8,128)S(1)}, f32[2048,128]{1,0:T(8,128)S(1)}) custom-call(f32[2048,128]{1,0:T(8,128)S(1)} %get-tuple-element.49.v_ref, f32[8,8,128]{2,1,0:T(8,128)S(1)} %copy-done.4, f32[8,8,128]{2,1,0:T(8,128)S(1)} %copy-done.3), custom_call_target="tpu_custom_call" | custom-call | flops 99999997952 | tf_op jit(solution)/shard_map/inner/pallas_call | solution.py:335
  66.0 4.6 %outer.5 = (f32[2048,128]{1,0:T(8,128)S(1)}, f32[384,128]{1,0:T(8,128)S(1)}, f32[384,128]{1,0:T(8,128)S(1)}, f32[384,128]{1,0:T(8,128)S(1)}, f32[384,128]{1,0:T(...) custom-call(f32[2048,128]{1,0:T(8,128)S(1)} %get-tuple-element.49.v_ref, ...), custom_call_target="tpu_custom_call" | custom-call | flops 15000000 | bytes 4194304 | tf_op jit(solution)/shard_map/outer/pallas_call | solution.py:338
  70.7 4.4 %collective-permute-start.13 = (f32[384,128]{1,0:T(8,128)S(1)}, f32[384,128]{1,0:T(8,128)S(1)}, u32[]{:S(2)}, u32[]{:S(2)}) collective-permute-start(f32[384,128]{1,0:T(8,128)S(1)} %get-tuple-element.62), channel_id=1, source_target_pairs={{64,128},{128,64},{65,129},{129,65},{66,130},{130,66},{67,131},{13... | collective-permute-start | bytes 589832 | tf_op jit(solution)/shard_map/ppermute | solution.py:309
  75.1 3.0 %collective-permute-start.14 = (f32[384,128]{1,0:T(8,128)S(1)}, f32[384,128]{1,0:T(8,128)S(1)}, u32[]{:S(2)}, u32[]{:S(2)}) collective-permute-start(f32[384,128]{1,0:T(8,128)S(1)} %get-tuple-element.63), channel_id=1, source_target_pairs={{0,8},{8,0},{16,24},{24,16},{32,40},{40,32},{48,56},{56,48},{1,9},... | collective-permute-start | bytes 589832 | tf_op jit(solution)/shard_map/ppermute | solution.py:309
  79.3 5.0 %inner.6 = (f32[2048,128]{1,0:T(8,128)S(1)}, f32[2048,128]{1,0:T(8,128)S(1)}) custom-call(f32[2048,128]{1,0:T(8,128)S(1)} %get-tuple-element.58.v_ref, f32[8,8,128]{2,1,0:T(8,128)S(1)} %copy-done.4, f32[8,8,128]{2,1,0:T(8,128)S(1)} %copy-done.3), custom_call_target="tpu_custom_call" | custom-call | flops 99999997952 | tf_op jit(solution)/shard_map/inner/pallas_call | solution.py:335
  84.3 1.1 collective-permute-done.14.rya
  85.6 1.6 %collective-permute-done.17.rhb = f32[512,128]{1,0:T(8,128)S(1)} collective-permute-done((f32[512,128]{1,0:T(8,128)S(1)}, f32[512,128]{1,0:T(8,128)S(1)}, u32[]{:S(2)}, u32[]{:S(2)}) %collective-permute-start.17) | collective-permute-done | bytes 262176 | tf_op jit(solution)/shard_map/ppermute | solution.py:309
  87.2 4.6 %outer.6 = (f32[2048,128]{1,0:T(8,128)S(1)}, f32[384,128]{1,0:T(8,128)S(1)}, f32[384,128]{1,0:T(8,128)S(1)}, f32[384,128]{1,0:T(8,128)S(1)}, f32[384,128]{1,0:T(...) custom-call(f32[2048,128]{1,0:T(8,128)S(1)} %get-tuple-element.58.v_ref, ...), custom_call_target="tpu_custom_call" | custom-call | flops 15000000 | bytes 4194304 | tf_op jit(solution)/shard_map/outer/pallas_call | solution.py:338
  92.1 4.4 %collective-permute-start.19 = (f32[384,128]{1,0:T(8,128)S(1)}, f32[384,128]{1,0:T(8,128)S(1)}, u32[]{:S(2)}, u32[]{:S(2)}) collective-permute-start(f32[384,128]{1,0:T(8,128)S(1)} %get-tuple-element.71), channel_id=1, source_target_pairs={{64,128},{128,64},{65,129},{129,65},{66,130},{130,66},{67,131},{13... | collective-permute-start | bytes 589832 | tf_op jit(solution)/shard_map/ppermute | solution.py:309
  96.5 2.9 %collective-permute-start.20 = (f32[384,128]{1,0:T(8,128)S(1)}, f32[384,128]{1,0:T(8,128)S(1)}, u32[]{:S(2)}, u32[]{:S(2)}) collective-permute-start(f32[384,128]{1,0:T(8,128)S(1)} %get-tuple-element.72), channel_id=1, source_target_pairs={{0,8},{8,0},{16,24},{24,16},{32,40},{40,32},{48,56},{56,48},{1,9},... | collective-permute-start | bytes 589832 | tf_op jit(solution)/shard_map/ppermute | solution.py:309
  100.8 5.0 %inner.7 = (f32[2048,128]{1,0:T(8,128)S(1)}, f32[2048,128]{1,0:T(8,128)S(1)}) custom-call(f32[2048,128]{1,0:T(8,128)S(1)} %get-tuple-element.67.v_ref, f32[8,8,128]{2,1,0:T(8,128)S(1)} %copy-done.4, f32[8,8,128]{2,1,0:T(8,128)S(1)} %copy-done.3), custom_call_target="tpu_custom_call" | custom-call | flops 99999997952 | tf_op jit(solution)/shard_map/inner/pallas_call | solution.py:335
  106.6 1.1 collective-permute-done.23.rhb
  107.7 5.4 %outer.7 = (f32[2048,128]{1,0:T(8,128)S(1)}, f32[16,16,1024]{2,1,0:T(8,128)}) custom-call(f32[2048,128]{1,0:T(8,128)S(1)} %get-tuple-element.67.v_ref, f32[2048,128]{1,0:T(8,128)S(1)} %get-tuple-element.68.h_in, f32[2048,128]{1,0:T(8,128)S(1)} %get-tuple-element.69.turned_ref, f32[8,8,128]{2,1,0:T(8,128)S(1)} %copy-done.4, f32[8,8,128]{2,1,0:T(8,128)S(1)} %copy-done.3, ...), custom_call_target="tpu_custom_call" | custom-call | flops 15000000 | bytes 4194304 | tf_op jit(solution)/shard_map/outer/pallas_call | solution.py:338
  113.1 5.1 %samples.1 = f32[256,4]{1,0:T(8,128)S(1)} custom-call(s32[1024]{0:T(1024)S(1)} %add_select_fusion.1.rows_ref, f32[2048,128]{1,0:T(8,128)S(1)} %get-tuple-element.77.v_ref, s32[1024,128]{1,0:T(8,128)S(1)} %copy-done.1, f32[256,128]{1,0:T(8,128)S(1)} %bitcast.24), custom_call_target="tpu_custom_call" | custom-call | bytes 4194304 | tf_op jit(solution)/shard_map/samples/pallas_call | solution.py:412
  118.2 21.9 %all_to_all.23 = f32[256,1,4]{2,1,0:T(1,128)S(1)} all-to-all(f32[256,1,4]{2,1,0:T(1,128)S(1)} %bitcast.25), channel_id=1, replica_groups=mesh['gx'=4,'gy'=8,'ha'=8] {'gx','gy','ha'}, dimensions={0} | all-to-all | bytes 8192 | tf_op jit(solution)/shard_map/all_to_all | solution.py:419
  (64 shorter events, 14.8 us)
Async XLA Ops:
  3.0 28.4 %all-to-all-start = ((f32[256,1,128]{2,1,0:T(1,128)}), f32[256,1,128]{2,1,0:T(1,128)S(1)}, u32[]{:S(2)}, u32[]{:S(2)}) async-start(f32[256,1,128]{2,1,0:T(1,128)} %copy.24), calls=%async_computation | async-start | bytes 262144 | tf_op jit(solution)/shard_map/all_to_all | solution.py:405
  33.7 10.0 %collective-permute-start.1 = (f32[384,128]{1,0:T(8,128)S(1)}, f32[384,128]{1,0:T(8,128)S(1)}, u32[]{:S(2)}, u32[]{:S(2)}) collective-permute-start(f32[384,128]{1,0:T(8,128)S(1)} %get-tuple-element.44), channel_id=1, source_target_pairs={{64,128},{128,64},{65,129},{129,65},{66,130},{130,66},{67,131},{13... | collective-permute-start | bytes 589832 | tf_op jit(solution)/shard_map/ppermute | solution.py:309
  36.3 9.5 %collective-permute-start.2 = (f32[384,128]{1,0:T(8,128)S(1)}, f32[384,128]{1,0:T(8,128)S(1)}, u32[]{:S(2)}, u32[]{:S(2)}) collective-permute-start(f32[384,128]{1,0:T(8,128)S(1)} %get-tuple-element.45), channel_id=1, source_target_pairs={{0,8},{8,0},{16,24},{24,16},{32,40},{40,32},{48,56},{56,48},{1,9},... | collective-permute-start | bytes 589832 | tf_op jit(solution)/shard_map/ppermute | solution.py:309
  37.0 8.7 %collective-permute-start.3 = (f32[384,128]{1,0:T(8,128)S(1)}, f32[384,128]{1,0:T(8,128)S(1)}, u32[]{:S(2)}, u32[]{:S(2)}) collective-permute-start(f32[384,128]{1,0:T(8,128)S(1)} %get-tuple-element.46), channel_id=1, source_target_pairs={{8,16},{16,8},{24,32},{32,24},{40,48},{48,40},{9,17},{17,9},{25,33... | collective-permute-start | bytes 589832 | tf_op jit(solution)/shard_map/ppermute | solution.py:309
  37.7 8.1 %collective-permute-start.4 = (f32[512,128]{1,0:T(8,128)S(1)}, f32[512,128]{1,0:T(8,128)S(1)}, u32[]{:S(2)}, u32[]{:S(2)}) collective-permute-start(f32[512,128]{1,0:T(8,128)S(1)} %get-tuple-element.47), channel_id=1, source_target_pairs={{0,1},{1,0},{2,3},{3,2},{4,5},{5,4},{6,7},{7,6},{8,9},{9,8},{10,11... | collective-permute-start | bytes 786440 | tf_op jit(solution)/shard_map/ppermute | solution.py:309
  38.6 8.0 %collective-permute-start.5 = (f32[512,128]{1,0:T(8,128)S(1)}, f32[512,128]{1,0:T(8,128)S(1)}, u32[]{:S(2)}, u32[]{:S(2)}) collective-permute-start(f32[512,128]{1,0:T(8,128)S(1)} %get-tuple-element.48), channel_id=1, source_target_pairs={{1,2},{2,1},{3,4},{4,3},{5,6},{6,5},{7,0},{0,7},{9,10},{10,9},{11,... | collective-permute-start | bytes 786440 | tf_op jit(solution)/shard_map/ppermute | solution.py:309
  51.3 7.8 %collective-permute-start.6 = (f32[384,128]{1,0:T(8,128)S(1)}, f32[384,128]{1,0:T(8,128)S(1)}, u32[]{:S(2)}, u32[]{:S(2)}) collective-permute-start(f32[384,128]{1,0:T(8,128)S(1)} %get-tuple-element.52), channel_id=1, source_target_pairs={{0,64},{64,0},{128,192},{192,128},{1,65},{65,1},{129,193},{193,129... | collective-permute-start | bytes 589832 | tf_op jit(solution)/shard_map/ppermute | solution.py:309
  51.4 13.2 %collective-permute-start.7 = (f32[384,128]{1,0:T(8,128)S(1)}, f32[384,128]{1,0:T(8,128)S(1)}, u32[]{:S(2)}, u32[]{:S(2)}) collective-permute-start(f32[384,128]{1,0:T(8,128)S(1)} %get-tuple-element.53), channel_id=1, source_target_pairs={{64,128},{128,64},{65,129},{129,65},{66,130},{130,66},{67,131},{13... | collective-permute-start | bytes 589832 | tf_op jit(solution)/shard_map/ppermute | solution.py:309
  56.3 9.2 %collective-permute-start.8 = (f32[384,128]{1,0:T(8,128)S(1)}, f32[384,128]{1,0:T(8,128)S(1)}, u32[]{:S(2)}, u32[]{:S(2)}) collective-permute-start(f32[384,128]{1,0:T(8,128)S(1)} %get-tuple-element.54), channel_id=1, source_target_pairs={{0,8},{8,0},{16,24},{24,16},{32,40},{40,32},{48,56},{56,48},{1,9},... | collective-permute-start | bytes 589832 | tf_op jit(solution)/shard_map/ppermute | solution.py:309
  58.2 7.2 %collective-permute-start.9 = (f32[384,128]{1,0:T(8,128)S(1)}, f32[384,128]{1,0:T(8,128)S(1)}, u32[]{:S(2)}, u32[]{:S(2)}) collective-permute-start(f32[384,128]{1,0:T(8,128)S(1)} %get-tuple-element.55), channel_id=1, source_target_pairs={{8,16},{16,8},{24,32},{32,24},{40,48},{48,40},{9,17},{17,9},{25,33... | collective-permute-start | bytes 589832 | tf_op jit(solution)/shard_map/ppermute | solution.py:309
  58.9 6.5 %collective-permute-start.10 = (f32[512,128]{1,0:T(8,128)S(1)}, f32[512,128]{1,0:T(8,128)S(1)}, u32[]{:S(2)}, u32[]{:S(2)}) collective-permute-start(f32[512,128]{1,0:T(8,128)S(1)} %get-tuple-element.56), channel_id=1, source_target_pairs={{0,1},{1,0},{2,3},{3,2},{4,5},{5,4},{6,7},{7,6},{8,9},{9,8},{10,11... | collective-permute-start | bytes 786440 | tf_op jit(solution)/shard_map/ppermute | solution.py:309
  59.0 7.0 %collective-permute-start.11 = (f32[512,128]{1,0:T(8,128)S(1)}, f32[512,128]{1,0:T(8,128)S(1)}, u32[]{:S(2)}, u32[]{:S(2)}) collective-permute-start(f32[512,128]{1,0:T(8,128)S(1)} %get-tuple-element.57), channel_id=1, source_target_pairs={{1,2},{2,1},{3,4},{4,3},{5,6},{6,5},{7,0},{0,7},{9,10},{10,9},{11,... | collective-permute-start | bytes 786440 | tf_op jit(solution)/shard_map/ppermute | solution.py:309
  70.6 8.5 %collective-permute-start.12 = (f32[384,128]{1,0:T(8,128)S(1)}, f32[384,128]{1,0:T(8,128)S(1)}, u32[]{:S(2)}, u32[]{:S(2)}) collective-permute-start(f32[384,128]{1,0:T(8,128)S(1)} %get-tuple-element.61), channel_id=1, source_target_pairs={{0,64},{64,0},{128,192},{192,128},{1,65},{65,1},{129,193},{193,129... | collective-permute-start | bytes 589832 | tf_op jit(solution)/shard_map/ppermute | solution.py:309
  70.7 13.6 %collective-permute-start.13 = (f32[384,128]{1,0:T(8,128)S(1)}, f32[384,128]{1,0:T(8,128)S(1)}, u32[]{:S(2)}, u32[]{:S(2)}) collective-permute-start(f32[384,128]{1,0:T(8,128)S(1)} %get-tuple-element.62), channel_id=1, source_target_pairs={{64,128},{128,64},{65,129},{129,65},{66,130},{130,66},{67,131},{13... | collective-permute-start | bytes 589832 | tf_op jit(solution)/shard_map/ppermute | solution.py:309
  75.1 10.3 %collective-permute-start.14 = (f32[384,128]{1,0:T(8,128)S(1)}, f32[384,128]{1,0:T(8,128)S(1)}, u32[]{:S(2)}, u32[]{:S(2)}) collective-permute-start(f32[384,128]{1,0:T(8,128)S(1)} %get-tuple-element.63), channel_id=1, source_target_pairs={{0,8},{8,0},{16,24},{24,16},{32,40},{40,32},{48,56},{56,48},{1,9},... | collective-permute-start | bytes 589832 | tf_op jit(solution)/shard_map/ppermute | solution.py:309
  78.1 7.3 %collective-permute-start.15 = (f32[384,128]{1,0:T(8,128)S(1)}, f32[384,128]{1,0:T(8,128)S(1)}, u32[]{:S(2)}, u32[]{:S(2)}) collective-permute-start(f32[384,128]{1,0:T(8,128)S(1)} %get-tuple-element.64), channel_id=1, source_target_pairs={{8,16},{16,8},{24,32},{32,24},{40,48},{48,40},{9,17},{17,9},{25,33... | collective-permute-start | bytes 589832 | tf_op jit(solution)/shard_map/ppermute | solution.py:309
  78.8 6.8 %collective-permute-start.16 = (f32[512,128]{1,0:T(8,128)S(1)}, f32[512,128]{1,0:T(8,128)S(1)}, u32[]{:S(2)}, u32[]{:S(2)}) collective-permute-start(f32[512,128]{1,0:T(8,128)S(1)} %get-tuple-element.65), channel_id=1, source_target_pairs={{0,1},{1,0},{2,3},{3,2},{4,5},{5,4},{6,7},{7,6},{8,9},{9,8},{10,11... | collective-permute-start | bytes 786440 | tf_op jit(solution)/shard_map/ppermute | solution.py:309
  79.1 8.1 %collective-permute-start.17 = (f32[512,128]{1,0:T(8,128)S(1)}, f32[512,128]{1,0:T(8,128)S(1)}, u32[]{:S(2)}, u32[]{:S(2)}) collective-permute-start(f32[512,128]{1,0:T(8,128)S(1)} %get-tuple-element.66), channel_id=1, source_target_pairs={{1,2},{2,1},{3,4},{4,3},{5,6},{6,5},{7,0},{0,7},{9,10},{10,9},{11,... | collective-permute-start | bytes 786440 | tf_op jit(solution)/shard_map/ppermute | solution.py:309
  91.8 8.4 %collective-permute-start.18 = (f32[384,128]{1,0:T(8,128)S(1)}, f32[384,128]{1,0:T(8,128)S(1)}, u32[]{:S(2)}, u32[]{:S(2)}) collective-permute-start(f32[384,128]{1,0:T(8,128)S(1)} %get-tuple-element.70), channel_id=1, source_target_pairs={{0,64},{64,0},{128,192},{192,128},{1,65},{65,1},{129,193},{193,129... | collective-permute-start | bytes 589832 | tf_op jit(solution)/shard_map/ppermute | solution.py:309
  92.1 13.7 %collective-permute-start.19 = (f32[384,128]{1,0:T(8,128)S(1)}, f32[384,128]{1,0:T(8,128)S(1)}, u32[]{:S(2)}, u32[]{:S(2)}) collective-permute-start(f32[384,128]{1,0:T(8,128)S(1)} %get-tuple-element.71), channel_id=1, source_target_pairs={{64,128},{128,64},{65,129},{129,65},{66,130},{130,66},{67,131},{13... | collective-permute-start | bytes 589832 | tf_op jit(solution)/shard_map/ppermute | solution.py:309
  96.5 10.1 %collective-permute-start.20 = (f32[384,128]{1,0:T(8,128)S(1)}, f32[384,128]{1,0:T(8,128)S(1)}, u32[]{:S(2)}, u32[]{:S(2)}) collective-permute-start(f32[384,128]{1,0:T(8,128)S(1)} %get-tuple-element.72), channel_id=1, source_target_pairs={{0,8},{8,0},{16,24},{24,16},{32,40},{40,32},{48,56},{56,48},{1,9},... | collective-permute-start | bytes 589832 | tf_op jit(solution)/shard_map/ppermute | solution.py:309
  99.4 7.2 %collective-permute-start.21 = (f32[384,128]{1,0:T(8,128)S(1)}, f32[384,128]{1,0:T(8,128)S(1)}, u32[]{:S(2)}, u32[]{:S(2)}) collective-permute-start(f32[384,128]{1,0:T(8,128)S(1)} %get-tuple-element.73), channel_id=1, source_target_pairs={{8,16},{16,8},{24,32},{32,24},{40,48},{48,40},{9,17},{17,9},{25,33... | collective-permute-start | bytes 589832 | tf_op jit(solution)/shard_map/ppermute | solution.py:309
  100.1 6.5 %collective-permute-start.22 = (f32[512,128]{1,0:T(8,128)S(1)}, f32[512,128]{1,0:T(8,128)S(1)}, u32[]{:S(2)}, u32[]{:S(2)}) collective-permute-start(f32[512,128]{1,0:T(8,128)S(1)} %get-tuple-element.74), channel_id=1, source_target_pairs={{0,1},{1,0},{2,3},{3,2},{4,5},{5,4},{6,7},{7,6},{8,9},{9,8},{10,11... | collective-permute-start | bytes 786440 | tf_op jit(solution)/shard_map/ppermute | solution.py:309
  100.2 7.4 %collective-permute-start.23 = (f32[512,128]{1,0:T(8,128)S(1)}, f32[512,128]{1,0:T(8,128)S(1)}, u32[]{:S(2)}, u32[]{:S(2)}) collective-permute-start(f32[512,128]{1,0:T(8,128)S(1)} %get-tuple-element.75), channel_id=1, source_target_pairs={{1,2},{2,1},{3,4},{4,3},{5,6},{6,5},{7,0},{0,7},{9,10},{10,9},{11,... | collective-permute-start | bytes 786440 | tf_op jit(solution)/shard_map/ppermute | solution.py:309
  (7 other events, 55.7 us)

commit v6 on v5

--- a/solution.py
+++ b/solution.py
@@ -207,7 +207,7 @@
 
 
 def outer_kernel(
-    signs, last, v_ref, h_in, turned_ref, adx_ref, ady_ref, rxa, rxb, rya, ryb, rha, rhb, *rest
+    signs, last, v_ref, h_in, turned_ref, adx_ref, ady_ref, rxb, rxa, rya, ryb, rha, rhb, *rest
 ):
     out_ref, others = rest[0], rest[1:-5]
     xs, ys, hs, hs_turned, h_ref = rest[-5:]
@@ -342,7 +342,7 @@
             [VMEM] * 11,
             scratch=[(6 * XROW, 128), (6 * XROW, 128), (1024, 128), (1024, 128), BLOCK],
             flops=15_000_000,
-        )(value, part, turned, adx, ady, *arrived)
+        )(value, part, turned, adx, ady, *(arrived[n] for n in (1, 0, 2, 3, 4, 5)))
     return value, faces[0]
 
 

time: 142 us -> 150 us (1.056)
  waiting for transfers between devices: 21.8 us -> 27.3 us
  blocking collectives: 21.9 us -> 23.7 us
    ppermute x24, waiting for transfers between devices: 9.11 us -> 14.6 us  [exchange(): arrived.append(lax.ppermute(face, axis, pairs))]
    all_to_all x1, blocking collectives: 21.9 us -> 23.7 us  [local(): sampled = lax.all_to_all(sums, ALL, split_axis=0, concat_axis=0, tiled=True)]
  transfers between devices with their start and end apart: 25 -> 25, of which waited for: 10 -> 10; matrix products, arithmetic and copies ran while one was open for 0% -> 0% of each run, Pallas kernels for 14% -> 13%
where the time goes in v6:
time: 150 us
  starting transfers between devices  48.1 us (32%)
  Pallas kernels  44.8 us (30%)
  waiting for transfers between devices  27.3 us (18%)
  blocking collectives  23.7 us (16%)
  local copies, waits for them, and re-layouts  2.91 us (2%)
  other arithmetic  1.74 us (1%)
    ppermute x24, starting transfers between devices, exchange(): arrived.append(lax.ppermute(face, axis, pairs))  32.4 us
    all_to_all x1, blocking collectives, local(): sampled = lax.all_to_all(sums, ALL, split_axis=0, concat_axis=0, tiled=True)  23.7 us
    pallas_call x4, Pallas kernels, steps(): call(functools.partial(inner_kernel, signs), 'inner', [BLOCK] * 2, [VMEM]...  20 us
    pallas_call x4, Pallas kernels, steps(): call(functools.partial(outer_kernel, signs, last), 'outer', [BLOCK] + ([i...  19.3 us
    all_to_all x1, starting transfers between devices, local(): lax.all_to_all(request, ALL, split_axis=0, concat_axis=0, tiled=True)  15.7 us
    ppermute x24, waiting for transfers between devices, exchange(): arrived.append(lax.ppermute(face, axis, pairs))  14.6 us
    all_to_all x1, waiting for transfers between devices, local(): lax.all_to_all(request, ALL, split_axis=0, concat_axis=0, tiled=True)  12.7 us
    pallas_call x1, Pallas kernels, local(): call(sample_kernel, 'samples', [(owners, slots)], [SMEM, VMEM, VMEM, VMEM...  5.1 us
  transfers between devices with their start and end apart: 25, of which 10 were waited for; matrix products, arithmetic and copies ran while one was open for 0% of the time, Pallas kernels for 13%

profile of v6, /device:TPU:1, one launch (start us, length us, event | category | flops | bytes accessed | tf_op | source)
XLA Modules:
  0.0 149.6 jit_solution(6083260855447865346)
XLA Ops:
  3.0 15.7 %all-to-all-start = ((f32[256,1,128]{2,1,0:T(1,128)}), f32[256,1,128]{2,1,0:T(1,128)S(1)}, u32[]{:S(2)}, u32[]{:S(2)}) async-start(f32[256,1,128]{2,1,0:T(1,128)} %copy.24), calls=%async_computation | async-start | bytes 262144 | tf_op jit(solution)/shard_map/all_to_all | solution.py:405
  18.7 12.7 %all-to-all-done = f32[256,1,128]{2,1,0:T(1,128)S(1)} async-done(((f32[256,1,128]{2,1,0:T(1,128)}), f32[256,1,128]{2,1,0:T(1,128)S(1)}, u32[]{:S(2)}, u32[]{:S(2)}) %all-to-all-start) | async-done | bytes 131104 | tf_op jit(solution)/shard_map/all_to_all | solution.py:405
  32.9 3.0 %collective-permute-start = (f32[384,128]{1,0:T(8,128)S(1)}, f32[384,128]{1,0:T(8,128)S(1)}, u32[]{:S(2)}, u32[]{:S(2)}) collective-permute-start(f32[384,128]{1,0:T(8,128)S(1)} %get-tuple-element.43), channel_id=1, source_target_pairs={{64,128},{128,64},{65,129},{129,65},{66,130},{130,66},{67,131},{13... | collective-permute-start | bytes 589832 | tf_op jit(solution)/shard_map/ppermute | solution.py:309
  38.7 3.9 %collective-permute-done.rxb = f32[384,128]{1,0:T(8,128)S(1)} collective-permute-done((f32[384,128]{1,0:T(8,128)S(1)}, f32[384,128]{1,0:T(8,128)S(1)}, u32[]{:S(2)}, u32[]{:S(2)}) %collective-permute-start) | collective-permute-done | bytes 196640 | tf_op jit(solution)/shard_map/ppermute | solution.py:309
  43.0 5.0 %inner.4 = (f32[2048,128]{1,0:T(8,128)S(1)}, f32[2048,128]{1,0:T(8,128)S(1)}) custom-call(f32[2048,128]{1,0:T(8,128)S(1)} %get-tuple-element.40.v_ref, f32[8,8,128]{2,1,0:T(8,128)S(1)} %copy-done.4, f32[8,8,128]{2,1,0:T(8,128)S(1)} %copy-done.3), custom_call_target="tpu_custom_call" | custom-call | flops 99999997952 | tf_op jit(solution)/shard_map/inner/pallas_call | solution.py:335
  48.1 1.3 collective-permute-done.5.rhb
  49.4 4.6 %outer.4 = (f32[2048,128]{1,0:T(8,128)S(1)}, f32[384,128]{1,0:T(8,128)S(1)}, f32[384,128]{1,0:T(8,128)S(1)}, f32[384,128]{1,0:T(8,128)S(1)}, f32[384,128]{1,0:T(...) custom-call(f32[2048,128]{1,0:T(8,128)S(1)} %get-tuple-element.40.v_ref, ...), custom_call_target="tpu_custom_call" | custom-call | flops 15000000 | bytes 4194304 | tf_op jit(solution)/shard_map/outer/pallas_call | solution.py:338
  54.0 3.1 %collective-permute-start.6 = (f32[384,128]{1,0:T(8,128)S(1)}, f32[384,128]{1,0:T(8,128)S(1)}, u32[]{:S(2)}, u32[]{:S(2)}) collective-permute-start(f32[384,128]{1,0:T(8,128)S(1)} %get-tuple-element.52), channel_id=1, source_target_pairs={{64,128},{128,64},{65,129},{129,65},{66,130},{130,66},{67,131},{13... | collective-permute-start | bytes 589832 | tf_op jit(solution)/shard_map/ppermute | solution.py:309
  57.3 1.4 collective-permute-start.8
  59.4 3.1 %collective-permute-done.6.rxb = f32[384,128]{1,0:T(8,128)S(1)} collective-permute-done((f32[384,128]{1,0:T(8,128)S(1)}, f32[384,128]{1,0:T(8,128)S(1)}, u32[]{:S(2)}, u32[]{:S(2)}) %collective-permute-start.6) | collective-permute-done | bytes 196640 | tf_op jit(solution)/shard_map/ppermute | solution.py:309
  63.9 5.0 %inner.5 = (f32[2048,128]{1,0:T(8,128)S(1)}, f32[2048,128]{1,0:T(8,128)S(1)}) custom-call(f32[2048,128]{1,0:T(8,128)S(1)} %get-tuple-element.49.v_ref, f32[8,8,128]{2,1,0:T(8,128)S(1)} %copy-done.4, f32[8,8,128]{2,1,0:T(8,128)S(1)} %copy-done.3), custom_call_target="tpu_custom_call" | custom-call | flops 99999997952 | tf_op jit(solution)/shard_map/inner/pallas_call | solution.py:335
  69.9 4.6 %outer.5 = (f32[2048,128]{1,0:T(8,128)S(1)}, f32[384,128]{1,0:T(8,128)S(1)}, f32[384,128]{1,0:T(8,128)S(1)}, f32[384,128]{1,0:T(8,128)S(1)}, f32[384,128]{1,0:T(...) custom-call(f32[2048,128]{1,0:T(8,128)S(1)} %get-tuple-element.49.v_ref, ...), custom_call_target="tpu_custom_call" | custom-call | flops 15000000 | bytes 4194304 | tf_op jit(solution)/shard_map/outer/pallas_call | solution.py:338
  74.5 5.1 %collective-permute-start.12 = (f32[384,128]{1,0:T(8,128)S(1)}, f32[384,128]{1,0:T(8,128)S(1)}, u32[]{:S(2)}, u32[]{:S(2)}) collective-permute-start(f32[384,128]{1,0:T(8,128)S(1)} %get-tuple-element.61), channel_id=1, source_target_pairs={{64,128},{128,64},{65,129},{129,65},{66,130},{130,66},{67,131},{13... | collective-permute-start | bytes 589832 | tf_op jit(solution)/shard_map/ppermute | solution.py:309
  79.7 2.3 %collective-permute-start.14 = (f32[384,128]{1,0:T(8,128)S(1)}, f32[384,128]{1,0:T(8,128)S(1)}, u32[]{:S(2)}, u32[]{:S(2)}) collective-permute-start(f32[384,128]{1,0:T(8,128)S(1)} %get-tuple-element.63), channel_id=1, source_target_pairs={{0,8},{8,0},{16,24},{24,16},{32,40},{40,32},{48,56},{56,48},{1,9},... | collective-permute-start | bytes 589832 | tf_op jit(solution)/shard_map/ppermute | solution.py:309
  83.9 5.0 %inner.6 = (f32[2048,128]{1,0:T(8,128)S(1)}, f32[2048,128]{1,0:T(8,128)S(1)}) custom-call(f32[2048,128]{1,0:T(8,128)S(1)} %get-tuple-element.58.v_ref, f32[8,8,128]{2,1,0:T(8,128)S(1)} %copy-done.4, f32[8,8,128]{2,1,0:T(8,128)S(1)} %copy-done.3), custom_call_target="tpu_custom_call" | custom-call | flops 99999997952 | tf_op jit(solution)/shard_map/inner/pallas_call | solution.py:335
  89.0 1.7 %collective-permute-done.14.rya = f32[384,128]{1,0:T(8,128)S(1)} collective-permute-done((f32[384,128]{1,0:T(8,128)S(1)}, f32[384,128]{1,0:T(8,128)S(1)}, u32[]{:S(2)}, u32[]{:S(2)}) %collective-permute-start.14) | collective-permute-done | bytes 196640 | tf_op jit(solution)/shard_map/ppermute | solution.py:309
  91.3 4.6 %outer.6 = (f32[2048,128]{1,0:T(8,128)S(1)}, f32[384,128]{1,0:T(8,128)S(1)}, f32[384,128]{1,0:T(8,128)S(1)}, f32[384,128]{1,0:T(8,128)S(1)}, f32[384,128]{1,0:T(...) custom-call(f32[2048,128]{1,0:T(8,128)S(1)} %get-tuple-element.58.v_ref, ...), custom_call_target="tpu_custom_call" | custom-call | flops 15000000 | bytes 4194304 | tf_op jit(solution)/shard_map/outer/pallas_call | solution.py:338
  95.9 6.5 %collective-permute-start.18 = (f32[384,128]{1,0:T(8,128)S(1)}, f32[384,128]{1,0:T(8,128)S(1)}, u32[]{:S(2)}, u32[]{:S(2)}) collective-permute-start(f32[384,128]{1,0:T(8,128)S(1)} %get-tuple-element.70), channel_id=1, source_target_pairs={{64,128},{128,64},{65,129},{129,65},{66,130},{130,66},{67,131},{13... | collective-permute-start | bytes 589832 | tf_op jit(solution)/shard_map/ppermute | solution.py:309
  102.7 2.4 %collective-permute-start.20 = (f32[384,128]{1,0:T(8,128)S(1)}, f32[384,128]{1,0:T(8,128)S(1)}, u32[]{:S(2)}, u32[]{:S(2)}) collective-permute-start(f32[384,128]{1,0:T(8,128)S(1)} %get-tuple-element.72), channel_id=1, source_target_pairs={{0,8},{8,0},{16,24},{24,16},{32,40},{40,32},{48,56},{56,48},{1,9},... | collective-permute-start | bytes 589832 | tf_op jit(solution)/shard_map/ppermute | solution.py:309
  106.3 5.0 %inner.7 = (f32[2048,128]{1,0:T(8,128)S(1)}, f32[2048,128]{1,0:T(8,128)S(1)}) custom-call(f32[2048,128]{1,0:T(8,128)S(1)} %get-tuple-element.67.v_ref, f32[8,8,128]{2,1,0:T(8,128)S(1)} %copy-done.4, f32[8,8,128]{2,1,0:T(8,128)S(1)} %copy-done.3), custom_call_target="tpu_custom_call" | custom-call | flops 99999997952 | tf_op jit(solution)/shard_map/inner/pallas_call | solution.py:335
  111.3 2.1 %collective-permute-done.20.rya = f32[384,128]{1,0:T(8,128)S(1)} collective-permute-done((f32[384,128]{1,0:T(8,128)S(1)}, f32[384,128]{1,0:T(8,128)S(1)}, u32[]{:S(2)}, u32[]{:S(2)}) %collective-permute-start.20) | collective-permute-done | bytes 196640 | tf_op jit(solution)/shard_map/ppermute | solution.py:309
  114.0 5.4 %outer.7 = (f32[2048,128]{1,0:T(8,128)S(1)}, f32[16,16,1024]{2,1,0:T(8,128)}) custom-call(f32[2048,128]{1,0:T(8,128)S(1)} %get-tuple-element.67.v_ref, f32[2048,128]{1,0:T(8,128)S(1)} %get-tuple-element.68.h_in, f32[2048,128]{1,0:T(8,128)S(1)} %get-tuple-element.69.turned_ref, f32[8,8,128]{2,1,0:T(8,128)S(1)} %copy-done.4, f32[8,8,128]{2,1,0:T(8,128)S(1)} %copy-done.3, ...), custom_call_target="tpu_custom_call" | custom-call | flops 15000000 | bytes 4194304 | tf_op jit(solution)/shard_map/outer/pallas_call | solution.py:338
  119.5 5.1 %samples.1 = f32[256,4]{1,0:T(8,128)S(1)} custom-call(s32[1024]{0:T(1024)S(1)} %add_select_fusion.1.rows_ref, f32[2048,128]{1,0:T(8,128)S(1)} %get-tuple-element.77.v_ref, s32[1024,128]{1,0:T(8,128)S(1)} %copy-done.1, f32[256,128]{1,0:T(8,128)S(1)} %bitcast.24), custom_call_target="tpu_custom_call" | custom-call | bytes 4194304 | tf_op jit(solution)/shard_map/samples/pallas_call | solution.py:412
  124.6 23.7 %all_to_all.23 = f32[256,1,4]{2,1,0:T(1,128)S(1)} all-to-all(f32[256,1,4]{2,1,0:T(1,128)S(1)} %bitcast.25), channel_id=1, replica_groups=mesh['gx'=4,'gy'=8,'ha'=8] {'gx','gy','ha'}, dimensions={0} | all-to-all | bytes 8192 | tf_op jit(solution)/shard_map/all_to_all | solution.py:419
  (64 shorter events, 16.2 us)
Async XLA Ops:
  3.0 28.4 %all-to-all-start = ((f32[256,1,128]{2,1,0:T(1,128)}), f32[256,1,128]{2,1,0:T(1,128)S(1)}, u32[]{:S(2)}, u32[]{:S(2)}) async-start(f32[256,1,128]{2,1,0:T(1,128)} %copy.24), calls=%async_computation | async-start | bytes 262144 | tf_op jit(solution)/shard_map/all_to_all | solution.py:405
  32.9 9.8 %collective-permute-start = (f32[384,128]{1,0:T(8,128)S(1)}, f32[384,128]{1,0:T(8,128)S(1)}, u32[]{:S(2)}, u32[]{:S(2)}) collective-permute-start(f32[384,128]{1,0:T(8,128)S(1)} %get-tuple-element.43), channel_id=1, source_target_pairs={{64,128},{128,64},{65,129},{129,65},{66,130},{130,66},{67,131},{13... | collective-permute-start | bytes 589832 | tf_op jit(solution)/shard_map/ppermute | solution.py:309
  35.9 12.1 %collective-permute-start.1 = (f32[384,128]{1,0:T(8,128)S(1)}, f32[384,128]{1,0:T(8,128)S(1)}, u32[]{:S(2)}, u32[]{:S(2)}) collective-permute-start(f32[384,128]{1,0:T(8,128)S(1)} %get-tuple-element.44), channel_id=1, source_target_pairs={{0,64},{64,0},{128,192},{192,128},{1,65},{65,1},{129,193},{193,129... | collective-permute-start | bytes 589832 | tf_op jit(solution)/shard_map/ppermute | solution.py:309
  36.0 12.0 %collective-permute-start.2 = (f32[384,128]{1,0:T(8,128)S(1)}, f32[384,128]{1,0:T(8,128)S(1)}, u32[]{:S(2)}, u32[]{:S(2)}) collective-permute-start(f32[384,128]{1,0:T(8,128)S(1)} %get-tuple-element.45), channel_id=1, source_target_pairs={{0,8},{8,0},{16,24},{24,16},{32,40},{40,32},{48,56},{56,48},{1,9},... | collective-permute-start | bytes 589832 | tf_op jit(solution)/shard_map/ppermute | solution.py:309
  37.1 11.0 %collective-permute-start.3 = (f32[384,128]{1,0:T(8,128)S(1)}, f32[384,128]{1,0:T(8,128)S(1)}, u32[]{:S(2)}, u32[]{:S(2)}) collective-permute-start(f32[384,128]{1,0:T(8,128)S(1)} %get-tuple-element.46), channel_id=1, source_target_pairs={{8,16},{16,8},{24,32},{32,24},{40,48},{48,40},{9,17},{17,9},{25,33... | collective-permute-start | bytes 589832 | tf_op jit(solution)/shard_map/ppermute | solution.py:309
  37.8 10.3 %collective-permute-start.4 = (f32[512,128]{1,0:T(8,128)S(1)}, f32[512,128]{1,0:T(8,128)S(1)}, u32[]{:S(2)}, u32[]{:S(2)}) collective-permute-start(f32[512,128]{1,0:T(8,128)S(1)} %get-tuple-element.47), channel_id=1, source_target_pairs={{0,1},{1,0},{2,3},{3,2},{4,5},{5,4},{6,7},{7,6},{8,9},{9,8},{10,11... | collective-permute-start | bytes 786440 | tf_op jit(solution)/shard_map/ppermute | solution.py:309
  54.0 8.5 %collective-permute-start.6 = (f32[384,128]{1,0:T(8,128)S(1)}, f32[384,128]{1,0:T(8,128)S(1)}, u32[]{:S(2)}, u32[]{:S(2)}) collective-permute-start(f32[384,128]{1,0:T(8,128)S(1)} %get-tuple-element.52), channel_id=1, source_target_pairs={{64,128},{128,64},{65,129},{129,65},{66,130},{130,66},{67,131},{13... | collective-permute-start | bytes 589832 | tf_op jit(solution)/shard_map/ppermute | solution.py:309
  57.2 11.7 %collective-permute-start.7 = (f32[384,128]{1,0:T(8,128)S(1)}, f32[384,128]{1,0:T(8,128)S(1)}, u32[]{:S(2)}, u32[]{:S(2)}) collective-permute-start(f32[384,128]{1,0:T(8,128)S(1)} %get-tuple-element.53), channel_id=1, source_target_pairs={{0,64},{64,0},{128,192},{192,128},{1,65},{65,1},{129,193},{193,129... | collective-permute-start | bytes 589832 | tf_op jit(solution)/shard_map/ppermute | solution.py:309
  57.3 11.6 %collective-permute-start.8 = (f32[384,128]{1,0:T(8,128)S(1)}, f32[384,128]{1,0:T(8,128)S(1)}, u32[]{:S(2)}, u32[]{:S(2)}) collective-permute-start(f32[384,128]{1,0:T(8,128)S(1)} %get-tuple-element.54), channel_id=1, source_target_pairs={{0,8},{8,0},{16,24},{24,16},{32,40},{40,32},{48,56},{56,48},{1,9},... | collective-permute-start | bytes 589832 | tf_op jit(solution)/shard_map/ppermute | solution.py:309
  58.7 10.2 %collective-permute-start.9 = (f32[384,128]{1,0:T(8,128)S(1)}, f32[384,128]{1,0:T(8,128)S(1)}, u32[]{:S(2)}, u32[]{:S(2)}) collective-permute-start(f32[384,128]{1,0:T(8,128)S(1)} %get-tuple-element.55), channel_id=1, source_target_pairs={{8,16},{16,8},{24,32},{32,24},{40,48},{48,40},{9,17},{17,9},{25,33... | collective-permute-start | bytes 589832 | tf_op jit(solution)/shard_map/ppermute | solution.py:309
  59.3 9.6 %collective-permute-start.10 = (f32[512,128]{1,0:T(8,128)S(1)}, f32[512,128]{1,0:T(8,128)S(1)}, u32[]{:S(2)}, u32[]{:S(2)}) collective-permute-start(f32[512,128]{1,0:T(8,128)S(1)} %get-tuple-element.56), channel_id=1, source_target_pairs={{0,1},{1,0},{2,3},{3,2},{4,5},{5,4},{6,7},{7,6},{8,9},{9,8},{10,11... | collective-permute-start | bytes 786440 | tf_op jit(solution)/shard_map/ppermute | solution.py:309
  62.5 7.4 %collective-permute-start.11 = (f32[512,128]{1,0:T(8,128)S(1)}, f32[512,128]{1,0:T(8,128)S(1)}, u32[]{:S(2)}, u32[]{:S(2)}) collective-permute-start(f32[512,128]{1,0:T(8,128)S(1)} %get-tuple-element.57), channel_id=1, source_target_pairs={{1,2},{2,1},{3,4},{4,3},{5,6},{6,5},{7,0},{0,7},{9,10},{10,9},{11,... | collective-permute-start | bytes 786440 | tf_op jit(solution)/shard_map/ppermute | solution.py:309
  74.5 8.5 %collective-permute-start.12 = (f32[384,128]{1,0:T(8,128)S(1)}, f32[384,128]{1,0:T(8,128)S(1)}, u32[]{:S(2)}, u32[]{:S(2)}) collective-permute-start(f32[384,128]{1,0:T(8,128)S(1)} %get-tuple-element.61), channel_id=1, source_target_pairs={{64,128},{128,64},{65,129},{129,65},{66,130},{130,66},{67,131},{13... | collective-permute-start | bytes 589832 | tf_op jit(solution)/shard_map/ppermute | solution.py:309
  79.6 9.3 %collective-permute-start.13 = (f32[384,128]{1,0:T(8,128)S(1)}, f32[384,128]{1,0:T(8,128)S(1)}, u32[]{:S(2)}, u32[]{:S(2)}) collective-permute-start(f32[384,128]{1,0:T(8,128)S(1)} %get-tuple-element.62), channel_id=1, source_target_pairs={{0,64},{64,0},{128,192},{192,128},{1,65},{65,1},{129,193},{193,129... | collective-permute-start | bytes 589832 | tf_op jit(solution)/shard_map/ppermute | solution.py:309
  79.7 11.0 %collective-permute-start.14 = (f32[384,128]{1,0:T(8,128)S(1)}, f32[384,128]{1,0:T(8,128)S(1)}, u32[]{:S(2)}, u32[]{:S(2)}) collective-permute-start(f32[384,128]{1,0:T(8,128)S(1)} %get-tuple-element.63), channel_id=1, source_target_pairs={{0,8},{8,0},{16,24},{24,16},{32,40},{40,32},{48,56},{56,48},{1,9},... | collective-permute-start | bytes 589832 | tf_op jit(solution)/shard_map/ppermute | solution.py:309
  82.0 8.7 %collective-permute-start.15 = (f32[384,128]{1,0:T(8,128)S(1)}, f32[384,128]{1,0:T(8,128)S(1)}, u32[]{:S(2)}, u32[]{:S(2)}) collective-permute-start(f32[384,128]{1,0:T(8,128)S(1)} %get-tuple-element.64), channel_id=1, source_target_pairs={{8,16},{16,8},{24,32},{32,24},{40,48},{48,40},{9,17},{17,9},{25,33... | collective-permute-start | bytes 589832 | tf_op jit(solution)/shard_map/ppermute | solution.py:309
  82.6 8.0 %collective-permute-start.16 = (f32[512,128]{1,0:T(8,128)S(1)}, f32[512,128]{1,0:T(8,128)S(1)}, u32[]{:S(2)}, u32[]{:S(2)}) collective-permute-start(f32[512,128]{1,0:T(8,128)S(1)} %get-tuple-element.65), channel_id=1, source_target_pairs={{0,1},{1,0},{2,3},{3,2},{4,5},{5,4},{6,7},{7,6},{8,9},{9,8},{10,11... | collective-permute-start | bytes 786440 | tf_op jit(solution)/shard_map/ppermute | solution.py:309
  83.0 8.2 %collective-permute-start.17 = (f32[512,128]{1,0:T(8,128)S(1)}, f32[512,128]{1,0:T(8,128)S(1)}, u32[]{:S(2)}, u32[]{:S(2)}) collective-permute-start(f32[512,128]{1,0:T(8,128)S(1)} %get-tuple-element.66), channel_id=1, source_target_pairs={{1,2},{2,1},{3,4},{4,3},{5,6},{6,5},{7,0},{0,7},{9,10},{10,9},{11,... | collective-permute-start | bytes 786440 | tf_op jit(solution)/shard_map/ppermute | solution.py:309
  95.9 10.1 %collective-permute-start.18 = (f32[384,128]{1,0:T(8,128)S(1)}, f32[384,128]{1,0:T(8,128)S(1)}, u32[]{:S(2)}, u32[]{:S(2)}) collective-permute-start(f32[384,128]{1,0:T(8,128)S(1)} %get-tuple-element.70), channel_id=1, source_target_pairs={{64,128},{128,64},{65,129},{129,65},{66,130},{130,66},{67,131},{13... | collective-permute-start | bytes 589832 | tf_op jit(solution)/shard_map/ppermute | solution.py:309
  102.4 8.9 %collective-permute-start.19 = (f32[384,128]{1,0:T(8,128)S(1)}, f32[384,128]{1,0:T(8,128)S(1)}, u32[]{:S(2)}, u32[]{:S(2)}) collective-permute-start(f32[384,128]{1,0:T(8,128)S(1)} %get-tuple-element.71), channel_id=1, source_target_pairs={{0,64},{64,0},{128,192},{192,128},{1,65},{65,1},{129,193},{193,129... | collective-permute-start | bytes 589832 | tf_op jit(solution)/shard_map/ppermute | solution.py:309
  102.7 10.7 %collective-permute-start.20 = (f32[384,128]{1,0:T(8,128)S(1)}, f32[384,128]{1,0:T(8,128)S(1)}, u32[]{:S(2)}, u32[]{:S(2)}) collective-permute-start(f32[384,128]{1,0:T(8,128)S(1)} %get-tuple-element.72), channel_id=1, source_target_pairs={{0,8},{8,0},{16,24},{24,16},{32,40},{40,32},{48,56},{56,48},{1,9},... | collective-permute-start | bytes 589832 | tf_op jit(solution)/shard_map/ppermute | solution.py:309
  105.1 8.3 %collective-permute-start.21 = (f32[384,128]{1,0:T(8,128)S(1)}, f32[384,128]{1,0:T(8,128)S(1)}, u32[]{:S(2)}, u32[]{:S(2)}) collective-permute-start(f32[384,128]{1,0:T(8,128)S(1)} %get-tuple-element.73), channel_id=1, source_target_pairs={{8,16},{16,8},{24,32},{32,24},{40,48},{48,40},{9,17},{17,9},{25,33... | collective-permute-start | bytes 589832 | tf_op jit(solution)/shard_map/ppermute | solution.py:309
  105.8 7.6 %collective-permute-start.22 = (f32[512,128]{1,0:T(8,128)S(1)}, f32[512,128]{1,0:T(8,128)S(1)}, u32[]{:S(2)}, u32[]{:S(2)}) collective-permute-start(f32[512,128]{1,0:T(8,128)S(1)} %get-tuple-element.74), channel_id=1, source_target_pairs={{0,1},{1,0},{2,3},{3,2},{4,5},{5,4},{6,7},{7,6},{8,9},{9,8},{10,11... | collective-permute-start | bytes 786440 | tf_op jit(solution)/shard_map/ppermute | solution.py:309
  106.0 8.0 %collective-permute-start.23 = (f32[512,128]{1,0:T(8,128)S(1)}, f32[512,128]{1,0:T(8,128)S(1)}, u32[]{:S(2)}, u32[]{:S(2)}) collective-permute-start(f32[512,128]{1,0:T(8,128)S(1)} %get-tuple-element.75), channel_id=1, source_target_pairs={{1,2},{2,1},{3,4},{4,3},{5,6},{6,5},{7,0},{0,7},{9,10},{10,9},{11,... | collective-permute-start | bytes 786440 | tf_op jit(solution)/shard_map/ppermute | solution.py:309
  (7 other events, 65.4 us)

commit v7 on v6

--- a/solution.py
+++ b/solution.py
@@ -207,7 +207,7 @@
 
 
 def outer_kernel(
-    signs, last, v_ref, h_in, turned_ref, adx_ref, ady_ref, rxb, rxa, rya, ryb, rha, rhb, *rest
+    signs, last, v_ref, h_in, turned_ref, adx_ref, ady_ref, rxa, rxb, ryb, rya, rha, rhb, *rest
 ):
     out_ref, others = rest[0], rest[1:-5]
     xs, ys, hs, hs_turned, h_ref = rest[-5:]
@@ -342,7 +342,7 @@
             [VMEM] * 11,
             scratch=[(6 * XROW, 128), (6 * XROW, 128), (1024, 128), (1024, 128), BLOCK],
             flops=15_000_000,
-        )(value, part, turned, adx, ady, *(arrived[n] for n in (1, 0, 2, 3, 4, 5)))
+        )(value, part, turned, adx, ady, *(arrived[n] for n in (0, 1, 3, 2, 4, 5)))
     return value, faces[0]
 
 

time: 150 us -> 143 us (0.953)
  waiting for transfers between devices: 27.3 us -> 20.3 us
  starting transfers between devices: 48.1 us -> 51.3 us
  blocking collectives: 23.7 us -> 21 us
    ppermute x24, waiting for transfers between devices: 14.6 us -> 7.52 us  [exchange(): arrived.append(lax.ppermute(face, axis, pairs))]
    ppermute x24, starting transfers between devices: 32.4 us -> 35.6 us  [exchange(): arrived.append(lax.ppermute(face, axis, pairs))]
    all_to_all x1, blocking collectives: 23.7 us -> 21 us  [local(): sampled = lax.all_to_all(sums, ALL, split_axis=0, concat_axis=0, tiled=True)]
  transfers between devices with their start and end apart: 25 -> 25, of which waited for: 10 -> 9; matrix products, arithmetic and copies ran while one was open for 0% -> 0% of each run, Pallas kernels for 13% -> 14%
where the time goes in v7:
time: 143 us
  starting transfers between devices  51.3 us (36%)
  Pallas kernels  44.8 us (31%)
  blocking collectives  21 us (15%)
  waiting for transfers between devices  20.3 us (14%)
  local copies, waits for them, and re-layouts  2.91 us (2%)
  other arithmetic  1.74 us (1%)
    ppermute x24, starting transfers between devices, exchange(): arrived.append(lax.ppermute(face, axis, pairs))  35.6 us
    all_to_all x1, blocking collectives, local(): sampled = lax.all_to_all(sums, ALL, split_axis=0, concat_axis=0, tiled=True)  21 us
    pallas_call x4, Pallas kernels, steps(): call(functools.partial(inner_kernel, signs), 'inner', [BLOCK] * 2, [VMEM]...  20 us
    pallas_call x4, Pallas kernels, steps(): call(functools.partial(outer_kernel, signs, last), 'outer', [BLOCK] + ([i...  19.3 us
    all_to_all x1, starting transfers between devices, local(): lax.all_to_all(request, ALL, split_axis=0, concat_axis=0, tiled=True)  15.7 us
    all_to_all x1, waiting for transfers between devices, local(): lax.all_to_all(request, ALL, split_axis=0, concat_axis=0, tiled=True)  12.7 us
    ppermute x24, waiting for transfers between devices, exchange(): arrived.append(lax.ppermute(face, axis, pairs))  7.52 us
    pallas_call x1, Pallas kernels, local(): call(sample_kernel, 'samples', [(owners, slots)], [SMEM, VMEM, VMEM, VMEM...  5.1 us
  transfers between devices with their start and end apart: 25, of which 9 were waited for; matrix products, arithmetic and copies ran while one was open for 0% of the time, Pallas kernels for 14%

profile of v7, /device:TPU:1, one launch (start us, length us, event | category | flops | bytes accessed | tf_op | source)
XLA Modules:
  0.0 142.9 jit_solution(10453210983061290492)
XLA Ops:
  1.3 0.9 reshape.33
  3.0 15.7 %all-to-all-start = ((f32[256,1,128]{2,1,0:T(1,128)}), f32[256,1,128]{2,1,0:T(1,128)S(1)}, u32[]{:S(2)}, u32[]{:S(2)}) async-start(f32[256,1,128]{2,1,0:T(1,128)} %copy.24), calls=%async_computation | async-start | bytes 262144 | tf_op jit(solution)/shard_map/all_to_all | solution.py:405
  18.7 12.7 %all-to-all-done = f32[256,1,128]{2,1,0:T(1,128)S(1)} async-done(((f32[256,1,128]{2,1,0:T(1,128)}), f32[256,1,128]{2,1,0:T(1,128)S(1)}, u32[]{:S(2)}, u32[]{:S(2)}) %all-to-all-start) | async-done | bytes 131104 | tf_op jit(solution)/shard_map/all_to_all | solution.py:405
  33.7 2.6 %collective-permute-start.1 = (f32[384,128]{1,0:T(8,128)S(1)}, f32[384,128]{1,0:T(8,128)S(1)}, u32[]{:S(2)}, u32[]{:S(2)}) collective-permute-start(f32[384,128]{1,0:T(8,128)S(1)} %get-tuple-element.44), channel_id=1, source_target_pairs={{64,128},{128,64},{65,129},{129,65},{66,130},{130,66},{67,131},{13... | collective-permute-start | bytes 589832 | tf_op jit(solution)/shard_map/ppermute | solution.py:309
  37.0 2.9 %collective-permute-start.3 = (f32[384,128]{1,0:T(8,128)S(1)}, f32[384,128]{1,0:T(8,128)S(1)}, u32[]{:S(2)}, u32[]{:S(2)}) collective-permute-start(f32[384,128]{1,0:T(8,128)S(1)} %get-tuple-element.46), channel_id=1, source_target_pairs={{0,8},{8,0},{16,24},{24,16},{32,40},{40,32},{48,56},{56,48},{1,9},... | collective-permute-start | bytes 589832 | tf_op jit(solution)/shard_map/ppermute | solution.py:309
  40.6 5.0 %inner.4 = (f32[2048,128]{1,0:T(8,128)S(1)}, f32[2048,128]{1,0:T(8,128)S(1)}) custom-call(f32[2048,128]{1,0:T(8,128)S(1)} %get-tuple-element.40.v_ref, f32[8,8,128]{2,1,0:T(8,128)S(1)} %copy-done.4, f32[8,8,128]{2,1,0:T(8,128)S(1)} %copy-done.3), custom_call_target="tpu_custom_call" | custom-call | flops 99999997952 | tf_op jit(solution)/shard_map/inner/pallas_call | solution.py:335
  45.7 2.7 %collective-permute-done.3.rya = f32[384,128]{1,0:T(8,128)S(1)} collective-permute-done((f32[384,128]{1,0:T(8,128)S(1)}, f32[384,128]{1,0:T(8,128)S(1)}, u32[]{:S(2)}, u32[]{:S(2)}) %collective-permute-start.3) | collective-permute-done | bytes 196640 | tf_op jit(solution)/shard_map/ppermute | solution.py:309
  48.5 4.6 %outer.4 = (f32[2048,128]{1,0:T(8,128)S(1)}, f32[384,128]{1,0:T(8,128)S(1)}, f32[384,128]{1,0:T(8,128)S(1)}, f32[384,128]{1,0:T(8,128)S(1)}, f32[384,128]{1,0:T(...) custom-call(f32[2048,128]{1,0:T(8,128)S(1)} %get-tuple-element.40.v_ref, ...), custom_call_target="tpu_custom_call" | custom-call | flops 15000000 | bytes 4194304 | tf_op jit(solution)/shard_map/outer/pallas_call | solution.py:338
  53.2 4.3 %collective-permute-start.7 = (f32[384,128]{1,0:T(8,128)S(1)}, f32[384,128]{1,0:T(8,128)S(1)}, u32[]{:S(2)}, u32[]{:S(2)}) collective-permute-start(f32[384,128]{1,0:T(8,128)S(1)} %get-tuple-element.53), channel_id=1, source_target_pairs={{64,128},{128,64},{65,129},{129,65},{66,130},{130,66},{67,131},{13... | collective-permute-start | bytes 589832 | tf_op jit(solution)/shard_map/ppermute | solution.py:309
  58.2 3.7 %collective-permute-start.9 = (f32[384,128]{1,0:T(8,128)S(1)}, f32[384,128]{1,0:T(8,128)S(1)}, u32[]{:S(2)}, u32[]{:S(2)}) collective-permute-start(f32[384,128]{1,0:T(8,128)S(1)} %get-tuple-element.55), channel_id=1, source_target_pairs={{0,8},{8,0},{16,24},{24,16},{32,40},{40,32},{48,56},{56,48},{1,9},... | collective-permute-start | bytes 589832 | tf_op jit(solution)/shard_map/ppermute | solution.py:309
  62.4 5.0 %inner.5 = (f32[2048,128]{1,0:T(8,128)S(1)}, f32[2048,128]{1,0:T(8,128)S(1)}) custom-call(f32[2048,128]{1,0:T(8,128)S(1)} %get-tuple-element.49.v_ref, f32[8,8,128]{2,1,0:T(8,128)S(1)} %copy-done.4, f32[8,8,128]{2,1,0:T(8,128)S(1)} %copy-done.3), custom_call_target="tpu_custom_call" | custom-call | flops 99999997952 | tf_op jit(solution)/shard_map/inner/pallas_call | solution.py:335
  68.8 4.6 %outer.5 = (f32[2048,128]{1,0:T(8,128)S(1)}, f32[384,128]{1,0:T(8,128)S(1)}, f32[384,128]{1,0:T(8,128)S(1)}, f32[384,128]{1,0:T(8,128)S(1)}, f32[384,128]{1,0:T(...) custom-call(f32[2048,128]{1,0:T(8,128)S(1)} %get-tuple-element.49.v_ref, ...), custom_call_target="tpu_custom_call" | custom-call | flops 15000000 | bytes 4194304 | tf_op jit(solution)/shard_map/outer/pallas_call | solution.py:338
  73.5 4.3 %collective-permute-start.13 = (f32[384,128]{1,0:T(8,128)S(1)}, f32[384,128]{1,0:T(8,128)S(1)}, u32[]{:S(2)}, u32[]{:S(2)}) collective-permute-start(f32[384,128]{1,0:T(8,128)S(1)} %get-tuple-element.62), channel_id=1, source_target_pairs={{64,128},{128,64},{65,129},{129,65},{66,130},{130,66},{67,131},{13... | collective-permute-start | bytes 589832 | tf_op jit(solution)/shard_map/ppermute | solution.py:309
  78.5 4.6 %collective-permute-start.15 = (f32[384,128]{1,0:T(8,128)S(1)}, f32[384,128]{1,0:T(8,128)S(1)}, u32[]{:S(2)}, u32[]{:S(2)}) collective-permute-start(f32[384,128]{1,0:T(8,128)S(1)} %get-tuple-element.64), channel_id=1, source_target_pairs={{0,8},{8,0},{16,24},{24,16},{32,40},{40,32},{48,56},{56,48},{1,9},... | collective-permute-start | bytes 589832 | tf_op jit(solution)/shard_map/ppermute | solution.py:309
  83.2 5.0 %inner.6 = (f32[2048,128]{1,0:T(8,128)S(1)}, f32[2048,128]{1,0:T(8,128)S(1)}) custom-call(f32[2048,128]{1,0:T(8,128)S(1)} %get-tuple-element.58.v_ref, f32[8,8,128]{2,1,0:T(8,128)S(1)} %copy-done.4, f32[8,8,128]{2,1,0:T(8,128)S(1)} %copy-done.3), custom_call_target="tpu_custom_call" | custom-call | flops 99999997952 | tf_op jit(solution)/shard_map/inner/pallas_call | solution.py:335
  88.2 1.8 %collective-permute-done.15.rya = f32[384,128]{1,0:T(8,128)S(1)} collective-permute-done((f32[384,128]{1,0:T(8,128)S(1)}, f32[384,128]{1,0:T(8,128)S(1)}, u32[]{:S(2)}, u32[]{:S(2)}) %collective-permute-start.15) | collective-permute-done | bytes 196640 | tf_op jit(solution)/shard_map/ppermute | solution.py:309
  90.6 4.6 %outer.6 = (f32[2048,128]{1,0:T(8,128)S(1)}, f32[384,128]{1,0:T(8,128)S(1)}, f32[384,128]{1,0:T(8,128)S(1)}, f32[384,128]{1,0:T(8,128)S(1)}, f32[384,128]{1,0:T(...) custom-call(f32[2048,128]{1,0:T(8,128)S(1)} %get-tuple-element.58.v_ref, ...), custom_call_target="tpu_custom_call" | custom-call | flops 15000000 | bytes 4194304 | tf_op jit(solution)/shard_map/outer/pallas_call | solution.py:338
  95.5 3.8 %collective-permute-start.19 = (f32[384,128]{1,0:T(8,128)S(1)}, f32[384,128]{1,0:T(8,128)S(1)}, u32[]{:S(2)}, u32[]{:S(2)}) collective-permute-start(f32[384,128]{1,0:T(8,128)S(1)} %get-tuple-element.71), channel_id=1, source_target_pairs={{64,128},{128,64},{65,129},{129,65},{66,130},{130,66},{67,131},{13... | collective-permute-start | bytes 589832 | tf_op jit(solution)/shard_map/ppermute | solution.py:309
  100.0 3.7 %collective-permute-start.21 = (f32[384,128]{1,0:T(8,128)S(1)}, f32[384,128]{1,0:T(8,128)S(1)}, u32[]{:S(2)}, u32[]{:S(2)}) collective-permute-start(f32[384,128]{1,0:T(8,128)S(1)} %get-tuple-element.73), channel_id=1, source_target_pairs={{0,8},{8,0},{16,24},{24,16},{32,40},{40,32},{48,56},{56,48},{1,9},... | collective-permute-start | bytes 589832 | tf_op jit(solution)/shard_map/ppermute | solution.py:309
  104.2 5.0 %inner.7 = (f32[2048,128]{1,0:T(8,128)S(1)}, f32[2048,128]{1,0:T(8,128)S(1)}) custom-call(f32[2048,128]{1,0:T(8,128)S(1)} %get-tuple-element.67.v_ref, f32[8,8,128]{2,1,0:T(8,128)S(1)} %copy-done.4, f32[8,8,128]{2,1,0:T(8,128)S(1)} %copy-done.3), custom_call_target="tpu_custom_call" | custom-call | flops 99999997952 | tf_op jit(solution)/shard_map/inner/pallas_call | solution.py:335
  109.2 0.9 collective-permute-done.21.rya
  110.1 5.4 %outer.7 = (f32[2048,128]{1,0:T(8,128)S(1)}, f32[16,16,1024]{2,1,0:T(8,128)}) custom-call(f32[2048,128]{1,0:T(8,128)S(1)} %get-tuple-element.67.v_ref, f32[2048,128]{1,0:T(8,128)S(1)} %get-tuple-element.68.h_in, f32[2048,128]{1,0:T(8,128)S(1)} %get-tuple-element.69.turned_ref, f32[8,8,128]{2,1,0:T(8,128)S(1)} %copy-done.4, f32[8,8,128]{2,1,0:T(8,128)S(1)} %copy-done.3, ...), custom_call_target="tpu_custom_call" | custom-call | flops 15000000 | bytes 4194304 | tf_op jit(solution)/shard_map/outer/pallas_call | solution.py:338
  115.6 5.1 %samples.1 = f32[256,4]{1,0:T(8,128)S(1)} custom-call(s32[1024]{0:T(1024)S(1)} %add_select_fusion.1.rows_ref, f32[2048,128]{1,0:T(8,128)S(1)} %get-tuple-element.77.v_ref, s32[1024,128]{1,0:T(8,128)S(1)} %copy-done.1, f32[256,128]{1,0:T(8,128)S(1)} %bitcast.24), custom_call_target="tpu_custom_call" | custom-call | bytes 4194304 | tf_op jit(solution)/shard_map/samples/pallas_call | solution.py:412
  120.7 21.0 %all_to_all.23 = f32[256,1,4]{2,1,0:T(1,128)S(1)} all-to-all(f32[256,1,4]{2,1,0:T(1,128)S(1)} %bitcast.25), channel_id=1, replica_groups=mesh['gx'=4,'gy'=8,'ha'=8] {'gx','gy','ha'}, dimensions={0} | all-to-all | bytes 8192 | tf_op jit(solution)/shard_map/all_to_all | solution.py:419
  (64 shorter events, 12.1 us)
Async XLA Ops:
  3.0 28.4 %all-to-all-start = ((f32[256,1,128]{2,1,0:T(1,128)}), f32[256,1,128]{2,1,0:T(1,128)S(1)}, u32[]{:S(2)}, u32[]{:S(2)}) async-start(f32[256,1,128]{2,1,0:T(1,128)} %copy.24), calls=%async_computation | async-start | bytes 262144 | tf_op jit(solution)/shard_map/all_to_all | solution.py:405
  32.9 7.7 %collective-permute-start = (f32[384,128]{1,0:T(8,128)S(1)}, f32[384,128]{1,0:T(8,128)S(1)}, u32[]{:S(2)}, u32[]{:S(2)}) collective-permute-start(f32[384,128]{1,0:T(8,128)S(1)} %get-tuple-element.43), channel_id=1, source_target_pairs={{0,64},{64,0},{128,192},{192,128},{1,65},{65,1},{129,193},{193,129... | collective-permute-start | bytes 589832 | tf_op jit(solution)/shard_map/ppermute | solution.py:309
  33.7 12.0 %collective-permute-start.1 = (f32[384,128]{1,0:T(8,128)S(1)}, f32[384,128]{1,0:T(8,128)S(1)}, u32[]{:S(2)}, u32[]{:S(2)}) collective-permute-start(f32[384,128]{1,0:T(8,128)S(1)} %get-tuple-element.44), channel_id=1, source_target_pairs={{64,128},{128,64},{65,129},{129,65},{66,130},{130,66},{67,131},{13... | collective-permute-start | bytes 589832 | tf_op jit(solution)/shard_map/ppermute | solution.py:309
  36.3 9.4 %collective-permute-start.2 = (f32[384,128]{1,0:T(8,128)S(1)}, f32[384,128]{1,0:T(8,128)S(1)}, u32[]{:S(2)}, u32[]{:S(2)}) collective-permute-start(f32[384,128]{1,0:T(8,128)S(1)} %get-tuple-element.45), channel_id=1, source_target_pairs={{8,16},{16,8},{24,32},{32,24},{40,48},{48,40},{9,17},{17,9},{25,33... | collective-permute-start | bytes 589832 | tf_op jit(solution)/shard_map/ppermute | solution.py:309
  37.0 11.4 %collective-permute-start.3 = (f32[384,128]{1,0:T(8,128)S(1)}, f32[384,128]{1,0:T(8,128)S(1)}, u32[]{:S(2)}, u32[]{:S(2)}) collective-permute-start(f32[384,128]{1,0:T(8,128)S(1)} %get-tuple-element.46), channel_id=1, source_target_pairs={{0,8},{8,0},{16,24},{24,16},{32,40},{40,32},{48,56},{56,48},{1,9},... | collective-permute-start | bytes 589832 | tf_op jit(solution)/shard_map/ppermute | solution.py:309
  39.8 8.6 %collective-permute-start.4 = (f32[512,128]{1,0:T(8,128)S(1)}, f32[512,128]{1,0:T(8,128)S(1)}, u32[]{:S(2)}, u32[]{:S(2)}) collective-permute-start(f32[512,128]{1,0:T(8,128)S(1)} %get-tuple-element.47), channel_id=1, source_target_pairs={{0,1},{1,0},{2,3},{3,2},{4,5},{5,4},{6,7},{7,6},{8,9},{9,8},{10,11... | collective-permute-start | bytes 786440 | tf_op jit(solution)/shard_map/ppermute | solution.py:309
  40.6 7.9 %collective-permute-start.5 = (f32[512,128]{1,0:T(8,128)S(1)}, f32[512,128]{1,0:T(8,128)S(1)}, u32[]{:S(2)}, u32[]{:S(2)}) collective-permute-start(f32[512,128]{1,0:T(8,128)S(1)} %get-tuple-element.48), channel_id=1, source_target_pairs={{1,2},{2,1},{3,4},{4,3},{5,6},{6,5},{7,0},{0,7},{9,10},{10,9},{11,... | collective-permute-start | bytes 786440 | tf_op jit(solution)/shard_map/ppermute | solution.py:309
  53.1 8.8 %collective-permute-start.6 = (f32[384,128]{1,0:T(8,128)S(1)}, f32[384,128]{1,0:T(8,128)S(1)}, u32[]{:S(2)}, u32[]{:S(2)}) collective-permute-start(f32[384,128]{1,0:T(8,128)S(1)} %get-tuple-element.52), channel_id=1, source_target_pairs={{0,64},{64,0},{128,192},{192,128},{1,65},{65,1},{129,193},{193,129... | collective-permute-start | bytes 589832 | tf_op jit(solution)/shard_map/ppermute | solution.py:309
  53.2 14.2 %collective-permute-start.7 = (f32[384,128]{1,0:T(8,128)S(1)}, f32[384,128]{1,0:T(8,128)S(1)}, u32[]{:S(2)}, u32[]{:S(2)}) collective-permute-start(f32[384,128]{1,0:T(8,128)S(1)} %get-tuple-element.53), channel_id=1, source_target_pairs={{64,128},{128,64},{65,129},{129,65},{66,130},{130,66},{67,131},{13... | collective-permute-start | bytes 589832 | tf_op jit(solution)/shard_map/ppermute | solution.py:309
  57.5 9.9 %collective-permute-start.8 = (f32[384,128]{1,0:T(8,128)S(1)}, f32[384,128]{1,0:T(8,128)S(1)}, u32[]{:S(2)}, u32[]{:S(2)}) collective-permute-start(f32[384,128]{1,0:T(8,128)S(1)} %get-tuple-element.54), channel_id=1, source_target_pairs={{8,16},{16,8},{24,32},{32,24},{40,48},{48,40},{9,17},{17,9},{25,33... | collective-permute-start | bytes 589832 | tf_op jit(solution)/shard_map/ppermute | solution.py:309
  58.2 10.0 %collective-permute-start.9 = (f32[384,128]{1,0:T(8,128)S(1)}, f32[384,128]{1,0:T(8,128)S(1)}, u32[]{:S(2)}, u32[]{:S(2)}) collective-permute-start(f32[384,128]{1,0:T(8,128)S(1)} %get-tuple-element.55), channel_id=1, source_target_pairs={{0,8},{8,0},{16,24},{24,16},{32,40},{40,32},{48,56},{56,48},{1,9},... | collective-permute-start | bytes 589832 | tf_op jit(solution)/shard_map/ppermute | solution.py:309
  61.9 6.9 %collective-permute-start.11 = (f32[512,128]{1,0:T(8,128)S(1)}, f32[512,128]{1,0:T(8,128)S(1)}, u32[]{:S(2)}, u32[]{:S(2)}) collective-permute-start(f32[512,128]{1,0:T(8,128)S(1)} %get-tuple-element.57), channel_id=1, source_target_pairs={{1,2},{2,1},{3,4},{4,3},{5,6},{6,5},{7,0},{0,7},{9,10},{10,9},{11,... | collective-permute-start | bytes 786440 | tf_op jit(solution)/shard_map/ppermute | solution.py:309
  73.4 9.7 %collective-permute-start.12 = (f32[384,128]{1,0:T(8,128)S(1)}, f32[384,128]{1,0:T(8,128)S(1)}, u32[]{:S(2)}, u32[]{:S(2)}) collective-permute-start(f32[384,128]{1,0:T(8,128)S(1)} %get-tuple-element.61), channel_id=1, source_target_pairs={{0,64},{64,0},{128,192},{192,128},{1,65},{65,1},{129,193},{193,129... | collective-permute-start | bytes 589832 | tf_op jit(solution)/shard_map/ppermute | solution.py:309
  73.5 14.7 %collective-permute-start.13 = (f32[384,128]{1,0:T(8,128)S(1)}, f32[384,128]{1,0:T(8,128)S(1)}, u32[]{:S(2)}, u32[]{:S(2)}) collective-permute-start(f32[384,128]{1,0:T(8,128)S(1)} %get-tuple-element.62), channel_id=1, source_target_pairs={{64,128},{128,64},{65,129},{129,65},{66,130},{130,66},{67,131},{13... | collective-permute-start | bytes 589832 | tf_op jit(solution)/shard_map/ppermute | solution.py:309
  77.8 10.4 %collective-permute-start.14 = (f32[384,128]{1,0:T(8,128)S(1)}, f32[384,128]{1,0:T(8,128)S(1)}, u32[]{:S(2)}, u32[]{:S(2)}) collective-permute-start(f32[384,128]{1,0:T(8,128)S(1)} %get-tuple-element.63), channel_id=1, source_target_pairs={{8,16},{16,8},{24,32},{32,24},{40,48},{48,40},{9,17},{17,9},{25,33... | collective-permute-start | bytes 589832 | tf_op jit(solution)/shard_map/ppermute | solution.py:309
  78.5 11.5 %collective-permute-start.15 = (f32[384,128]{1,0:T(8,128)S(1)}, f32[384,128]{1,0:T(8,128)S(1)}, u32[]{:S(2)}, u32[]{:S(2)}) collective-permute-start(f32[384,128]{1,0:T(8,128)S(1)} %get-tuple-element.64), channel_id=1, source_target_pairs={{0,8},{8,0},{16,24},{24,16},{32,40},{40,32},{48,56},{56,48},{1,9},... | collective-permute-start | bytes 589832 | tf_op jit(solution)/shard_map/ppermute | solution.py:309
  83.1 7.0 %collective-permute-start.16 = (f32[512,128]{1,0:T(8,128)S(1)}, f32[512,128]{1,0:T(8,128)S(1)}, u32[]{:S(2)}, u32[]{:S(2)}) collective-permute-start(f32[512,128]{1,0:T(8,128)S(1)} %get-tuple-element.65), channel_id=1, source_target_pairs={{0,1},{1,0},{2,3},{3,2},{4,5},{5,4},{6,7},{7,6},{8,9},{9,8},{10,11... | collective-permute-start | bytes 786440 | tf_op jit(solution)/shard_map/ppermute | solution.py:309
  83.1 7.5 %collective-permute-start.17 = (f32[512,128]{1,0:T(8,128)S(1)}, f32[512,128]{1,0:T(8,128)S(1)}, u32[]{:S(2)}, u32[]{:S(2)}) collective-permute-start(f32[512,128]{1,0:T(8,128)S(1)} %get-tuple-element.66), channel_id=1, source_target_pairs={{1,2},{2,1},{3,4},{4,3},{5,6},{6,5},{7,0},{0,7},{9,10},{10,9},{11,... | collective-permute-start | bytes 786440 | tf_op jit(solution)/shard_map/ppermute | solution.py:309
  95.2 8.5 %collective-permute-start.18 = (f32[384,128]{1,0:T(8,128)S(1)}, f32[384,128]{1,0:T(8,128)S(1)}, u32[]{:S(2)}, u32[]{:S(2)}) collective-permute-start(f32[384,128]{1,0:T(8,128)S(1)} %get-tuple-element.70), channel_id=1, source_target_pairs={{0,64},{64,0},{128,192},{192,128},{1,65},{65,1},{129,193},{193,129... | collective-permute-start | bytes 589832 | tf_op jit(solution)/shard_map/ppermute | solution.py:309
  95.5 13.7 %collective-permute-start.19 = (f32[384,128]{1,0:T(8,128)S(1)}, f32[384,128]{1,0:T(8,128)S(1)}, u32[]{:S(2)}, u32[]{:S(2)}) collective-permute-start(f32[384,128]{1,0:T(8,128)S(1)} %get-tuple-element.71), channel_id=1, source_target_pairs={{64,128},{128,64},{65,129},{129,65},{66,130},{130,66},{67,131},{13... | collective-permute-start | bytes 589832 | tf_op jit(solution)/shard_map/ppermute | solution.py:309
  99.3 9.9 %collective-permute-start.20 = (f32[384,128]{1,0:T(8,128)S(1)}, f32[384,128]{1,0:T(8,128)S(1)}, u32[]{:S(2)}, u32[]{:S(2)}) collective-permute-start(f32[384,128]{1,0:T(8,128)S(1)} %get-tuple-element.72), channel_id=1, source_target_pairs={{8,16},{16,8},{24,32},{32,24},{40,48},{48,40},{9,17},{17,9},{25,33... | collective-permute-start | bytes 589832 | tf_op jit(solution)/shard_map/ppermute | solution.py:309
  100.0 10.1 %collective-permute-start.21 = (f32[384,128]{1,0:T(8,128)S(1)}, f32[384,128]{1,0:T(8,128)S(1)}, u32[]{:S(2)}, u32[]{:S(2)}) collective-permute-start(f32[384,128]{1,0:T(8,128)S(1)} %get-tuple-element.73), channel_id=1, source_target_pairs={{0,8},{8,0},{16,24},{24,16},{32,40},{40,32},{48,56},{56,48},{1,9},... | collective-permute-start | bytes 589832 | tf_op jit(solution)/shard_map/ppermute | solution.py:309
  103.7 6.4 %collective-permute-start.22 = (f32[512,128]{1,0:T(8,128)S(1)}, f32[512,128]{1,0:T(8,128)S(1)}, u32[]{:S(2)}, u32[]{:S(2)}) collective-permute-start(f32[512,128]{1,0:T(8,128)S(1)} %get-tuple-element.74), channel_id=1, source_target_pairs={{0,1},{1,0},{2,3},{3,2},{4,5},{5,4},{6,7},{7,6},{8,9},{9,8},{10,11... | collective-permute-start | bytes 786440 | tf_op jit(solution)/shard_map/ppermute | solution.py:309
  103.7 6.4 %collective-permute-start.23 = (f32[512,128]{1,0:T(8,128)S(1)}, f32[512,128]{1,0:T(8,128)S(1)}, u32[]{:S(2)}, u32[]{:S(2)}) collective-permute-start(f32[512,128]{1,0:T(8,128)S(1)} %get-tuple-element.75), channel_id=1, source_target_pairs={{1,2},{2,1},{3,4},{4,3},{5,6},{6,5},{7,0},{0,7},{9,10},{10,9},{11,... | collective-permute-start | bytes 786440 | tf_op jit(solution)/shard_map/ppermute | solution.py:309
  (7 other events, 60.2 us)
